TPU v7x, 32 devices: a whole 2x2x4 slice. The times are simulated.
32 devices in a mesh: groups: 2 (over x), dp: 8 (over z, y), head: 2 (over core).
Axes of the slice: x: 2, y: 2, z: 4, core: 2. Of those that a mesh axis runs over, the one named last changes fastest.
Arguments:
- queries: bfloat16 [96, 128, 576], P(('groups', 'dp'), 'head'), parts along dimension 0, as said below
- latent_key_cache: bfloat16 [96, 192, 576], P(('groups', 'dp')), parts along dimension 0, as said below
- lengths: int32 [96], P(('groups', 'dp')), parts along dimension 0, may hold values from 48 to 192, as said below
- counts: int32 [16], P('groups'), parts along dimension 0, may hold values from 1 to 6, as said below
- residual: bfloat16 [96, 7168], P(('groups', 'dp', 'head')), parts along dimension 0
- value_up_weight: bfloat16 [2, 64, 512, 128], P('head', 'dp'), may hold values from -0.25 to 0.25
- output_proj: bfloat16 [2, 8192, 7168], P('head', 'dp'), may hold values from -0.125 to 0.125
- norm_gain: float32 [7168], replicated, may hold values from 0.1 to 1.9
- gate_weight: bfloat16 [7168, 9216], P(None, ('dp', 'head')), may hold values from -0.0625 to 0.0625
- up_weight: bfloat16 [7168, 9216], P(None, ('dp', 'head')), may hold values from -0.0625 to 0.0625
- down_weight: bfloat16 [9216, 7168], P(('dp', 'head')), may hold values from -0.125 to 0.125
Outputs:
- layer_out: bfloat16 [96, 7168], P(('groups', 'dp', 'head')), parts along dimension 0
There are 2 independent parts, one for each index of `groups`. A program takes and returns all parts, laid end to end along the dimension named above; an argument that names none is the same for every part. Nothing has to cross between parts.
Inputs may be any that keep to these rules, and one draw needn't show every extreme that they name: Rank r's live rows are its first counts[r] slots; in every draw some rank has all 6 slots live. `lengths`: in every draw some live row has a cache of exactly 192 positions. real-valued latent queries of order one, larger where a query follows a cached key. `latent_key_cache`: real-valued latent keys of order one.
All inputs are finite; a program needn't handle non-finite values.
Results may differ from a plain program's by a relative error of at most 0.006.
Values may be sent and summed in bfloat16 or wider, within the bound.
No kernel may reach another device: no remote copies, remote signals or barrier semaphores. Data moves between devices by JAX's collectives and lax.ppermute only.
A program may use at most 128 MiB of HBM per device.

v0:
```python
import jax
import jax.numpy as jnp
from jax import lax
from jax.sharding import PartitionSpec as P

LATENT_WIDTH = 512


score_scale = 0.07216878364870322
norm_epsilon = 1e-06
masked_score = -1e30


def on_device(
    queries,
    latent_key_cache,
    lengths,
    counts,
    residual,
    value_up_weight,
    output_proj,
    norm_gain,
    gate_weight,
    up_weight,
    down_weight,
):
    slot_count = queries.shape[0]
    cache_length = latent_key_cache.shape[1]
    owner_rows = residual.shape[0]
    my_rank = lax.axis_index("dp")
    live_count = jnp.sum(
        jnp.where(jnp.arange(counts.shape[0], dtype=jnp.int32) == my_rank, counts, 0)
    )
    live_slots = jnp.arange(slot_count, dtype=jnp.int32) < live_count
    scores = (
        jnp.einsum("rhc,rjc->rhj", queries, latent_key_cache, preferred_element_type=jnp.float32)
        * score_scale
    )
    positions = jnp.arange(cache_length, dtype=jnp.int32)
    valid_keys = positions[None, :] < lengths[:, None]
    scores, key_values = (
        jnp.where(valid_keys[:, None, :], scores, masked_score),
        latent_key_cache[:, :, :LATENT_WIDTH],
    )
    row_top = jnp.max(scores, axis=-1, keepdims=True)
    probs_full = jnp.exp(scores - row_top)
    softmax_denominator = jnp.sum(probs_full, axis=-1)
    weighted_latent = jnp.einsum(
        "ukw,uwm->ukm",
        probs_full.astype(jnp.bfloat16),
        key_values,
        preferred_element_type=jnp.float32,
    )
    latent_out = jnp.where(
        live_slots[:, None, None], weighted_latent / softmax_denominator[:, :, None], 0.0
    ).astype(jnp.bfloat16)
    arrived = lax.all_to_all(latent_out, "dp", split_axis=1, concat_axis=0, tiled=True)
    values = jnp.einsum(
        "rhc,hcd->rhd", arrived, value_up_weight[0], preferred_element_type=jnp.float32
    ).astype(jnp.bfloat16)
    flat_values = values.reshape(values.shape[0], values.shape[1] * values.shape[2])
    proj_local = output_proj[0]
    picked = flat_values
    attention = lax.psum_scatter(
        jnp.dot(picked, proj_local, preferred_element_type=jnp.float32),
        ("dp", "head"),
        scatter_dimension=0,
        tiled=True,
    )
    layer_state = residual.astype(jnp.float32) + attention
    mean_square = jnp.mean(layer_state * layer_state, axis=-1, keepdims=True)
    normed = (layer_state * lax.rsqrt(mean_square + norm_epsilon) * norm_gain).astype(jnp.bfloat16)
    row_piece = lax.all_gather(normed, ("dp", "head"), axis=0, tiled=True)
    gate_part = jnp.dot(row_piece, gate_weight, preferred_element_type=jnp.float32)
    up_part = jnp.dot(row_piece, up_weight, preferred_element_type=jnp.float32)
    hidden_units = (jax.nn.silu(gate_part) * up_part).astype(jnp.bfloat16)
    picked = hidden_units
    feed_forward = lax.psum_scatter(
        jnp.dot(picked, down_weight, preferred_element_type=jnp.float32),
        ("dp", "head"),
        scatter_dimension=0,
        tiled=True,
    )
    owner_slots = lax.axis_index("head") * owner_rows + jnp.arange(owner_rows, dtype=jnp.int32)
    owner_live = owner_slots < live_count
    return jnp.where(owner_live[:, None], layer_state + feed_forward, 0.0).astype(jnp.bfloat16)


def solution(mesh):
    in_specs = (
        P(("groups", "dp"), "head", None),
        P(("groups", "dp"), None, None),
        P(("groups", "dp")),
        P("groups"),
        P(("groups", "dp", "head"), None),
        P("head", "dp", None, None),
        P("head", "dp", None),
        P(),
        P(None, ("dp", "head")),
        P(None, ("dp", "head")),
        P(("dp", "head"), None),
    )
    out_specs = P(("groups", "dp", "head"), None)
    return jax.shard_map(
        on_device, mesh=mesh, in_specs=in_specs, out_specs=out_specs, check_vma=False
    )
```

profile of v0, /device:TPU:0, one launch (start us, length us, event | category | flops | bytes accessed | tf_op | source)
XLA Modules:
  0.0 279.8 jit_solution(1279240230014231295)
XLA Ops:
  6.5 0.0 copy-start
  6.5 0.0 copy-start.1
  6.5 0.0 all-reduce.5.cloned.1.call-start
  6.5 1.4 fusion.26
  8.0 0.6 iota_compare_fusion.1
  8.6 0.7 iota_compare_fusion
  9.4 2.3 fusion.28
  11.7 0.2 fusion.11
  11.9 0.0 copy-done.1
  11.9 0.4 fusion.3
  12.3 0.2 copy.19
  12.6 21.6 %all_to_all.18 = bf16[6,64,512]{2,0,1:T(8,128)(2,1)S(1)} all-to-all(bf16[6,64,512]{2,0,1:T(8,128)(2,1)S(1)} %copy.19), channel_id=1, replica_groups=mesh['groups'=2,'dp'=8,'head'=2] {'dp'}, dimensions={1} | all-to-all | bytes 786432 | tf_op jit(solution)/shard_map/all_to_all | solution.py:57
  34.2 0.1 copy.21
  34.3 0.0 copy-done
  34.3 0.4 fusion.6
  34.7 0.0 copy-start.4
  34.7 0.0 copy-start.2
  34.7 9.0 %fusion = f32[48,7168]{1,0:T(8,128)} fusion(bf16[1,1024,7168]{2,1,0:T(8,128)(2,1)} %param.17, bf16[8,6,8,128]{3,2,1,0:T(8,128)(2,1)S(1)} %fusion.6), kind=kOutput, calls=%fused_computation | convolution fusion | flops 704643072 | bytes 16154624 | tf_op jit(solution)/shard_map/dot_general | solution.py:65
  43.7 0.0 copy-start.3
  43.7 0.0 all-reduce.5.cloned.1.call-update
  43.8 0.0 all-reduce.7.cloned.1.call-start
  43.8 0.0 copy-done.4
  43.8 0.7 dynamic-slice
  45.1 92.1 %all-reduce.5.cloned.1.call-done = f32[48,7168]{1,0:T(8,128)} async-done(((f32[48,7168]{1,0:T(8,128)}), f32[48,7168]{1,0:T(8,128)}) %all-reduce.5.cloned.1.call-update) | async-done | bytes 1376272
  137.3 0.0 copy-done.2
  137.3 1.2 multiply_reduce_fusion
  138.5 0.0 copy-done.3
  138.5 1.1 fusion.25
  139.6 21.8 %all-gather = bf16[16,3,7168]{2,1,0:T(4,128)(2,1)S(1)} all-gather(bf16[1,3,7168]{2,1,0:T(4,128)(2,1)S(1)} %fusion.25), channel_id=1, replica_groups=mesh['groups'=2,'dp'=8,'head'=2] {'dp','head'}, dimensions={0}, use_global_device_ids=true | all-gather | bytes 731136 | tf_op jit(solution)/shard_map/all_gather | solution.py:73
  161.4 0.6 reshape.42
  162.0 5.8 %fusion.29 = f32[48,576]{1,0:T(8,128)S(1)} fusion(bf16[48,7168]{1,0:T(8,128)(2,1)S(1)} %reshape.42, bf16[7168,576]{0,1:T(8,128)(2,1)} %param.19), kind=kOutput, calls=%fused_computation.42 | convolution fusion | flops 396361728 | bytes 9056256 | tf_op jit(solution)/shard_map/dot_general | solution.py:74
  167.9 11.3 %fusion.9 = f32[48,7168]{1,0:T(8,128)} fusion(bf16[576,7168]{1,0:T(8,128)(2,1)} %param.21, bf16[48,7168]{1,0:T(8,128)(2,1)S(1)} %reshape.42, bf16[7168,576]{0,1:T(8,128)(2,1)} %param.20, f32[48,576]{1,0:T(8,128)S(1)} %fusion.29), kind=kOutput, calls=%fused_computation.13 | convolution fusion | flops 792889344 | bytes 18690048 | tf_op jit(solution)/shard_map/dot_general | solution.py:79
  179.1 0.0 all-reduce.7.cloned.1.call-update
  179.2 0.7 add_compare_fusion
  179.8 91.3 %all-reduce.7.cloned.1.call-done = f32[48,7168]{1,0:T(8,128)} async-done(((f32[48,7168]{1,0:T(8,128)}), f32[48,7168]{1,0:T(8,128)}) %all-reduce.7.cloned.1.call-update) | async-done | bytes 1376272
  271.1 1.9 fusion.21
  (1 shorter events, 0.0 us)
Async XLA Ops:
  6.5 27.8 %copy-start = (bf16[1,8,512,128]{3,2,1,0:T(8,128)(2,1)S(1)}, bf16[1,8,512,128]{3,2,1,0:T(8,128)(2,1)}, u32[]{:S(2)}) copy-start(bf16[1,8,512,128]{3,2,1,0:T(8,128)(2,1)} %param.16) | copy-start | bytes 3145732
  6.5 5.4 %copy-start.1 = (bf16[6,192,576]{2,1,0:T(8,128)(2,1)S(1)}, bf16[6,192,576]{2,1,0:T(8,128)(2,1)}, u32[]{:S(2)}) copy-start(bf16[6,192,576]{2,1,0:T(8,128)(2,1)} %param.12) | copy-start | bytes 3981316
  6.5 130.7 %all-reduce.5.cloned.1.call-start = ((), (), s32[]{:S(2)}) async-start(), calls=%async_computation.1 | async-start | bytes 2752512
  34.7 9.1 %copy-start.4 = (u32[32]{0:T(128)S(1)}, u32[32]{0:T(128)}, u32[]{:S(2)}) copy-start(u32[32]{0:T(128)} %constant.36) | copy-start | bytes 388
  34.7 102.6 %copy-start.2 = (bf16[3,7168]{1,0:T(4,128)(2,1)S(1)}, bf16[3,7168]{1,0:T(4,128)(2,1)}, u32[]{:S(2)}) copy-start(bf16[3,7168]{1,0:T(4,128)(2,1)} %param.15) | copy-start | bytes 129028
  43.7 94.8 %copy-start.3 = (f32[7168]{0:T(1024)S(1)}, f32[7168]{0:T(1024)}, u32[]{:S(2)}) copy-start(f32[7168]{0:T(1024)} %param.18) | copy-start | bytes 86020
  43.8 227.3 %all-reduce.7.cloned.1.call-start = ((), (), s32[]{:S(2)}) async-start(), calls=%async_computation.2 | async-start | bytes 2752512
Sparse Core Ops, SparseCore 0:
  43.9 93.3 all-reduce.4
  179.3 91.7 all-reduce.6
where the time goes:
time: 280 us
  waiting for transfers between devices  183 us (65%)
  blocking collectives  43.4 us (16%)
  matrix products  29.2 us (10%)
  between operations  14.2 us (5%)
  other arithmetic  7.91 us (3%)
    unnamed x4, waiting for transfers between devices  183 us
    all_gather x1, blocking collectives, on_device(): row_piece = lax.all_gather(normed, ('dp', 'head'), axis=0, tiled=True)  21.8 us
    all_to_all x1, blocking collectives, on_device(): lax.all_to_all(latent_out, 'dp', split_axis=1, concat_axis=0, tiled=True)  21.6 us
    dot_general x1, matrix products, on_device(): jnp.dot(picked, down_weight, preferred_element_type=jnp.float32)  11.3 us
    dot_general x1, matrix products, on_device(): jnp.dot(picked, proj_local, preferred_element_type=jnp.float32)  9.01 us
    dot_general x1, matrix products, on_device(): jnp.dot(row_piece, gate_weight, preferred_element_type=jnp.float32)  5.81 us
  transfers between devices with their start and end apart: 2, of which 2 were waited for; matrix products, arithmetic and copies ran while one was open for 0% of the time, Pallas kernels for 0%

commit v1 on v0

v1 whole, which is shorter than its diff:
```python
import jax
import jax.numpy as jnp
from jax import lax
from jax.sharding import PartitionSpec as P

LATENT_WIDTH = 512
LANES = 128

score_scale = 0.07216878364870322
norm_epsilon = 1e-06
masked_score = -1e30
f32 = jnp.float32
bf16 = jnp.bfloat16


def on_device(n_dp, queries, latent_key_cache, lengths, counts, residual, value_up_weight,
              output_proj, norm_gain, gate_weight, up_weight, down_weight):
    slots = queries.shape[0]
    heads = queries.shape[1]
    cache_length = latent_key_cache.shape[1]
    owner_rows, width = residual.shape
    tiles = width // LANES
    me = lax.axis_index("dp")
    my_head = lax.axis_index("head")

    def to_peer(x, k):
        return lax.ppermute(x, "dp", [(i, i ^ k) for i in range(n_dp)])

    def to_twin(x):
        return lax.ppermute(x, "head", [(0, 1), (1, 0)])

    def reduce_rows(part):
        mine = part[0] + to_twin(part[1].astype(bf16)).astype(f32)
        sent = mine.astype(bf16)
        total = mine[0]
        for k in range(1, n_dp):
            total = total + to_peer(sent[k], k).astype(f32)
        return total

    live_count = jnp.sum(jnp.where(jnp.arange(n_dp, dtype=jnp.int32) == me, counts, 0))
    live_slots = jnp.arange(slots, dtype=jnp.int32) < live_count
    scores = jnp.einsum("rhc,rjc->rhj", queries, latent_key_cache, preferred_element_type=f32) * score_scale
    positions = jnp.arange(cache_length, dtype=jnp.int32)
    valid = positions[None, :] < lengths[:, None]
    scores = jnp.where(valid[:, None, :], scores, masked_score)
    row_top = jnp.max(scores, axis=-1, keepdims=True)
    probs = jnp.exp(scores - row_top)
    denominator = jnp.sum(probs, axis=-1)
    weighted = jnp.einsum("ukw,uwm->ukm", probs.astype(bf16), latent_key_cache[:, :, :LATENT_WIDTH],
                          preferred_element_type=f32)
    latent = jnp.where(live_slots[:, None, None], weighted / denominator[:, :, None], 0.0).astype(bf16)
    per_rank = heads // n_dp
    latent = latent.reshape(slots, n_dp, per_rank, LATENT_WIDTH)
    blocks = []
    for k in range(n_dp):
        piece = lax.dynamic_index_in_dim(latent, me ^ k, 1, keepdims=False)
        blocks.append(to_peer(piece, k) if k else piece)
    arrived = jnp.stack(blocks)
    arrived = arrived.reshape(n_dp, 2, owner_rows, per_rank, LATENT_WIDTH)
    arrived = jnp.swapaxes(arrived, 0, 1)
    arrived = jnp.where(my_head == 0, arrived, arrived[::-1])
    arrived = arrived.reshape(n_dp * slots, per_rank, LATENT_WIDTH)
    values = jnp.einsum("rhc,hcd->rhd", arrived, value_up_weight[0], preferred_element_type=f32).astype(bf16)
    values = values.reshape(n_dp * slots, -1)
    part = jnp.dot(values, output_proj[0], preferred_element_type=f32)
    attention = reduce_rows(part.reshape(2, n_dp, owner_rows * tiles, LANES))
    attention = attention.reshape(owner_rows, tiles, LANES)
    state = residual.astype(f32).reshape(owner_rows, tiles, LANES) + attention
    mean_square = jnp.sum(state * state, axis=(1, 2), keepdims=True) / width
    normed = (state * lax.rsqrt(mean_square + norm_epsilon) * norm_gain.reshape(tiles, LANES)).astype(bf16)
    normed = normed.reshape(owner_rows * tiles, LANES)
    rows = jnp.stack([normed] + [to_peer(normed, k) for k in range(1, n_dp)])
    rows = jnp.stack([rows, to_twin(rows)])
    rows = rows.reshape(n_dp * slots, width)
    gate_part = jnp.dot(rows, gate_weight, preferred_element_type=f32)
    up_part = jnp.dot(rows, up_weight, preferred_element_type=f32)
    hidden = (jax.nn.silu(gate_part) * up_part).astype(bf16)
    part = jnp.dot(hidden, down_weight, preferred_element_type=f32)
    feed_forward = reduce_rows(part.reshape(2, n_dp, owner_rows * tiles, LANES))
    out = state + feed_forward.reshape(owner_rows, tiles, LANES)
    owner_live = my_head * owner_rows + jnp.arange(owner_rows, dtype=jnp.int32) < live_count
    return jnp.where(owner_live[:, None, None], out, 0.0).astype(bf16).reshape(owner_rows, width)


def solution(mesh):
    n_dp = mesh.shape["dp"]
    in_specs = (
        P(("groups", "dp"), "head", None),
        P(("groups", "dp"), None, None),
        P(("groups", "dp")),
        P("groups"),
        P(("groups", "dp", "head"), None),
        P("head", "dp", None, None),
        P("head", "dp", None),
        P(),
        P(None, ("dp", "head")),
        P(None, ("dp", "head")),
        P(("dp", "head"), None),
    )
    out_specs = P(("groups", "dp", "head"), None)

    def step(*args):
        return on_device(n_dp, *args)

    return jax.shard_map(step, mesh=mesh, in_specs=in_specs, out_specs=out_specs, check_vma=False)
```

time: 280 us -> 114 us (0.41)
  waiting for transfers between devices: 183 us -> 25.9 us
  starting transfers between devices: 0.04 us -> 47.5 us
  blocking collectives: 43.4 us -> 0 us
  between operations: 14.2 us -> 0.4 us
  local copies, waits for them, and re-layouts: 1.64 us -> 4.95 us
    unnamed x4 -> x0, waiting for transfers between devices: 183 us -> none
    ppermute x0 -> x31, starting transfers between devices: none -> 47.5 us  [the longest x28 47.3 us: to_peer(): return lax.ppermute(x, 'dp', [(i, i ^ k) for i in range(n_dp)])]
    ppermute x0 -> x31, waiting for transfers between devices: none -> 25.9 us  [the longest x28 22.4 us: to_peer(): return lax.ppermute(x, 'dp', [(i, i ^ k) for i in range(n_dp)])]
    all_gather x1 -> x0, blocking collectives: 21.8 us -> none  [on_device(): row_piece = lax.all_gather(normed, ('dp', 'head'), axis=0, tiled=True)]
    all_to_all x1 -> x0, blocking collectives: 21.6 us -> none  [on_device(): lax.all_to_all(latent_out, 'dp', split_axis=1, concat_axis=0, tiled=True)]
  transfers between devices with their start and end apart: 2 -> 31, of which waited for: 2 -> 13; matrix products, arithmetic and copies ran while one was open for 0% -> 3% of each run, Pallas kernels for 0% -> 0%
where the time goes in v1:
time: 114 us
  starting transfers between devices  47.5 us (42%)
  matrix products  28.2 us (25%)
  waiting for transfers between devices  25.9 us (23%)
  other arithmetic  7.03 us (6%)
  local copies, waits for them, and re-layouts  4.95 us (4%)
    ppermute x28, starting transfers between devices, to_peer(): return lax.ppermute(x, 'dp', [(i, i ^ k) for i in range(n_dp)])  47.3 us
    ppermute x28, waiting for transfers between devices, to_peer(): return lax.ppermute(x, 'dp', [(i, i ^ k) for i in range(n_dp)])  22.4 us
    dot_general x1, matrix products, on_device(): part = jnp.dot(hidden, down_weight, preferred_element_type=f32)  10.2 us
    dot_general x1, matrix products, on_device(): part = jnp.dot(values, output_proj[0], preferred_element_type=f32)  7.85 us
    dot_general x1, matrix products, on_device(): gate_part = jnp.dot(rows, gate_weight, preferred_element_type=f32)  5.81 us
    ppermute x3, waiting for transfers between devices, to_twin(): return lax.ppermute(x, 'head', [(0, 1), (1, 0)])  3.47 us
    dot_general x1, matrix products, on_device(): jnp.einsum('rhc,rjc->rhj', queries, latent_key_cache, preferred_element_t...  2.29 us
  transfers between devices with their start and end apart: 31, of which 13 were waited for; matrix products, arithmetic and copies ran while one was open for 3% of the time, Pallas kernels for 0%

profile of v1, /device:TPU:0, one launch (start us, length us, event | category | flops | bytes accessed | tf_op | source)
XLA Modules:
  0.0 114.0 jit_solution(425183669186474093)
XLA Ops:
  0.0 1.4 %fusion.39 = s32[]{:T(128)} fusion(s32[8]{0:T(128)} %param.14, s32[]{:T(128)S(6)} %axis_index.25), kind=kLoop, calls=%fused_computation.95 | loop fusion | flops 23 | bytes 40 | tf_op jit(solution)/shard_map/reduce_sum | solution.py:40
  1.4 0.6 iota_compare_fusion.1
  2.0 0.7 iota_compare_fusion
  2.8 2.3 %fusion.43 = (f32[6,64]{1,0:T(8,128)S(1)}, f32[6,64,192]{2,1,0:T(8,128)S(1)}) fusion(bf16[6,64,576]{2,1,0:T(8,128)(2,1)} %param.11, bf16[6,192,576]{2,1,0:T(8,128)(2,1)} %param.12, pred[6,192]{1,0:T(8,128)(4,1)S(1)} %iota_compare_fusion), kind=kOutput, calls=%fused_computation.102 | convolution fusion | flops 85155456 | bytes 2067072 | tf_op jit(solution)/shard_map/rhc,rjc->rhj/dot_general | solution.py:42
  5.3 1.7 %fusion.5 = bf16[6,8,8,512]{3,2,1,0:T(8,128)(2,1)S(1)} fusion(bf16[6,192,576]{2,1,0:T(8,128)(2,1)} %param.12, f32[6,64]{1,0:T(8,128)S(1)} %fusion.12, pred[6]{0:T(512)(128)(4,1)S(1)} %iota_compare_fusion.1, f32[6,64,192]{2,1,0:T(8,128)S(1)} %get-tuple-element.32, f32[6,64]{1,0:T(8,128)S(1)} %get-tuple-element.31), kind=kOutput, calls=%fused_computation.7 | convolution fusion | flops 76234752 | bytes 1870854 | tf_op jit(solution)/shard_map/ukw,uwm->ukm/dot_general | solution.py:49
  7.0 6.1 %collective-permute-start.6 = (bf16[6,8,512]{2,1,0:T(8,128)(2,1)S(1)}, bf16[6,8,512]{2,1,0:T(8,128)(2,1)S(1)}, u32[]{:S(2)}, u32[]{:S(2)}) collective-permute-start(bf16[6,8,512]{2,1,0:T(8,128)(2,1)S(1)} %get-tuple-element.9), channel_id=1, source_target_pairs={{0,14},{2,12},{4,10},{6,8},{8,6},{10,4},{12,2},{14,0},{1,15},{3,13... | collective-permute-start | bytes 147464 | tf_op jit(solution)/shard_map/ppermute | solution.py:27
  13.3 0.7 collective-permute-start.4
  14.1 2.0 %collective-permute-start.3 = (bf16[6,8,512]{2,1,0:T(8,128)(2,1)S(1)}, bf16[6,8,512]{2,1,0:T(8,128)(2,1)S(1)}, u32[]{:S(2)}, u32[]{:S(2)}) collective-permute-start(bf16[6,8,512]{2,1,0:T(8,128)(2,1)S(1)} %get-tuple-element.12), channel_id=1, source_target_pairs={{0,8},{2,10},{4,12},{6,14},{8,0},{10,2},{12,4},{14,6},{1,9},{3,11}... | collective-permute-start | bytes 147464 | tf_op jit(solution)/shard_map/ppermute | solution.py:27
  16.1 1.6 %collective-permute-start = (bf16[6,8,512]{2,1,0:T(8,128)(2,1)S(1)}, bf16[6,8,512]{2,1,0:T(8,128)(2,1)S(1)}, u32[]{:S(2)}, u32[]{:S(2)}) collective-permute-start(bf16[6,8,512]{2,1,0:T(8,128)(2,1)S(1)} %get-tuple-element.15), channel_id=1, source_target_pairs={{0,2},{2,0},{4,6},{6,4},{8,10},{10,8},{12,14},{14,12},{1,3},{3,1},... | collective-permute-start | bytes 147464 | tf_op jit(solution)/shard_map/ppermute | solution.py:27
  17.7 2.9 %collective-permute-done = bf16[6,8,512]{2,1,0:T(8,128)(2,1)S(1)} collective-permute-done((bf16[6,8,512]{2,1,0:T(8,128)(2,1)S(1)}, bf16[6,8,512]{2,1,0:T(8,128)(2,1)S(1)}, u32[]{:S(2)}, u32[]{:S(2)}) %collective-permute-start) | collective-permute-done | bytes 49184 | tf_op jit(solution)/shard_map/ppermute | solution.py:27
  20.6 1.0 collective-permute-start.1
  21.6 3.2 %collective-permute-done.1 = bf16[6,8,512]{2,1,0:T(8,128)(2,1)S(1)} collective-permute-done((bf16[6,8,512]{2,1,0:T(8,128)(2,1)S(1)}, bf16[6,8,512]{2,1,0:T(8,128)(2,1)S(1)}, u32[]{:S(2)}, u32[]{:S(2)}) %collective-permute-start.1) | collective-permute-done | bytes 49184 | tf_op jit(solution)/shard_map/ppermute | solution.py:27
  24.8 1.8 %collective-permute-start.2 = (bf16[6,8,512]{2,1,0:T(8,128)(2,1)S(1)}, bf16[6,8,512]{2,1,0:T(8,128)(2,1)S(1)}, u32[]{:S(2)}, u32[]{:S(2)}) collective-permute-start(bf16[6,8,512]{2,1,0:T(8,128)(2,1)S(1)} %get-tuple-element.13), channel_id=1, source_target_pairs={{0,6},{2,4},{4,2},{6,0},{8,14},{10,12},{12,10},{14,8},{1,7},{3,5},... | collective-permute-start | bytes 147464 | tf_op jit(solution)/shard_map/ppermute | solution.py:27
  26.6 3.2 %collective-permute-done.2 = bf16[6,8,512]{2,1,0:T(8,128)(2,1)S(1)} collective-permute-done((bf16[6,8,512]{2,1,0:T(8,128)(2,1)S(1)}, bf16[6,8,512]{2,1,0:T(8,128)(2,1)S(1)}, u32[]{:S(2)}, u32[]{:S(2)}) %collective-permute-start.2) | collective-permute-done | bytes 49184 | tf_op jit(solution)/shard_map/ppermute | solution.py:27
  30.4 7.8 %fusion = f32[48,7168]{1,0:T(8,128)S(1)} fusion(bf16[1,1024,7168]{2,1,0:T(8,128)(2,1)} %param.17, bf16[8,6,8,128]{3,2,1,0:T(8,128)(2,1)S(1)} %fusion.7), kind=kOutput, calls=%fused_computation | convolution fusion | flops 704643072 | bytes 16154624 | tf_op jit(solution)/shard_map/dot_general | solution.py:65
  38.3 0.9 convert_element_type.97
  39.4 1.8 %collective-permute-done.7 = bf16[8,168,128]{2,1,0:T(8,128)(2,1)} collective-permute-done((bf16[8,168,128]{2,1,0:T(8,128)(2,1)}, bf16[8,168,128]{2,1,0:T(8,128)(2,1)}, u32[]{:S(2)}, u32[]{:S(2)}) %collective-permute-start.7) | collective-permute-done | bytes 344096 | tf_op jit(solution)/shard_map/ppermute | solution.py:30
  41.2 1.1 fusion.42
  42.3 2.0 %collective-permute-start.8 = (bf16[168,128]{1,0:T(8,128)(2,1)S(1)}, bf16[168,128]{1,0:T(8,128)(2,1)S(1)}, u32[]{:S(2)}, u32[]{:S(2)}) collective-permute-start(bf16[168,128]{1,0:T(8,128)(2,1)S(1)} %get-tuple-element.24), channel_id=1, source_target_pairs={{0,2},{2,0},{4,6},{6,4},{8,10},{10,8},{12,14},{14,12},{1,3},{3,1},... | collective-permute-start | bytes 129032 | tf_op jit(solution)/shard_map/ppermute | solution.py:27
  44.3 2.9 %collective-permute-start.14 = (bf16[168,128]{1,0:T(8,128)(2,1)S(1)}, bf16[168,128]{1,0:T(8,128)(2,1)S(1)}, u32[]{:S(2)}, u32[]{:S(2)}) collective-permute-start(bf16[168,128]{1,0:T(8,128)(2,1)S(1)} %get-tuple-element.25), channel_id=1, source_target_pairs={{0,14},{2,12},{4,10},{6,8},{8,6},{10,4},{12,2},{14,0},{1,15},{3,13... | collective-permute-start | bytes 129032 | tf_op jit(solution)/shard_map/ppermute | solution.py:27
  47.6 1.1 collective-permute-start.12
  48.8 3.1 %collective-permute-start.11 = (bf16[168,128]{1,0:T(8,128)(2,1)S(1)}, bf16[168,128]{1,0:T(8,128)(2,1)S(1)}, u32[]{:S(2)}, u32[]{:S(2)}) collective-permute-start(bf16[168,128]{1,0:T(8,128)(2,1)S(1)} %get-tuple-element.28), channel_id=1, source_target_pairs={{0,8},{2,10},{4,12},{6,14},{8,0},{10,2},{12,4},{14,6},{1,9},{3,11}... | collective-permute-start | bytes 129032 | tf_op jit(solution)/shard_map/ppermute | solution.py:27
  51.9 1.0 collective-permute-start.10
  53.6 1.8 %collective-permute-done.12 = bf16[168,128]{1,0:T(8,128)(2,1)S(1)} collective-permute-done((bf16[168,128]{1,0:T(8,128)(2,1)S(1)}, bf16[168,128]{1,0:T(8,128)(2,1)S(1)}, u32[]{:S(2)}, u32[]{:S(2)}) %collective-permute-start.12) | collective-permute-done | bytes 43040 | tf_op jit(solution)/shard_map/ppermute | solution.py:27
  55.5 1.3 %collective-permute-done.10 = bf16[168,128]{1,0:T(8,128)(2,1)S(1)} collective-permute-done((bf16[168,128]{1,0:T(8,128)(2,1)S(1)}, bf16[168,128]{1,0:T(8,128)(2,1)S(1)}, u32[]{:S(2)}, u32[]{:S(2)}) %collective-permute-start.10) | collective-permute-done | bytes 43040 | tf_op jit(solution)/shard_map/ppermute | solution.py:27
  57.5 1.5 %collective-permute-start.15 = (bf16[168,128]{1,0:T(8,128)(2,1)S(1)}, bf16[168,128]{1,0:T(8,128)(2,1)S(1)}, u32[]{:S(2)}, u32[]{:S(2)}) collective-permute-start(bf16[168,128]{1,0:T(8,128)(2,1)S(1)} %get-tuple-element.34), channel_id=1, source_target_pairs={{0,2},{2,0},{4,6},{6,4},{8,10},{10,8},{12,14},{14,12},{1,3},{3,1},... | collective-permute-start | bytes 129032 | tf_op jit(solution)/shard_map/ppermute | solution.py:27
  59.0 2.8 %collective-permute-start.20 = (bf16[168,128]{1,0:T(8,128)(2,1)S(1)}, bf16[168,128]{1,0:T(8,128)(2,1)S(1)}, u32[]{:S(2)}, u32[]{:S(2)}) collective-permute-start(bf16[168,128]{1,0:T(8,128)(2,1)S(1)} %get-tuple-element.34), channel_id=1, source_target_pairs={{0,12},{2,14},{4,8},{6,10},{8,4},{10,6},{12,0},{14,2},{1,13},{3,15... | collective-permute-start | bytes 129032 | tf_op jit(solution)/shard_map/ppermute | solution.py:27
  61.8 3.4 %collective-permute-start.18 = (bf16[168,128]{1,0:T(8,128)(2,1)S(1)}, bf16[168,128]{1,0:T(8,128)(2,1)S(1)}, u32[]{:S(2)}, u32[]{:S(2)}) collective-permute-start(bf16[168,128]{1,0:T(8,128)(2,1)S(1)} %get-tuple-element.34), channel_id=1, source_target_pairs={{0,8},{2,10},{4,12},{6,14},{8,0},{10,2},{12,4},{14,6},{1,9},{3,11}... | collective-permute-start | bytes 129032 | tf_op jit(solution)/shard_map/ppermute | solution.py:27
  65.2 1.1 collective-permute-start.17
  66.3 1.4 %collective-permute-start.16 = (bf16[168,128]{1,0:T(8,128)(2,1)S(1)}, bf16[168,128]{1,0:T(8,128)(2,1)S(1)}, u32[]{:S(2)}, u32[]{:S(2)}) collective-permute-start(bf16[168,128]{1,0:T(8,128)(2,1)S(1)} %get-tuple-element.34), channel_id=1, source_target_pairs={{0,4},{2,6},{4,0},{6,2},{8,12},{10,14},{12,8},{14,10},{1,5},{3,7},... | collective-permute-start | bytes 129032 | tf_op jit(solution)/shard_map/ppermute | solution.py:27
  67.7 2.7 %collective-permute-done.16 = bf16[168,128]{1,0:T(8,128)(2,1)S(1)} collective-permute-done((bf16[168,128]{1,0:T(8,128)(2,1)S(1)}, bf16[168,128]{1,0:T(8,128)(2,1)S(1)}, u32[]{:S(2)}, u32[]{:S(2)}) %collective-permute-start.16) | collective-permute-done | bytes 43040 | tf_op jit(solution)/shard_map/ppermute | solution.py:27
  70.3 1.3 %collective-permute-start.21 = (bf16[168,128]{1,0:T(8,128)(2,1)S(1)}, bf16[168,128]{1,0:T(8,128)(2,1)S(1)}, u32[]{:S(2)}, u32[]{:S(2)}) collective-permute-start(bf16[168,128]{1,0:T(8,128)(2,1)S(1)} %get-tuple-element.34), channel_id=1, source_target_pairs={{0,14},{2,12},{4,10},{6,8},{8,6},{10,4},{12,2},{14,0},{1,15},{3,13... | collective-permute-start | bytes 129032 | tf_op jit(solution)/shard_map/ppermute | solution.py:27
  71.7 5.3 %collective-permute-done.21 = bf16[168,128]{1,0:T(8,128)(2,1)S(1)} collective-permute-done((bf16[168,128]{1,0:T(8,128)(2,1)S(1)}, bf16[168,128]{1,0:T(8,128)(2,1)S(1)}, u32[]{:S(2)}, u32[]{:S(2)}) %collective-permute-start.21) | collective-permute-done | bytes 43040 | tf_op jit(solution)/shard_map/ppermute | solution.py:27
  77.2 1.6 %collective-permute-done.22 = bf16[8,168,128]{2,1,0:T(8,128)(2,1)S(1)} collective-permute-done((bf16[8,168,128]{2,1,0:T(8,128)(2,1)S(1)}, bf16[8,168,128]{2,1,0:T(8,128)(2,1)S(1)}, u32[]{:S(2)}, u32[]{:S(2)}) %collective-permute-start.22) | collective-permute-done | bytes 344096 | tf_op jit(solution)/shard_map/ppermute | solution.py:30
  79.2 5.8 %fusion.44 = f32[48,576]{1,0:T(8,128)S(1)} fusion(bf16[48,7168]{1,0:T(8,128)(2,1)S(1)} %reshape.113, bf16[7168,576]{0,1:T(8,128)(2,1)} %param.19), kind=kOutput, calls=%fused_computation.103 | convolution fusion | flops 396361728 | bytes 9056256 | tf_op jit(solution)/shard_map/dot_general | solution.py:75
  85.0 10.2 %fusion.10 = f32[48,7168]{1,0:T(8,128)S(1)} fusion(bf16[576,7168]{1,0:T(8,128)(2,1)} %param.21, bf16[48,7168]{1,0:T(8,128)(2,1)S(1)} %reshape.113, bf16[7168,576]{0,1:T(8,128)(2,1)} %param.20, f32[48,576]{1,0:T(8,128)S(1)} %fusion.44), kind=kOutput, calls=%fused_computation.14 | convolution fusion | flops 792889344 | bytes 18690048 | tf_op jit(solution)/shard_map/dot_general | solution.py:78
  95.2 0.9 convert_element_type.110
  96.3 0.9 slice.100
  97.2 1.2 %squeeze.103 = f32[8,168,128]{2,1,0:T(8,128)S(1)} reshape(f32[24,7168]{1,0:T(8,128)} %slice.100) | data formatting | bytes 1376256 | tf_op jit(solution)/shard_map/squeeze | solution.py:33
  98.4 1.1 fusion.41
  99.5 0.9 collective-permute-start.24
  100.4 1.6 %collective-permute-start.30 = (bf16[168,128]{1,0:T(8,128)(2,1)S(1)}, bf16[168,128]{1,0:T(8,128)(2,1)S(1)}, u32[]{:S(2)}, u32[]{:S(2)}) collective-permute-start(bf16[168,128]{1,0:T(8,128)(2,1)S(1)} %get-tuple-element.18), channel_id=1, source_target_pairs={{0,14},{2,12},{4,10},{6,8},{8,6},{10,4},{12,2},{14,0},{1,15},{3,13... | collective-permute-start | bytes 129032 | tf_op jit(solution)/shard_map/ppermute | solution.py:27
  101.9 2.9 %collective-permute-start.29 = (bf16[168,128]{1,0:T(8,128)(2,1)S(1)}, bf16[168,128]{1,0:T(8,128)(2,1)S(1)}, u32[]{:S(2)}, u32[]{:S(2)}) collective-permute-start(bf16[168,128]{1,0:T(8,128)(2,1)S(1)} %get-tuple-element.19), channel_id=1, source_target_pairs={{0,12},{2,14},{4,8},{6,10},{8,4},{10,6},{12,0},{14,2},{1,13},{3,15... | collective-permute-start | bytes 129032 | tf_op jit(solution)/shard_map/ppermute | solution.py:27
  104.9 3.1 %collective-permute-start.27 = (bf16[168,128]{1,0:T(8,128)(2,1)S(1)}, bf16[168,128]{1,0:T(8,128)(2,1)S(1)}, u32[]{:S(2)}, u32[]{:S(2)}) collective-permute-start(bf16[168,128]{1,0:T(8,128)(2,1)S(1)} %get-tuple-element.21), channel_id=1, source_target_pairs={{0,8},{2,10},{4,12},{6,14},{8,0},{10,2},{12,4},{14,6},{1,9},{3,11}... | collective-permute-start | bytes 129032 | tf_op jit(solution)/shard_map/ppermute | solution.py:27
  108.0 2.7 %collective-permute-start.25 = (bf16[168,128]{1,0:T(8,128)(2,1)S(1)}, bf16[168,128]{1,0:T(8,128)(2,1)S(1)}, u32[]{:S(2)}, u32[]{:S(2)}) collective-permute-start(bf16[168,128]{1,0:T(8,128)(2,1)S(1)} %get-tuple-element.23), channel_id=1, source_target_pairs={{0,4},{2,6},{4,0},{6,2},{8,12},{10,14},{12,8},{14,10},{1,5},{3,7},... | collective-permute-start | bytes 129032 | tf_op jit(solution)/shard_map/ppermute | solution.py:27
  110.7 0.7 add_compare_fusion
  111.4 1.5 %collective-permute-done.26 = bf16[168,128]{1,0:T(8,128)(2,1)S(1)} collective-permute-done((bf16[168,128]{1,0:T(8,128)(2,1)S(1)}, bf16[168,128]{1,0:T(8,128)(2,1)S(1)}, u32[]{:S(2)}, u32[]{:S(2)}) %collective-permute-start.26) | collective-permute-done | bytes 43040 | tf_op jit(solution)/shard_map/ppermute | solution.py:27
  113.3 0.7 select_convert_fusion
  (74 shorter events, 4.1 us)
Async XLA Ops:
  0.0 30.0 %copy-start = (bf16[1,8,512,128]{3,2,1,0:T(8,128)(2,1)S(1)}, bf16[1,8,512,128]{3,2,1,0:T(8,128)(2,1)}, u32[]{:S(2)}) copy-start(bf16[1,8,512,128]{3,2,1,0:T(8,128)(2,1)} %param.16) | copy-start | bytes 3145732
  7.0 22.8 %collective-permute-start.6 = (bf16[6,8,512]{2,1,0:T(8,128)(2,1)S(1)}, bf16[6,8,512]{2,1,0:T(8,128)(2,1)S(1)}, u32[]{:S(2)}, u32[]{:S(2)}) collective-permute-start(bf16[6,8,512]{2,1,0:T(8,128)(2,1)S(1)} %get-tuple-element.9), channel_id=1, source_target_pairs={{0,14},{2,12},{4,10},{6,8},{8,6},{10,4},{12,2},{14,0},{1,15},{3,13... | collective-permute-start | bytes 147464 | tf_op jit(solution)/shard_map/ppermute | solution.py:27
  13.1 16.7 %collective-permute-start.5 = (bf16[6,8,512]{2,1,0:T(8,128)(2,1)S(1)}, bf16[6,8,512]{2,1,0:T(8,128)(2,1)S(1)}, u32[]{:S(2)}, u32[]{:S(2)}) collective-permute-start(bf16[6,8,512]{2,1,0:T(8,128)(2,1)S(1)} %get-tuple-element.10), channel_id=1, source_target_pairs={{0,12},{2,14},{4,8},{6,10},{8,4},{10,6},{12,0},{14,2},{1,13},{3,15... | collective-permute-start | bytes 147464 | tf_op jit(solution)/shard_map/ppermute | solution.py:27
  13.3 16.5 %collective-permute-start.4 = (bf16[6,8,512]{2,1,0:T(8,128)(2,1)S(1)}, bf16[6,8,512]{2,1,0:T(8,128)(2,1)S(1)}, u32[]{:S(2)}, u32[]{:S(2)}) collective-permute-start(bf16[6,8,512]{2,1,0:T(8,128)(2,1)S(1)} %get-tuple-element.11), channel_id=1, source_target_pairs={{0,10},{2,8},{4,14},{6,12},{8,2},{10,0},{12,6},{14,4},{1,11},{3,9}... | collective-permute-start | bytes 147464 | tf_op jit(solution)/shard_map/ppermute | solution.py:27
  14.1 15.7 %collective-permute-start.3 = (bf16[6,8,512]{2,1,0:T(8,128)(2,1)S(1)}, bf16[6,8,512]{2,1,0:T(8,128)(2,1)S(1)}, u32[]{:S(2)}, u32[]{:S(2)}) collective-permute-start(bf16[6,8,512]{2,1,0:T(8,128)(2,1)S(1)} %get-tuple-element.12), channel_id=1, source_target_pairs={{0,8},{2,10},{4,12},{6,14},{8,0},{10,2},{12,4},{14,6},{1,9},{3,11}... | collective-permute-start | bytes 147464 | tf_op jit(solution)/shard_map/ppermute | solution.py:27
  16.1 4.5 %collective-permute-start = (bf16[6,8,512]{2,1,0:T(8,128)(2,1)S(1)}, bf16[6,8,512]{2,1,0:T(8,128)(2,1)S(1)}, u32[]{:S(2)}, u32[]{:S(2)}) collective-permute-start(bf16[6,8,512]{2,1,0:T(8,128)(2,1)S(1)} %get-tuple-element.15), channel_id=1, source_target_pairs={{0,2},{2,0},{4,6},{6,4},{8,10},{10,8},{12,14},{14,12},{1,3},{3,1},... | collective-permute-start | bytes 147464 | tf_op jit(solution)/shard_map/ppermute | solution.py:27
  20.6 4.2 %collective-permute-start.1 = (bf16[6,8,512]{2,1,0:T(8,128)(2,1)S(1)}, bf16[6,8,512]{2,1,0:T(8,128)(2,1)S(1)}, u32[]{:S(2)}, u32[]{:S(2)}) collective-permute-start(bf16[6,8,512]{2,1,0:T(8,128)(2,1)S(1)} %get-tuple-element.14), channel_id=1, source_target_pairs={{0,4},{2,6},{4,0},{6,2},{8,12},{10,14},{12,8},{14,10},{1,5},{3,7},... | collective-permute-start | bytes 147464 | tf_op jit(solution)/shard_map/ppermute | solution.py:27
  24.8 5.0 %collective-permute-start.2 = (bf16[6,8,512]{2,1,0:T(8,128)(2,1)S(1)}, bf16[6,8,512]{2,1,0:T(8,128)(2,1)S(1)}, u32[]{:S(2)}, u32[]{:S(2)}) collective-permute-start(bf16[6,8,512]{2,1,0:T(8,128)(2,1)S(1)} %get-tuple-element.13), channel_id=1, source_target_pairs={{0,6},{2,4},{4,2},{6,0},{8,14},{10,12},{12,10},{14,8},{1,7},{3,5},... | collective-permute-start | bytes 147464 | tf_op jit(solution)/shard_map/ppermute | solution.py:27
  30.4 23.1 %copy-start.1 = (bf16[3,7168]{1,0:T(4,128)(2,1)S(1)}, bf16[3,7168]{1,0:T(4,128)(2,1)}, u32[]{:S(2)}) copy-start(bf16[3,7168]{1,0:T(4,128)(2,1)} %param.15) | copy-start | bytes 129028
  30.4 27.0 %copy-start.2 = (f32[7168]{0:T(1024)S(1)}, f32[7168]{0:T(1024)}, u32[]{:S(2)}) copy-start(f32[7168]{0:T(1024)} %param.18) | copy-start | bytes 86020
  39.2 2.0 %collective-permute-start.7 = (bf16[8,168,128]{2,1,0:T(8,128)(2,1)}, bf16[8,168,128]{2,1,0:T(8,128)(2,1)}, u32[]{:S(2)}, u32[]{:S(2)}) collective-permute-start(bf16[8,168,128]{2,1,0:T(8,128)(2,1)} %convert_element_type.97), channel_id=1, source_target_pairs={{0,1},{1,0},{2,3},{3,2},{4,5},{5,4},{6,7},{7,6},{8,9},{9,8},{10,11... | collective-permute-start | bytes 1032200 | tf_op jit(solution)/shard_map/ppermute | solution.py:30
  42.3 9.6 %collective-permute-start.8 = (bf16[168,128]{1,0:T(8,128)(2,1)S(1)}, bf16[168,128]{1,0:T(8,128)(2,1)S(1)}, u32[]{:S(2)}, u32[]{:S(2)}) collective-permute-start(bf16[168,128]{1,0:T(8,128)(2,1)S(1)} %get-tuple-element.24), channel_id=1, source_target_pairs={{0,2},{2,0},{4,6},{6,4},{8,10},{10,8},{12,14},{14,12},{1,3},{3,1},... | collective-permute-start | bytes 129032 | tf_op jit(solution)/shard_map/ppermute | solution.py:27
  44.3 8.6 %collective-permute-start.14 = (bf16[168,128]{1,0:T(8,128)(2,1)S(1)}, bf16[168,128]{1,0:T(8,128)(2,1)S(1)}, u32[]{:S(2)}, u32[]{:S(2)}) collective-permute-start(bf16[168,128]{1,0:T(8,128)(2,1)S(1)} %get-tuple-element.25), channel_id=1, source_target_pairs={{0,14},{2,12},{4,10},{6,8},{8,6},{10,4},{12,2},{14,0},{1,15},{3,13... | collective-permute-start | bytes 129032 | tf_op jit(solution)/shard_map/ppermute | solution.py:27
  47.2 6.3 %collective-permute-start.13 = (bf16[168,128]{1,0:T(8,128)(2,1)S(1)}, bf16[168,128]{1,0:T(8,128)(2,1)S(1)}, u32[]{:S(2)}, u32[]{:S(2)}) collective-permute-start(bf16[168,128]{1,0:T(8,128)(2,1)S(1)} %get-tuple-element.26), channel_id=1, source_target_pairs={{0,12},{2,14},{4,8},{6,10},{8,4},{10,6},{12,0},{14,2},{1,13},{3,15... | collective-permute-start | bytes 129032 | tf_op jit(solution)/shard_map/ppermute | solution.py:27
  47.6 7.7 %collective-permute-start.12 = (bf16[168,128]{1,0:T(8,128)(2,1)S(1)}, bf16[168,128]{1,0:T(8,128)(2,1)S(1)}, u32[]{:S(2)}, u32[]{:S(2)}) collective-permute-start(bf16[168,128]{1,0:T(8,128)(2,1)S(1)} %get-tuple-element.27), channel_id=1, source_target_pairs={{0,10},{2,8},{4,14},{6,12},{8,2},{10,0},{12,6},{14,4},{1,11},{3,9}... | collective-permute-start | bytes 129032 | tf_op jit(solution)/shard_map/ppermute | solution.py:27
  48.8 6.7 %collective-permute-start.11 = (bf16[168,128]{1,0:T(8,128)(2,1)S(1)}, bf16[168,128]{1,0:T(8,128)(2,1)S(1)}, u32[]{:S(2)}, u32[]{:S(2)}) collective-permute-start(bf16[168,128]{1,0:T(8,128)(2,1)S(1)} %get-tuple-element.28), channel_id=1, source_target_pairs={{0,8},{2,10},{4,12},{6,14},{8,0},{10,2},{12,4},{14,6},{1,9},{3,11}... | collective-permute-start | bytes 129032 | tf_op jit(solution)/shard_map/ppermute | solution.py:27
  51.9 4.9 %collective-permute-start.10 = (bf16[168,128]{1,0:T(8,128)(2,1)S(1)}, bf16[168,128]{1,0:T(8,128)(2,1)S(1)}, u32[]{:S(2)}, u32[]{:S(2)}) collective-permute-start(bf16[168,128]{1,0:T(8,128)(2,1)S(1)} %get-tuple-element.29), channel_id=1, source_target_pairs={{0,6},{2,4},{4,2},{6,0},{8,14},{10,12},{12,10},{14,8},{1,7},{3,5},... | collective-permute-start | bytes 129032 | tf_op jit(solution)/shard_map/ppermute | solution.py:27
  52.9 4.0 %collective-permute-start.9 = (bf16[168,128]{1,0:T(8,128)(2,1)S(1)}, bf16[168,128]{1,0:T(8,128)(2,1)S(1)}, u32[]{:S(2)}, u32[]{:S(2)}) collective-permute-start(bf16[168,128]{1,0:T(8,128)(2,1)S(1)} %get-tuple-element.30), channel_id=1, source_target_pairs={{0,4},{2,6},{4,0},{6,2},{8,12},{10,14},{12,8},{14,10},{1,5},{3,7},... | collective-permute-start | bytes 129032 | tf_op jit(solution)/shard_map/ppermute | solution.py:27
  57.5 8.8 %collective-permute-start.15 = (bf16[168,128]{1,0:T(8,128)(2,1)S(1)}, bf16[168,128]{1,0:T(8,128)(2,1)S(1)}, u32[]{:S(2)}, u32[]{:S(2)}) collective-permute-start(bf16[168,128]{1,0:T(8,128)(2,1)S(1)} %get-tuple-element.34), channel_id=1, source_target_pairs={{0,2},{2,0},{4,6},{6,4},{8,10},{10,8},{12,14},{14,12},{1,3},{3,1},... | collective-permute-start | bytes 129032 | tf_op jit(solution)/shard_map/ppermute | solution.py:27
  59.0 12.7 %collective-permute-start.20 = (bf16[168,128]{1,0:T(8,128)(2,1)S(1)}, bf16[168,128]{1,0:T(8,128)(2,1)S(1)}, u32[]{:S(2)}, u32[]{:S(2)}) collective-permute-start(bf16[168,128]{1,0:T(8,128)(2,1)S(1)} %get-tuple-element.34), channel_id=1, source_target_pairs={{0,12},{2,14},{4,8},{6,10},{8,4},{10,6},{12,0},{14,2},{1,13},{3,15... | collective-permute-start | bytes 129032 | tf_op jit(solution)/shard_map/ppermute | solution.py:27
  61.8 9.8 %collective-permute-start.19 = (bf16[168,128]{1,0:T(8,128)(2,1)S(1)}, bf16[168,128]{1,0:T(8,128)(2,1)S(1)}, u32[]{:S(2)}, u32[]{:S(2)}) collective-permute-start(bf16[168,128]{1,0:T(8,128)(2,1)S(1)} %get-tuple-element.34), channel_id=1, source_target_pairs={{0,10},{2,8},{4,14},{6,12},{8,2},{10,0},{12,6},{14,4},{1,11},{3,9}... | collective-permute-start | bytes 129032 | tf_op jit(solution)/shard_map/ppermute | solution.py:27
  61.8 9.8 %collective-permute-start.18 = (bf16[168,128]{1,0:T(8,128)(2,1)S(1)}, bf16[168,128]{1,0:T(8,128)(2,1)S(1)}, u32[]{:S(2)}, u32[]{:S(2)}) collective-permute-start(bf16[168,128]{1,0:T(8,128)(2,1)S(1)} %get-tuple-element.34), channel_id=1, source_target_pairs={{0,8},{2,10},{4,12},{6,14},{8,0},{10,2},{12,4},{14,6},{1,9},{3,11}... | collective-permute-start | bytes 129032 | tf_op jit(solution)/shard_map/ppermute | solution.py:27
  65.2 6.4 %collective-permute-start.17 = (bf16[168,128]{1,0:T(8,128)(2,1)S(1)}, bf16[168,128]{1,0:T(8,128)(2,1)S(1)}, u32[]{:S(2)}, u32[]{:S(2)}) collective-permute-start(bf16[168,128]{1,0:T(8,128)(2,1)S(1)} %get-tuple-element.34), channel_id=1, source_target_pairs={{0,6},{2,4},{4,2},{6,0},{8,14},{10,12},{12,10},{14,8},{1,7},{3,5},... | collective-permute-start | bytes 129032 | tf_op jit(solution)/shard_map/ppermute | solution.py:27
  66.3 4.0 %collective-permute-start.16 = (bf16[168,128]{1,0:T(8,128)(2,1)S(1)}, bf16[168,128]{1,0:T(8,128)(2,1)S(1)}, u32[]{:S(2)}, u32[]{:S(2)}) collective-permute-start(bf16[168,128]{1,0:T(8,128)(2,1)S(1)} %get-tuple-element.34), channel_id=1, source_target_pairs={{0,4},{2,6},{4,0},{6,2},{8,12},{10,14},{12,8},{14,10},{1,5},{3,7},... | collective-permute-start | bytes 129032 | tf_op jit(solution)/shard_map/ppermute | solution.py:27
  70.3 6.7 %collective-permute-start.21 = (bf16[168,128]{1,0:T(8,128)(2,1)S(1)}, bf16[168,128]{1,0:T(8,128)(2,1)S(1)}, u32[]{:S(2)}, u32[]{:S(2)}) collective-permute-start(bf16[168,128]{1,0:T(8,128)(2,1)S(1)} %get-tuple-element.34), channel_id=1, source_target_pairs={{0,14},{2,12},{4,10},{6,8},{8,6},{10,4},{12,2},{14,0},{1,15},{3,13... | collective-permute-start | bytes 129032 | tf_op jit(solution)/shard_map/ppermute | solution.py:27
  77.1 1.7 %collective-permute-start.22 = (bf16[8,168,128]{2,1,0:T(8,128)(2,1)S(1)}, bf16[8,168,128]{2,1,0:T(8,128)(2,1)S(1)}, u32[]{:S(2)}, u32[]{:S(2)}) collective-permute-start(bf16[8,168,128]{2,1,0:T(8,128)(2,1)S(1)} %bitcast_dynamic-update-slice_fusion), channel_id=1, source_target_pairs={{0,1},{1,0},{2,3},{3,2},{4,5},{5,4},{6,7},{7,6},{8,9},{9,8},{10,11... | collective-permute-start | bytes 1032200 | tf_op jit(solution)/shard_map/ppermute | solution.py:30
  96.1 2.2 %collective-permute-start.23 = (bf16[8,168,128]{2,1,0:T(8,128)(2,1)}, bf16[8,168,128]{2,1,0:T(8,128)(2,1)}, u32[]{:S(2)}, u32[]{:S(2)}) collective-permute-start(bf16[8,168,128]{2,1,0:T(8,128)(2,1)} %convert_element_type.110), channel_id=1, source_target_pairs={{0,1},{1,0},{2,3},{3,2},{4,5},{5,4},{6,7},{7,6},{8,9},{9,8},{10,11... | collective-permute-start | bytes 1032200 | tf_op jit(solution)/shard_map/ppermute | solution.py:30
  99.5 8.5 %collective-permute-start.24 = (bf16[168,128]{1,0:T(8,128)(2,1)S(1)}, bf16[168,128]{1,0:T(8,128)(2,1)S(1)}, u32[]{:S(2)}, u32[]{:S(2)}) collective-permute-start(bf16[168,128]{1,0:T(8,128)(2,1)S(1)} %get-tuple-element.17), channel_id=1, source_target_pairs={{0,2},{2,0},{4,6},{6,4},{8,10},{10,8},{12,14},{14,12},{1,3},{3,1},... | collective-permute-start | bytes 129032 | tf_op jit(solution)/shard_map/ppermute | solution.py:27
  100.4 7.7 %collective-permute-start.30 = (bf16[168,128]{1,0:T(8,128)(2,1)S(1)}, bf16[168,128]{1,0:T(8,128)(2,1)S(1)}, u32[]{:S(2)}, u32[]{:S(2)}) collective-permute-start(bf16[168,128]{1,0:T(8,128)(2,1)S(1)} %get-tuple-element.18), channel_id=1, source_target_pairs={{0,14},{2,12},{4,10},{6,8},{8,6},{10,4},{12,2},{14,0},{1,15},{3,13... | collective-permute-start | bytes 129032 | tf_op jit(solution)/shard_map/ppermute | solution.py:27
  101.9 9.4 %collective-permute-start.29 = (bf16[168,128]{1,0:T(8,128)(2,1)S(1)}, bf16[168,128]{1,0:T(8,128)(2,1)S(1)}, u32[]{:S(2)}, u32[]{:S(2)}) collective-permute-start(bf16[168,128]{1,0:T(8,128)(2,1)S(1)} %get-tuple-element.19), channel_id=1, source_target_pairs={{0,12},{2,14},{4,8},{6,10},{8,4},{10,6},{12,0},{14,2},{1,13},{3,15... | collective-permute-start | bytes 129032 | tf_op jit(solution)/shard_map/ppermute | solution.py:27
  104.9 6.5 %collective-permute-start.28 = (bf16[168,128]{1,0:T(8,128)(2,1)S(1)}, bf16[168,128]{1,0:T(8,128)(2,1)S(1)}, u32[]{:S(2)}, u32[]{:S(2)}) collective-permute-start(bf16[168,128]{1,0:T(8,128)(2,1)S(1)} %get-tuple-element.20), channel_id=1, source_target_pairs={{0,10},{2,8},{4,14},{6,12},{8,2},{10,0},{12,6},{14,4},{1,11},{3,9}... | collective-permute-start | bytes 129032 | tf_op jit(solution)/shard_map/ppermute | solution.py:27
  104.9 6.5 %collective-permute-start.27 = (bf16[168,128]{1,0:T(8,128)(2,1)S(1)}, bf16[168,128]{1,0:T(8,128)(2,1)S(1)}, u32[]{:S(2)}, u32[]{:S(2)}) collective-permute-start(bf16[168,128]{1,0:T(8,128)(2,1)S(1)} %get-tuple-element.21), channel_id=1, source_target_pairs={{0,8},{2,10},{4,12},{6,14},{8,0},{10,2},{12,4},{14,6},{1,9},{3,11}... | collective-permute-start | bytes 129032 | tf_op jit(solution)/shard_map/ppermute | solution.py:27
  108.0 4.9 %collective-permute-start.26 = (bf16[168,128]{1,0:T(8,128)(2,1)S(1)}, bf16[168,128]{1,0:T(8,128)(2,1)S(1)}, u32[]{:S(2)}, u32[]{:S(2)}) collective-permute-start(bf16[168,128]{1,0:T(8,128)(2,1)S(1)} %get-tuple-element.22), channel_id=1, source_target_pairs={{0,6},{2,4},{4,2},{6,0},{8,14},{10,12},{12,10},{14,8},{1,7},{3,5},... | collective-permute-start | bytes 129032 | tf_op jit(solution)/shard_map/ppermute | solution.py:27
  108.0 5.1 %collective-permute-start.25 = (bf16[168,128]{1,0:T(8,128)(2,1)S(1)}, bf16[168,128]{1,0:T(8,128)(2,1)S(1)}, u32[]{:S(2)}, u32[]{:S(2)}) collective-permute-start(bf16[168,128]{1,0:T(8,128)(2,1)S(1)} %get-tuple-element.23), channel_id=1, source_target_pairs={{0,4},{2,6},{4,0},{6,2},{8,12},{10,14},{12,8},{14,10},{1,5},{3,7},... | collective-permute-start | bytes 129032 | tf_op jit(solution)/shard_map/ppermute | solution.py:27

commit v2 on v1

v2 whole, which is shorter than its diff:
```python
import functools

import jax
import jax.numpy as jnp
from jax import lax
from jax.experimental import pallas as pl
from jax.experimental.pallas import tpu as pltpu
from jax.sharding import PartitionSpec as P

LATENT_WIDTH = 512
PARTS = 4

score_scale = 0.07216878364870322
norm_epsilon = 1e-06
masked_score = -1e30
f32 = jnp.float32
bf16 = jnp.bfloat16
VMEM = pltpu.VMEM
MIB = 1 << 20


def in_hbm(arrays):
    return [pltpu.with_memory_space_constraint(x, pltpu.HBM) for x in arrays]


def vmem(n):
    return [pl.BlockSpec(memory_space=VMEM)] * n


def params(mib):
    return pltpu.CompilerParams(vmem_limit_bytes=mib * MIB)


def load_kernel(count, pieces, *refs):
    sources, targets, sems = refs[1 : 1 + count], refs[1 + count : 1 + 2 * count], refs[1 + 2 * count]
    copies = row_copies(sources, targets, sems, pieces)
    for copy in copies:
        copy.start()
    for copy in copies:
        copy.wait()


def row_copies(sources, targets, sems, pieces):
    copies = []
    for n, (source, target) in enumerate(zip(sources, targets)):
        count = pieces if source.shape[0] % (16 * pieces) == 0 else 1
        step = source.shape[0] // count
        for p in range(count):
            at = pl.ds(p * step, step)
            copies.append(pltpu.make_async_copy(source.at[at], target.at[at], sems.at[n, p]))
    return copies


def load(after, weights, mib):
    pieces = 4
    size = sum(w.size for w in weights) * 2
    return pl.pallas_call(
        functools.partial(load_kernel, len(weights), pieces),
        out_shape=[jax.ShapeDtypeStruct(w.shape, w.dtype) for w in weights],
        in_specs=[pl.BlockSpec(memory_space=pl.ANY)] * (1 + len(weights)),
        out_specs=vmem(len(weights)),
        scratch_shapes=[pltpu.SemaphoreType.DMA((len(weights), pieces))],
        compiler_params=params(mib),
        cost_estimate=pl.CostEstimate(flops=0, bytes_accessed=2 * size, transcendentals=0),
        name="load",
    )(after, *in_hbm(weights))


def row_ids(rows, columns, slots):
    i = lax.broadcasted_iota(jnp.int32, (rows, columns), 0).astype(f32)
    unit = float(slots * PARTS)
    block = jnp.floor((i + 0.5) / unit)
    inner = i - block * unit
    part = jnp.floor((inner + 0.5) / slots)
    return part, block * slots + (inner - part * slots)


def attention_kernel(n_dp, counts_hbm, lengths_hbm, q_hbm, cache_hbm, *refs):
    n_weights = 2
    weights, outs = refs[:n_weights], refs[n_weights : n_weights + n_dp]
    loaded = refs[n_weights + n_dp : 2 * n_weights + n_dp]
    counts_ref, lengths_ref, q_ref, cache_ref, held, sems, scalar_sems, weight_sems = refs[2 * n_weights + n_dp :]
    fetches = row_copies(weights, loaded, weight_sems, weight_sems.shape[1])
    slots = q_ref.shape[0]
    scalars = [
        pltpu.make_async_copy(counts_hbm, counts_ref, scalar_sems.at[0]),
        pltpu.make_async_copy(lengths_hbm, lengths_ref, scalar_sems.at[1]),
    ]
    copies = []
    for row in range(slots):
        copies.append(
            (
                pltpu.make_async_copy(q_hbm.at[row], q_ref.at[row], sems.at[0, row]),
                pltpu.make_async_copy(cache_hbm.at[row], cache_ref.at[row], sems.at[1, row]),
            )
        )
    for copy in scalars + [c for pair in copies for c in pair]:
        copy.start()
    for copy in fetches:
        copy.start()
    for copy in scalars:
        copy.wait()
    me = lax.axis_index("dp")
    for row in range(slots):
        for copy in copies[row]:
            copy.wait()
        q = q_ref[row]
        cache = cache_ref[row]
        scores = lax.dot_general(q, cache, (((1,), (1,)), ((), ())), preferred_element_type=f32) * score_scale
        position = lax.broadcasted_iota(jnp.int32, scores.shape, 1)
        scores = jnp.where(position < lengths_ref[row], scores, masked_score)
        probs = jnp.exp(scores - jnp.max(scores, axis=-1, keepdims=True))
        denominator = jnp.sum(probs, axis=-1, keepdims=True)
        weighted = jnp.dot(probs.astype(bf16), cache[:, :LATENT_WIDTH], preferred_element_type=f32)
        latent = jnp.where(row < counts_ref[me], weighted / denominator, 0.0).astype(bf16)
        held[row] = latent.reshape(held.shape[1:])
    for k in range(n_dp):
        for row in range(slots):
            outs[k][row] = held[row, me ^ k]
    for copy in fetches:
        copy.wait()


def attend(n_dp, counts, lengths, queries, cache, weights):
    slots, heads, _ = queries.shape
    per_rank = heads // n_dp
    block = jax.ShapeDtypeStruct((slots, per_rank, LATENT_WIDTH), bf16)
    return pl.pallas_call(
        functools.partial(attention_kernel, n_dp),
        out_shape=[block] * n_dp + [jax.ShapeDtypeStruct(w.shape, w.dtype) for w in weights],
        in_specs=[pl.BlockSpec(memory_space=pl.ANY)] * (4 + len(weights)),
        out_specs=vmem(n_dp + len(weights)),
        scratch_shapes=[
            pltpu.SMEM(counts.shape, jnp.int32),
            pltpu.SMEM(lengths.shape, jnp.int32),
            VMEM(queries.shape, bf16),
            VMEM(cache.shape, bf16),
            VMEM((slots, n_dp, per_rank, LATENT_WIDTH), bf16),
            pltpu.SemaphoreType.DMA((2, slots)),
            pltpu.SemaphoreType.DMA((2,)),
            pltpu.SemaphoreType.DMA((len(weights), 2)),
        ],
        compiler_params=params(8),
        name="attend",
    )(*in_hbm([counts, lengths, queries, cache, *weights]))


def spread(rows, slots):
    wide_rows = rows * PARTS
    _, source = row_ids(wide_rows, rows, slots)
    column = lax.broadcasted_iota(jnp.int32, (wide_rows, rows), 1).astype(f32)
    return (source == column).astype(bf16)


def expand(x, slots):
    return jnp.dot(spread(x.shape[0], slots), x, preferred_element_type=f32).astype(bf16)


def write_units(wide_ref, weight_ref, acc_ref, keep_ref, give_ref, slots):
    rows, depth = wide_ref.shape
    part_width = acc_ref.shape[1]
    part, _ = row_ids(rows, depth, slots)
    for q in range(PARTS):
        wide = wide_ref[...]
        left = jnp.where(part == q, wide, jnp.zeros_like(wide))
        product = jnp.dot(left, weight_ref[:, pl.ds(q * part_width, part_width)], preferred_element_type=f32)
        if q == 0:
            acc_ref[...] = product
        elif q < PARTS - 1:
            acc_ref[...] += product
        else:
            product = acc_ref[...] + product
            keep_ref[...] = product[: rows // 2]
            give_ref[...] = product[rows // 2 :].astype(bf16)


def block_order(n_dp):
    return list(reversed(range(n_dp)))


def project_kernel(n_dp, slots, *refs):
    blocks = refs[:n_dp]
    up_ref, weight_ref, _, keep_ref, give_ref, rows_ref, values_ref, wide_ref, acc_ref = refs[n_dp:]
    per_rank = up_ref.shape[0]
    rows = n_dp * slots

    me_head = lax.axis_index("head")
    size = slots * per_rank
    for n, k in enumerate(block_order(n_dp)):
        place = ((k & 1) ^ me_head) * (n_dp // 2) + (k >> 1)
        x = blocks[n][...].astype(f32).reshape(size, -1)
        for c in range(rows_ref.shape[0]):
            rows_ref[c, pl.ds(pl.multiple_of(place * size, 4), size), :] = x[:, c * 128 : (c + 1) * 128]
    for j in range(per_rank):
        x = [rows_ref[c, pl.ds(j, rows, stride=per_rank), :] for c in range(rows_ref.shape[0])]
        x = jnp.concatenate(x, axis=1).astype(bf16)
        v = jnp.dot(x, up_ref[j], preferred_element_type=f32).astype(bf16)
        values_ref[:, pl.ds(j * v.shape[1], v.shape[1])] = v
    wide_ref[...] = expand(values_ref[...], slots)
    write_units(wide_ref, weight_ref, acc_ref, keep_ref, give_ref, slots)


def unit_mib(rows, part):
    return -(-8 * rows * PARTS * part * 4 // MIB)


def project(n_dp, blocks, value_up, weight, after):
    slots, per_rank, _ = blocks[0].shape
    depth, width = weight.shape
    rows = n_dp * slots
    part = width // PARTS
    own = rows * PARTS // 2
    out = lambda dtype: jax.ShapeDtypeStruct((own, part), dtype)
    return pl.pallas_call(
        functools.partial(project_kernel, n_dp, slots),
        out_shape=[out(f32), out(bf16)],
        in_specs=vmem(n_dp + 2) + [pl.BlockSpec(memory_space=pl.ANY)],
        out_specs=vmem(2),
        scratch_shapes=[
            VMEM((LATENT_WIDTH // 128, rows * per_rank, 128), f32),
            VMEM((rows, depth), bf16),
            VMEM((rows * PARTS, depth), bf16),
            VMEM((rows * PARTS, part), f32),
        ],
        compiler_params=params(unit_mib(rows, part)),
        name="project",
    )(*blocks, value_up, weight, after)


def add_kernel(n_units, keep_ref, got_ref, *outs):
    unit = outs[0].shape[0]
    for s in range(n_units):
        at = pl.ds(s * unit, unit)
        total = keep_ref[at, :] + got_ref[at, :].astype(f32)
        outs[s][...] = total.astype(bf16)
        if s == 0:
            outs[n_units][...] = total


def add_halves(n_units, keep, got):
    unit = keep.shape[0] // n_units
    shape = lambda dtype: jax.ShapeDtypeStruct((unit, keep.shape[1]), dtype)
    return pl.pallas_call(
        functools.partial(add_kernel, n_units),
        out_shape=[shape(bf16)] * n_units + [shape(f32)],
        in_specs=vmem(2),
        out_specs=vmem(n_units + 1),
        compiler_params=params(4),
        name="add_halves",
    )(keep, got)


def sum_kernel(n_units, *refs):
    own_ref, got, out_ref = refs[0], refs[1 : 1 + n_units], refs[-1]
    me_head = lax.axis_index("head")
    first = jnp.where(me_head == 0, own_ref[...], got[0][...].astype(f32))
    for ref in got[1:]:
        first = first + ref[...].astype(f32)
    out_ref[...] = first


def sum_units(own, got, after):
    return pl.pallas_call(
        functools.partial(sum_kernel, len(got)),
        out_shape=jax.ShapeDtypeStruct(own.shape, f32),
        in_specs=vmem(1 + len(got)) + [pl.BlockSpec(memory_space=pl.ANY)] * len(after),
        out_specs=vmem(1)[0],
        compiler_params=params(4),
        name="sum_units",
    )(own, *got, *after)


def prepare_kernel(slots, mine_ref, twin_ref, gain_ref, residual_ref, gains_ref):
    me_head = lax.axis_index("head")
    owner_rows = mine_ref.shape[0]
    part = residual_ref.shape[1]
    gain = gain_ref[...].reshape(1, PARTS * part)
    for q in range(PARTS):
        at = pl.ds(q * part, part)
        for ref, head in ((mine_ref, me_head), (twin_ref, 1 - me_head)):
            rows = ref[:, at].astype(f32)
            for r in range(owner_rows):
                residual_ref[pl.ds(q * slots + head * owner_rows + r, 1), :] = rows[r : r + 1]
        gains_ref[pl.ds(q * slots, slots), :] = jnp.broadcast_to(gain[:, q * part : (q + 1) * part], (slots, part))


def prepare(slots, mine, twin, gain):
    shape = jax.ShapeDtypeStruct((slots * PARTS, gain.shape[0] // PARTS), f32)
    return pl.pallas_call(
        functools.partial(prepare_kernel, slots),
        out_shape=[shape] * 2,
        in_specs=vmem(3),
        out_specs=vmem(2),
        compiler_params=params(4),
        name="prepare",
    )(mine, twin, gain)


def norm_kernel(slots, width, mine_ref, twin_ref, residual_ref, gain_ref, state_ref, normed_ref):
    state = mine_ref[...] + twin_ref[...] + residual_ref[...]
    state_ref[...] = state
    square = jnp.sum(state * state, axis=1, keepdims=True)
    rows = state.shape[0]
    _, slot = row_ids(rows, 1, slots)
    mean = jnp.zeros_like(square)
    for r in range(slots):
        total = jnp.sum(jnp.where(slot == r, square, 0.0), axis=0, keepdims=True)
        mean = jnp.where(slot == r, total, mean)
    scaled = state * lax.rsqrt(mean * (1.0 / width) + norm_epsilon)
    normed_ref[...] = (scaled * gain_ref[...]).astype(bf16)


def norm_rows(slots, mine, twin, residual, gain):
    shape = mine.shape
    return pl.pallas_call(
        functools.partial(norm_kernel, slots, shape[1] * PARTS),
        out_shape=[jax.ShapeDtypeStruct(shape, f32), jax.ShapeDtypeStruct(shape, bf16)],
        in_specs=vmem(4),
        out_specs=vmem(2),
        compiler_params=params(4),
        name="norm_rows",
    )(mine, twin, residual, gain)


def ffn_kernel(n_dp, slots, *refs):
    half = n_dp // 2
    normed_ref = refs[0]
    own, other = refs[1 : 1 + half], refs[1 + half : 1 + n_dp]
    gate_ref, up_ref, down_ref, keep_ref, give_ref, units_ref, wide_ref, acc_ref = refs[1 + n_dp :]
    rows = n_dp * slots
    unit, part = normed_ref.shape
    me_head = lax.axis_index("head")
    for s in range(half):
        mine, twins = own[s][...], other[s][...]
        if s == 0:
            mine = jnp.where(me_head == 0, normed_ref[...], mine)
            twins = jnp.where(me_head == 0, twins, normed_ref[...])
        units_ref[pl.ds(s * unit, unit), :] = mine
        units_ref[pl.ds((half + s) * unit, unit), :] = twins
    i = lax.broadcasted_iota(jnp.int32, (rows, rows * PARTS), 0).astype(f32)
    j = lax.broadcasted_iota(jnp.int32, (rows, rows * PARTS), 1).astype(f32)
    block = jnp.floor((i + 0.5) / slots)
    first = block * float(unit) + (i - block * slots)
    contract = (((1,), (1,)), ((), ()))
    gate = up = None
    for q in range(PARTS):
        pick = (first + float(q * slots) == j).astype(bf16)
        x = jnp.dot(pick, units_ref[...], preferred_element_type=f32).astype(bf16)
        at = pl.ds(q * part, part)
        gate_q = lax.dot_general(x, gate_ref[:, at], contract, preferred_element_type=f32)
        up_q = lax.dot_general(x, up_ref[:, at], contract, preferred_element_type=f32)
        gate = gate_q if q == 0 else gate + gate_q
        up = up_q if q == 0 else up + up_q
    hidden = (gate / (1.0 + jnp.exp(-gate)) * up).astype(bf16)
    wide_ref[...] = expand(hidden, slots)
    write_units(wide_ref, down_ref, acc_ref, keep_ref, give_ref, slots)


def feed_forward(n_dp, slots, normed, own, other, gate_t, up_t, down):
    _, part = normed.shape
    rows = n_dp * slots
    hidden = gate_t.shape[0]
    out = lambda dtype: jax.ShapeDtypeStruct((rows * PARTS // 2, part), dtype)
    return pl.pallas_call(
        functools.partial(ffn_kernel, n_dp, slots),
        out_shape=[out(f32), out(bf16)],
        in_specs=vmem(1 + n_dp + 3),
        out_specs=vmem(2),
        scratch_shapes=[
            VMEM((rows * PARTS, part), bf16),
            VMEM((rows * PARTS, hidden), bf16),
            VMEM((rows * PARTS, part), f32),
        ],
        compiler_params=params(unit_mib(rows, part)),
        name="feed_forward",
    )(normed, *own, *other, gate_t, up_t, down)


def final_kernel(slots, owner_rows, counts_ref, mine_ref, twin_ref, state_ref, out_ref):
    me, me_head = lax.axis_index("dp"), lax.axis_index("head")
    total = state_ref[...] + (mine_ref[...] + twin_ref[...])
    rows = total.shape[0]
    _, slot = row_ids(rows, 1, slots)
    total = jnp.where(slot < counts_ref[me].astype(f32), total, 0.0).astype(bf16)
    part = total.shape[1]
    padded = 8
    i = lax.broadcasted_iota(jnp.int32, (padded, rows), 0)
    j = lax.broadcasted_iota(jnp.int32, (padded, rows), 1)
    for q in range(PARTS):
        pick = (j == q * slots + me_head * owner_rows + i).astype(bf16)
        chosen = jnp.dot(pick, total, preferred_element_type=f32)
        out_ref[:, pl.ds(q * part, part)] = chosen[:owner_rows].astype(bf16)


def final_rows(slots, owner_rows, counts, mine, twin, state):
    return pl.pallas_call(
        functools.partial(final_kernel, slots, owner_rows),
        out_shape=jax.ShapeDtypeStruct((owner_rows, mine.shape[1] * PARTS), bf16),
        in_specs=[pl.BlockSpec(memory_space=pltpu.SMEM)] + vmem(3),
        out_specs=vmem(1)[0],
        compiler_params=params(4),
        name="final_rows",
    )(counts, mine, twin, state)


def on_device(n_dp, queries, latent_key_cache, lengths, counts, residual, value_up_weight,
              output_proj, norm_gain, gate_weight, up_weight, down_weight):
    slots = queries.shape[0]
    owner_rows = residual.shape[0]
    half = n_dp // 2

    def to_peer(x, k):
        return lax.ppermute(x, "dp", [(i, i ^ k) for i in range(n_dp)])

    def to_twin(x):
        return lax.ppermute(x, "head", [(0, 1), (1, 0)])

    def to_set(x, s):
        pairs = [(2 * i + h, 2 * (i ^ (2 * s + h)) + h) for i in range(n_dp) for h in range(2) if 2 * s + h]
        return lax.ppermute(x, ("dp", "head"), pairs)

    def reduce_units(keep, give, weights):
        units = add_halves(half, keep, to_twin(give))
        weights = load(units[half], weights, 2) if weights else []
        mine = sum_units(units[half], [to_set(units[s], s) for s in range(half)], weights)
        return mine, to_twin(mine), weights

    residual_unit, gain_unit = prepare(slots, residual, to_twin(residual), norm_gain)
    outs = attend(n_dp, counts, lengths, queries, latent_key_cache, [value_up_weight[0], output_proj[0]])
    blocks, (value_up, proj) = outs[:n_dp], outs[n_dp:]
    (gate,) = load(blocks[0], [gate_weight.T], 2)
    blocks = [to_peer(blocks[k], k) if k else blocks[0] for k in block_order(n_dp)]
    keep, give = project(n_dp, blocks, value_up, proj, gate)
    mine, twin, (up, down) = reduce_units(keep, give, [up_weight.T, down_weight])
    state, normed = norm_rows(slots, mine, twin, residual_unit, gain_unit)
    own = [to_set(normed, s) for s in range(half)]
    other = [to_twin(x) for x in own]
    keep, give = feed_forward(n_dp, slots, normed, own, other, gate, up, down)
    mine, twin, _ = reduce_units(keep, give, [])
    return final_rows(slots, owner_rows, counts, mine, twin, state)


def solution(mesh):
    n_dp = mesh.shape["dp"]
    in_specs = (
        P(("groups", "dp"), "head", None),
        P(("groups", "dp"), None, None),
        P(("groups", "dp")),
        P("groups"),
        P(("groups", "dp", "head"), None),
        P("head", "dp", None, None),
        P("head", "dp", None),
        P(),
        P(None, ("dp", "head")),
        P(None, ("dp", "head")),
        P(("dp", "head"), None),
    )
    out_specs = P(("groups", "dp", "head"), None)

    def step(*args):
        return on_device(n_dp, *args)

    return jax.shard_map(step, mesh=mesh, in_specs=in_specs, out_specs=out_specs, check_vma=False)
```

time: 114 us -> 82.3 us (0.72)
  Pallas kernels: 0 us -> 29.1 us
  matrix products: 28.2 us -> 0 us
  starting transfers between devices: 47.5 us -> 36.6 us
  waiting for transfers between devices: 25.9 us -> 16.2 us
  other arithmetic: 7.03 us -> 0 us
  local copies, waits for them, and re-layouts: 4.95 us -> 0.01 us
    ppermute x28 -> x7, starting transfers between devices: 47.3 us -> 12.6 us  [to_peer(): return lax.ppermute(x, 'dp', [(i, i ^ k) for i in range(n_dp)])]
    pallas_call x0 -> x12, Pallas kernels: none -> 29.1 us  [the longest x2 9.31 us: load(): pl.pallas_call(functools.partial(load_kernel, len(weights), pieces), out_...]
    dot_general x6 -> x0, matrix products: 28.2 us -> none  [the longest x1 10.2 us: on_device(): part = jnp.dot(hidden, down_weight, preferred_element_type=f32)]
    ppermute x28 -> x7, waiting for transfers between devices: 22.4 us -> 0.18 us  [to_peer(): return lax.ppermute(x, 'dp', [(i, i ^ k) for i in range(n_dp)])]
    ppermute x0 -> x12, starting transfers between devices: none -> 15.5 us  [to_set(): return lax.ppermute(x, ('dp', 'head'), pairs)]
    ppermute x0 -> x12, waiting for transfers between devices: none -> 10.2 us  [to_set(): return lax.ppermute(x, ('dp', 'head'), pairs)]
    ppermute x3 -> x9, starting transfers between devices: 0.2 us -> 8.49 us  [to_twin(): return lax.ppermute(x, 'head', [(0, 1), (1, 0)])]
    convert_element_type x3 -> x0, other arithmetic: 2.85 us -> none  [the longest x2 2.14 us: reduce_rows(): sent = mine.astype(bf16)]
  transfers between devices with their start and end apart: 31 -> 28, of which waited for: 13 -> 14; matrix products, arithmetic and copies ran while one was open for 3% -> 0% of each run, Pallas kernels for 0% -> 11%
where the time goes in v2:
time: 82.3 us; the launch traced here: 82.1 us
  starting transfers between devices  36.6 us (44%)
  Pallas kernels  29.1 us (35%)
  waiting for transfers between devices  16.2 us (20%)
    ppermute x12, starting transfers between devices, to_set(): return lax.ppermute(x, ('dp', 'head'), pairs)  15.5 us
    ppermute x7, starting transfers between devices, to_peer(): return lax.ppermute(x, 'dp', [(i, i ^ k) for i in range(n_dp)])  12.6 us
    ppermute x12, waiting for transfers between devices, to_set(): return lax.ppermute(x, ('dp', 'head'), pairs)  10.2 us
    pallas_call x2, Pallas kernels, load(): pl.pallas_call(functools.partial(load_kernel, len(weights), pieces), out_...  9.31 us
    ppermute x9, starting transfers between devices, to_twin(): return lax.ppermute(x, 'head', [(0, 1), (1, 0)])  8.49 us
    pallas_call x1, Pallas kernels, feed_forward(): pl.pallas_call(functools.partial(ffn_kernel, n_dp, slots), out_shape=[out...  7.97 us
    pallas_call x1, Pallas kernels, attend(): pl.pallas_call(functools.partial(attention_kernel, n_dp), out_shape=[bloc...  6.38 us
    ppermute x9, waiting for transfers between devices, to_twin(): return lax.ppermute(x, 'head', [(0, 1), (1, 0)])  5.8 us
  transfers between devices with their start and end apart: 28, of which 14 were waited for; matrix products, arithmetic and copies ran while one was open for 0% of the time, Pallas kernels for 11%

profile of v2, /device:TPU:0, one launch (start us, length us, event | category | flops | bytes accessed | tf_op | source)
XLA Modules:
  0.0 82.1 jit_solution(11038942897729606621)
XLA Ops:
  0.0 6.4 %attend.1 = (bf16[6,8,512]{2,1,0:T(8,128)(2,1)S(1)}, bf16[6,8,512]{2,1,0:T(8,128)(2,1)S(1)}, bf16[6,8,512]{2,1,0:T(8,128)(2,1)S(1)}, bf16[6,8,512]{2,1,0:T(8,128...) custom-call(s32[8]{0:T(128)} %counts_ref.1, ...), custom_call_target="tpu_custom_call" | custom-call | tf_op jit(solution)/shard_map/attend/pallas_call | solution.py:128
  6.4 6.1 %collective-permute-start = (bf16[6,8,512]{2,1,0:T(8,128)(2,1)S(1)}, bf16[6,8,512]{2,1,0:T(8,128)(2,1)S(1)}, u32[]{:S(2)}, u32[]{:S(2)}) collective-permute-start(bf16[6,8,512]{2,1,0:T(8,128)(2,1)S(1)} %get-tuple-element.35), channel_id=1, source_target_pairs={{0,14},{2,12},{4,10},{6,8},{8,6},{10,4},{12,2},{14,0},{1,15},{3,13... | collective-permute-start | bytes 147464 | tf_op jit(solution)/shard_map/ppermute | solution.py:413
  12.5 0.2 collective-permute-start.1
  12.7 0.7 collective-permute-start.2
  13.4 2.0 %collective-permute-start.3 = (bf16[6,8,512]{2,1,0:T(8,128)(2,1)S(1)}, bf16[6,8,512]{2,1,0:T(8,128)(2,1)S(1)}, u32[]{:S(2)}, u32[]{:S(2)}) collective-permute-start(bf16[6,8,512]{2,1,0:T(8,128)(2,1)S(1)} %get-tuple-element.38), channel_id=1, source_target_pairs={{0,8},{2,10},{4,12},{6,14},{8,0},{10,2},{12,4},{14,6},{1,9},{3,11}... | collective-permute-start | bytes 147464 | tf_op jit(solution)/shard_map/ppermute | solution.py:413
  15.5 2.3 %collective-permute-start.4 = (bf16[6,8,512]{2,1,0:T(8,128)(2,1)S(1)}, bf16[6,8,512]{2,1,0:T(8,128)(2,1)S(1)}, u32[]{:S(2)}, u32[]{:S(2)}) collective-permute-start(bf16[6,8,512]{2,1,0:T(8,128)(2,1)S(1)} %get-tuple-element.39), channel_id=1, source_target_pairs={{0,6},{2,4},{4,2},{6,0},{8,14},{10,12},{12,10},{14,8},{1,7},{3,5},... | collective-permute-start | bytes 147464 | tf_op jit(solution)/shard_map/ppermute | solution.py:413
  17.8 0.8 collective-permute-start.5
  18.5 0.4 collective-permute-start.6
  19.0 3.5 %load.2.refs_10_.refs_9_ = bf16[576,7168]{1,0:T(8,128)(2,1)S(1)} custom-call(bf16[6,8,512]{2,1,0:T(8,128)(2,1)S(1)} %get-tuple-element.42.refs_0_.refs_7_, bf16[576,7168]{1,0:T(8,128)(2,1)} %bitcast.5), custom_call_target="tpu_custom_call" | custom-call | bytes 16515072 | tf_op jit(solution)/shard_map/load/pallas_call | solution.py:57
  22.5 0.2 collective-permute-done.6.refs_6_
  22.6 3.6 %project.1 = (f32[96,1792]{1,0:T(8,128)S(1)}, bf16[96,1792]{1,0:T(8,128)(2,1)S(1)}) custom-call(bf16[6,8,512]{2,1,0:T(8,128)(2,1)S(1)} %collective-permute-done.refs_0_, bf16[6,8,512]{2,1,0:T(8,128)(2,1)S(1)} %collective-permute-done.1.refs_1_, bf16[6,8,512]{2,1,0:T(8,128)(2,1)S(1)} %collective-permute-done.2.refs_2_, ...), custom_call_target="tpu_custom_call" | custom-call | tf_op jit(solution)/shard_map/project/pallas_call | solution.py:214
  26.3 1.6 %collective-permute-done.7.got_ref = bf16[96,1792]{1,0:T(8,128)(2,1)S(1)} collective-permute-done((bf16[96,1792]{1,0:T(8,128)(2,1)S(1)}, bf16[96,1792]{1,0:T(8,128)(2,1)S(1)}, u32[]{:S(2)}, u32[]{:S(2)}) %collective-permute-start.7) | collective-permute-done | bytes 344096 | tf_op jit(solution)/shard_map/ppermute | solution.py:416
  28.0 0.7 collective-permute-start.8
  28.7 1.3 %collective-permute-start.9 = (bf16[24,1792]{1,0:T(8,128)(2,1)S(1)}, bf16[24,1792]{1,0:T(8,128)(2,1)S(1)}, u32[]{:S(2)}, u32[]{:S(2)}) collective-permute-start(bf16[24,1792]{1,0:T(8,128)(2,1)S(1)} %get-tuple-element.49), channel_id=1, source_target_pairs={{0,4},{1,7},{2,6},{3,5},{4,0},{5,3},{6,2},{7,1},{8,12},{9,15},{10,... | collective-permute-start | bytes 258056 | tf_op jit(solution)/shard_map/ppermute | solution.py:420
  30.0 2.9 %collective-permute-start.10 = (bf16[24,1792]{1,0:T(8,128)(2,1)S(1)}, bf16[24,1792]{1,0:T(8,128)(2,1)S(1)}, u32[]{:S(2)}, u32[]{:S(2)}) collective-permute-start(bf16[24,1792]{1,0:T(8,128)(2,1)S(1)} %get-tuple-element.50), channel_id=1, source_target_pairs={{0,8},{1,11},{2,10},{3,9},{4,12},{5,15},{6,14},{7,13},{8,0},{9,3},... | collective-permute-start | bytes 258056 | tf_op jit(solution)/shard_map/ppermute | solution.py:420
  32.9 0.2 collective-permute-start.11
  33.1 5.9 %load.3 = (bf16[576,7168]{1,0:T(8,128)(2,1)S(1)}, bf16[576,7168]{1,0:T(8,128)(2,1)S(1)}) custom-call(f32[24,1792]{1,0:T(8,128)S(1)} %get-tuple-element.47.refs_0_, bf16[576,7168]{1,0:T(8,128)(2,1)} %bitcast.6, bf16[576,7168]{1,0:T(8,128)(2,1)} %refs_2_.1), custom_call_target="tpu_custom_call" | custom-call | bytes 33030144 | tf_op jit(solution)/shard_map/load/pallas_call | solution.py:57
  39.0 0.2 collective-permute-done.11.refs_4_
  39.3 2.8 %collective-permute-start.12 = (f32[24,1792]{1,0:T(8,128)S(1)}, f32[24,1792]{1,0:T(8,128)S(1)}, u32[]{:S(2)}, u32[]{:S(2)}) collective-permute-start(f32[24,1792]{1,0:T(8,128)S(1)} %sum_units.2.mine_ref), channel_id=1, source_target_pairs={{0,1},{1,0},{2,3},{3,2},{4,5},{5,4},{6,7},{7,6},{8,9},{9,8},{10,11... | collective-permute-start | bytes 516104 | tf_op jit(solution)/shard_map/ppermute | solution.py:416
  42.1 0.7 collective-permute-start.13
  42.8 0.9 %collective-permute-done.13.twin_ref = bf16[3,7168]{1,0:T(4,128)(2,1)S(1)} collective-permute-done((bf16[3,7168]{1,0:T(4,128)(2,1)S(1)}, bf16[3,7168]{1,0:T(4,128)(2,1)S(1)}, u32[]{:S(2)}, u32[]{:S(2)}) %collective-permute-start.13) | collective-permute-done | bytes 43040 | tf_op jit(solution)/shard_map/ppermute | solution.py:416
  43.7 0.1 prepare.1
  43.8 0.2 norm_rows.1
  43.9 3.4 %collective-permute-start.17 = (bf16[24,1792]{1,0:T(8,128)(2,1)S(1)}, bf16[24,1792]{1,0:T(8,128)(2,1)S(1)}, u32[]{:S(2)}, u32[]{:S(2)}) collective-permute-start(bf16[24,1792]{1,0:T(8,128)(2,1)S(1)} %get-tuple-element.56.refs_0_), channel_id=1, source_target_pairs={{0,12},{1,15},{2,14},{3,13},{4,8},{5,11},{6,10},{7,9},{8,4},{9,7},... | collective-permute-start | bytes 258056 | tf_op jit(solution)/shard_map/ppermute | solution.py:420
  47.3 1.1 %collective-permute-start.15 = (bf16[24,1792]{1,0:T(8,128)(2,1)S(1)}, bf16[24,1792]{1,0:T(8,128)(2,1)S(1)}, u32[]{:S(2)}, u32[]{:S(2)}) collective-permute-start(bf16[24,1792]{1,0:T(8,128)(2,1)S(1)} %get-tuple-element.56.refs_0_), channel_id=1, source_target_pairs={{0,4},{1,7},{2,6},{3,5},{4,0},{5,3},{6,2},{7,1},{8,12},{9,15},{10,... | collective-permute-start | bytes 258056 | tf_op jit(solution)/shard_map/ppermute | solution.py:420
  48.4 0.8 %collective-permute-start.14 = (bf16[24,1792]{1,0:T(8,128)(2,1)S(1)}, bf16[24,1792]{1,0:T(8,128)(2,1)S(1)}, u32[]{:S(2)}, u32[]{:S(2)}) collective-permute-start(bf16[24,1792]{1,0:T(8,128)(2,1)S(1)} %get-tuple-element.56.refs_0_), channel_id=1, source_target_pairs={{1,3},{3,1},{5,7},{7,5},{9,11},{11,9},{13,15},{15,13},{17,19},{19,... | collective-permute-start | bytes 258056 | tf_op jit(solution)/shard_map/ppermute | solution.py:420
  49.2 2.0 %collective-permute-done.17.refs_4_ = bf16[24,1792]{1,0:T(8,128)(2,1)S(1)} collective-permute-done((bf16[24,1792]{1,0:T(8,128)(2,1)S(1)}, bf16[24,1792]{1,0:T(8,128)(2,1)S(1)}, u32[]{:S(2)}, u32[]{:S(2)}) %collective-permute-start.17) | collective-permute-done | bytes 86048 | tf_op jit(solution)/shard_map/ppermute | solution.py:420
  51.3 0.9 %collective-permute-start.21 = (bf16[24,1792]{1,0:T(8,128)(2,1)S(1)}, bf16[24,1792]{1,0:T(8,128)(2,1)S(1)}, u32[]{:S(2)}, u32[]{:S(2)}) collective-permute-start(bf16[24,1792]{1,0:T(8,128)(2,1)S(1)} %collective-permute-done.17.refs_4_), channel_id=1, source_target_pairs={{0,1},{1,0},{2,3},{3,2},{4,5},{5,4},{6,7},{7,6},{8,9},{9,8},{10,11... | collective-permute-start | bytes 258056 | tf_op jit(solution)/shard_map/ppermute | solution.py:416
  52.1 2.8 %collective-permute-done.16.refs_3_ = bf16[24,1792]{1,0:T(8,128)(2,1)S(1)} collective-permute-done((bf16[24,1792]{1,0:T(8,128)(2,1)S(1)}, bf16[24,1792]{1,0:T(8,128)(2,1)S(1)}, u32[]{:S(2)}, u32[]{:S(2)}) %collective-permute-start.16) | collective-permute-done | bytes 86048 | tf_op jit(solution)/shard_map/ppermute | solution.py:420
  54.9 0.5 collective-permute-start.20
  55.5 0.5 collective-permute-start.18
  56.0 0.4 collective-permute-done.20.refs_7_
  56.4 0.4 collective-permute-done.19.refs_6_
  56.8 0.2 collective-permute-done.18.refs_5_
  56.9 8.0 %feed_forward.1 = (f32[96,1792]{1,0:T(8,128)S(1)}, bf16[96,1792]{1,0:T(8,128)(2,1)S(1)}) custom-call(bf16[24,1792]{1,0:T(8,128)(2,1)S(1)} %get-tuple-element.56.refs_0_, bf16[24,1792]{1,0:T(8,128)(2,1)S(1)} %collective-permute-done.14.refs_1_, bf16[24,1792]{1,0:T(8,128)(2,1)S(1)} %collective-permute-done.15.refs_2_, ...), custom_call_target="tpu_custom_call" | custom-call | tf_op jit(solution)/shard_map/feed_forward/pallas_call | solution.py:364
  64.9 0.4 collective-permute-start.22
  65.3 1.3 %collective-permute-done.22.got_ref = bf16[96,1792]{1,0:T(8,128)(2,1)S(1)} collective-permute-done((bf16[96,1792]{1,0:T(8,128)(2,1)S(1)}, bf16[96,1792]{1,0:T(8,128)(2,1)S(1)}, u32[]{:S(2)}, u32[]{:S(2)}) %collective-permute-start.22) | collective-permute-done | bytes 344096 | tf_op jit(solution)/shard_map/ppermute | solution.py:416
  66.6 0.1 add_halves.3
  66.7 0.7 collective-permute-start.23
  67.4 0.8 collective-permute-start.24
  68.1 2.6 %collective-permute-start.25 = (bf16[24,1792]{1,0:T(8,128)(2,1)S(1)}, bf16[24,1792]{1,0:T(8,128)(2,1)S(1)}, u32[]{:S(2)}, u32[]{:S(2)}) collective-permute-start(bf16[24,1792]{1,0:T(8,128)(2,1)S(1)} %get-tuple-element.62), channel_id=1, source_target_pairs={{0,8},{1,11},{2,10},{3,9},{4,12},{5,15},{6,14},{7,13},{8,0},{9,3},... | collective-permute-start | bytes 258056 | tf_op jit(solution)/shard_map/ppermute | solution.py:420
  70.8 1.0 %collective-permute-start.26 = (bf16[24,1792]{1,0:T(8,128)(2,1)S(1)}, bf16[24,1792]{1,0:T(8,128)(2,1)S(1)}, u32[]{:S(2)}, u32[]{:S(2)}) collective-permute-start(bf16[24,1792]{1,0:T(8,128)(2,1)S(1)} %get-tuple-element.63), channel_id=1, source_target_pairs={{0,12},{1,15},{2,14},{3,13},{4,8},{5,11},{6,10},{7,9},{8,4},{9,7},... | collective-permute-start | bytes 258056 | tf_op jit(solution)/shard_map/ppermute | solution.py:420
  71.8 0.1 collective-permute-done.24.refs_2_
  71.9 1.8 %collective-permute-done.25.refs_3_ = bf16[24,1792]{1,0:T(8,128)(2,1)S(1)} collective-permute-done((bf16[24,1792]{1,0:T(8,128)(2,1)S(1)}, bf16[24,1792]{1,0:T(8,128)(2,1)S(1)}, u32[]{:S(2)}, u32[]{:S(2)}) %collective-permute-start.25) | collective-permute-done | bytes 86048 | tf_op jit(solution)/shard_map/ppermute | solution.py:420
  73.7 3.4 %collective-permute-done.26.refs_4_ = bf16[24,1792]{1,0:T(8,128)(2,1)S(1)} collective-permute-done((bf16[24,1792]{1,0:T(8,128)(2,1)S(1)}, bf16[24,1792]{1,0:T(8,128)(2,1)S(1)}, u32[]{:S(2)}, u32[]{:S(2)}) %collective-permute-start.26) | collective-permute-done | bytes 86048 | tf_op jit(solution)/shard_map/ppermute | solution.py:420
  77.1 2.6 %collective-permute-start.27 = (f32[24,1792]{1,0:T(8,128)S(1)}, f32[24,1792]{1,0:T(8,128)S(1)}, u32[]{:S(2)}, u32[]{:S(2)}) collective-permute-start(f32[24,1792]{1,0:T(8,128)S(1)} %sum_units.3.mine_ref), channel_id=1, source_target_pairs={{0,1},{1,0},{2,3},{3,2},{4,5},{5,4},{6,7},{7,6},{8,9},{9,8},{10,11... | collective-permute-start | bytes 516104 | tf_op jit(solution)/shard_map/ppermute | solution.py:416
  79.7 1.0 %collective-permute-done.27.twin_ref = f32[24,1792]{1,0:T(8,128)S(1)} collective-permute-done((f32[24,1792]{1,0:T(8,128)S(1)}, f32[24,1792]{1,0:T(8,128)S(1)}, u32[]{:S(2)}, u32[]{:S(2)}) %collective-permute-start.27) | collective-permute-done | bytes 172064 | tf_op jit(solution)/shard_map/ppermute | solution.py:416
  80.7 1.4 %final_rows.1 = bf16[3,7168]{1,0:T(4,128)(2,1)} custom-call(s32[8]{0:T(128)S(1)} %copy-done.2, f32[24,1792]{1,0:T(8,128)S(1)} %sum_units.3.mine_ref, f32[24,1792]{1,0:T(8,128)S(1)} %collective-permute-done.27.twin_ref, f32[24,1792]{1,0:T(8,128)S(1)} %get-tuple-element.64.state_ref), custom_call_target="tpu_custom_call" | custom-call | tf_op jit(solution)/shard_map/final_rows/pallas_call | solution.py:396
  (26 shorter events, 0.3 us)
Async XLA Ops:
  6.4 11.4 %collective-permute-start = (bf16[6,8,512]{2,1,0:T(8,128)(2,1)S(1)}, bf16[6,8,512]{2,1,0:T(8,128)(2,1)S(1)}, u32[]{:S(2)}, u32[]{:S(2)}) collective-permute-start(bf16[6,8,512]{2,1,0:T(8,128)(2,1)S(1)} %get-tuple-element.35), channel_id=1, source_target_pairs={{0,14},{2,12},{4,10},{6,8},{8,6},{10,4},{12,2},{14,0},{1,15},{3,13... | collective-permute-start | bytes 147464 | tf_op jit(solution)/shard_map/ppermute | solution.py:413
  12.5 6.1 %collective-permute-start.1 = (bf16[6,8,512]{2,1,0:T(8,128)(2,1)S(1)}, bf16[6,8,512]{2,1,0:T(8,128)(2,1)S(1)}, u32[]{:S(2)}, u32[]{:S(2)}) collective-permute-start(bf16[6,8,512]{2,1,0:T(8,128)(2,1)S(1)} %get-tuple-element.36), channel_id=1, source_target_pairs={{0,12},{2,14},{4,8},{6,10},{8,4},{10,6},{12,0},{14,2},{1,13},{3,15... | collective-permute-start | bytes 147464 | tf_op jit(solution)/shard_map/ppermute | solution.py:413
  12.7 9.8 %collective-permute-start.2 = (bf16[6,8,512]{2,1,0:T(8,128)(2,1)S(1)}, bf16[6,8,512]{2,1,0:T(8,128)(2,1)S(1)}, u32[]{:S(2)}, u32[]{:S(2)}) collective-permute-start(bf16[6,8,512]{2,1,0:T(8,128)(2,1)S(1)} %get-tuple-element.37), channel_id=1, source_target_pairs={{0,10},{2,8},{4,14},{6,12},{8,2},{10,0},{12,6},{14,4},{1,11},{3,9}... | collective-permute-start | bytes 147464 | tf_op jit(solution)/shard_map/ppermute | solution.py:413
  13.4 9.0 %collective-permute-start.3 = (bf16[6,8,512]{2,1,0:T(8,128)(2,1)S(1)}, bf16[6,8,512]{2,1,0:T(8,128)(2,1)S(1)}, u32[]{:S(2)}, u32[]{:S(2)}) collective-permute-start(bf16[6,8,512]{2,1,0:T(8,128)(2,1)S(1)} %get-tuple-element.38), channel_id=1, source_target_pairs={{0,8},{2,10},{4,12},{6,14},{8,0},{10,2},{12,4},{14,6},{1,9},{3,11}... | collective-permute-start | bytes 147464 | tf_op jit(solution)/shard_map/ppermute | solution.py:413
  15.5 7.0 %collective-permute-start.4 = (bf16[6,8,512]{2,1,0:T(8,128)(2,1)S(1)}, bf16[6,8,512]{2,1,0:T(8,128)(2,1)S(1)}, u32[]{:S(2)}, u32[]{:S(2)}) collective-permute-start(bf16[6,8,512]{2,1,0:T(8,128)(2,1)S(1)} %get-tuple-element.39), channel_id=1, source_target_pairs={{0,6},{2,4},{4,2},{6,0},{8,14},{10,12},{12,10},{14,8},{1,7},{3,5},... | collective-permute-start | bytes 147464 | tf_op jit(solution)/shard_map/ppermute | solution.py:413
  17.8 4.7 %collective-permute-start.5 = (bf16[6,8,512]{2,1,0:T(8,128)(2,1)S(1)}, bf16[6,8,512]{2,1,0:T(8,128)(2,1)S(1)}, u32[]{:S(2)}, u32[]{:S(2)}) collective-permute-start(bf16[6,8,512]{2,1,0:T(8,128)(2,1)S(1)} %get-tuple-element.40), channel_id=1, source_target_pairs={{0,4},{2,6},{4,0},{6,2},{8,12},{10,14},{12,8},{14,10},{1,5},{3,7},... | collective-permute-start | bytes 147464 | tf_op jit(solution)/shard_map/ppermute | solution.py:413
  18.5 4.1 %collective-permute-start.6 = (bf16[6,8,512]{2,1,0:T(8,128)(2,1)S(1)}, bf16[6,8,512]{2,1,0:T(8,128)(2,1)S(1)}, u32[]{:S(2)}, u32[]{:S(2)}) collective-permute-start(bf16[6,8,512]{2,1,0:T(8,128)(2,1)S(1)} %get-tuple-element.41), channel_id=1, source_target_pairs={{0,2},{2,0},{4,6},{6,4},{8,10},{10,8},{12,14},{14,12},{1,3},{3,1},... | collective-permute-start | bytes 147464 | tf_op jit(solution)/shard_map/ppermute | solution.py:413
  26.2 1.7 %collective-permute-start.7 = (bf16[96,1792]{1,0:T(8,128)(2,1)S(1)}, bf16[96,1792]{1,0:T(8,128)(2,1)S(1)}, u32[]{:S(2)}, u32[]{:S(2)}) collective-permute-start(bf16[96,1792]{1,0:T(8,128)(2,1)S(1)} %get-tuple-element.46), channel_id=1, source_target_pairs={{0,1},{1,0},{2,3},{3,2},{4,5},{5,4},{6,7},{7,6},{8,9},{9,8},{10,11... | collective-permute-start | bytes 1032200 | tf_op jit(solution)/shard_map/ppermute | solution.py:416
  28.0 11.0 %collective-permute-start.8 = (bf16[24,1792]{1,0:T(8,128)(2,1)S(1)}, bf16[24,1792]{1,0:T(8,128)(2,1)S(1)}, u32[]{:S(2)}, u32[]{:S(2)}) collective-permute-start(bf16[24,1792]{1,0:T(8,128)(2,1)S(1)} %get-tuple-element.48), channel_id=1, source_target_pairs={{1,3},{3,1},{5,7},{7,5},{9,11},{11,9},{13,15},{15,13},{17,19},{19,... | collective-permute-start | bytes 258056 | tf_op jit(solution)/shard_map/ppermute | solution.py:420
  28.7 10.3 %collective-permute-start.9 = (bf16[24,1792]{1,0:T(8,128)(2,1)S(1)}, bf16[24,1792]{1,0:T(8,128)(2,1)S(1)}, u32[]{:S(2)}, u32[]{:S(2)}) collective-permute-start(bf16[24,1792]{1,0:T(8,128)(2,1)S(1)} %get-tuple-element.49), channel_id=1, source_target_pairs={{0,4},{1,7},{2,6},{3,5},{4,0},{5,3},{6,2},{7,1},{8,12},{9,15},{10,... | collective-permute-start | bytes 258056 | tf_op jit(solution)/shard_map/ppermute | solution.py:420
  30.0 9.0 %collective-permute-start.10 = (bf16[24,1792]{1,0:T(8,128)(2,1)S(1)}, bf16[24,1792]{1,0:T(8,128)(2,1)S(1)}, u32[]{:S(2)}, u32[]{:S(2)}) collective-permute-start(bf16[24,1792]{1,0:T(8,128)(2,1)S(1)} %get-tuple-element.50), channel_id=1, source_target_pairs={{0,8},{1,11},{2,10},{3,9},{4,12},{5,15},{6,14},{7,13},{8,0},{9,3},... | collective-permute-start | bytes 258056 | tf_op jit(solution)/shard_map/ppermute | solution.py:420
  32.9 6.3 %collective-permute-start.11 = (bf16[24,1792]{1,0:T(8,128)(2,1)S(1)}, bf16[24,1792]{1,0:T(8,128)(2,1)S(1)}, u32[]{:S(2)}, u32[]{:S(2)}) collective-permute-start(bf16[24,1792]{1,0:T(8,128)(2,1)S(1)} %get-tuple-element.51), channel_id=1, source_target_pairs={{0,12},{1,15},{2,14},{3,13},{4,8},{5,11},{6,10},{7,9},{8,4},{9,7},... | collective-permute-start | bytes 258056 | tf_op jit(solution)/shard_map/ppermute | solution.py:420
  39.2 2.9 %copy-start = (bf16[3,7168]{1,0:T(4,128)(2,1)S(1)}, bf16[3,7168]{1,0:T(4,128)(2,1)}, u32[]{:S(2)}) copy-start(bf16[3,7168]{1,0:T(4,128)(2,1)} %mine_ref.1) | copy-start | bytes 129028
  39.2 4.5 %copy-start.1 = (f32[7168]{0:T(1024)S(1)}, f32[7168]{0:T(1024)}, u32[]{:S(2)}) copy-start(f32[7168]{0:T(1024)} %gain_ref.1) | copy-start | bytes 86020
  39.3 4.5 %collective-permute-start.12 = (f32[24,1792]{1,0:T(8,128)S(1)}, f32[24,1792]{1,0:T(8,128)S(1)}, u32[]{:S(2)}, u32[]{:S(2)}) collective-permute-start(f32[24,1792]{1,0:T(8,128)S(1)} %sum_units.2.mine_ref), channel_id=1, source_target_pairs={{0,1},{1,0},{2,3},{3,2},{4,5},{5,4},{6,7},{7,6},{8,9},{9,8},{10,11... | collective-permute-start | bytes 516104 | tf_op jit(solution)/shard_map/ppermute | solution.py:416
  42.1 1.6 %collective-permute-start.13 = (bf16[3,7168]{1,0:T(4,128)(2,1)S(1)}, bf16[3,7168]{1,0:T(4,128)(2,1)S(1)}, u32[]{:S(2)}, u32[]{:S(2)}) collective-permute-start(bf16[3,7168]{1,0:T(4,128)(2,1)S(1)} %copy-done), channel_id=1, source_target_pairs={{0,1},{1,0},{2,3},{3,2},{4,5},{5,4},{6,7},{7,6},{8,9},{9,8},{10,11... | collective-permute-start | bytes 129032 | tf_op jit(solution)/shard_map/ppermute | solution.py:416
  43.9 36.8 %copy-start.2 = (s32[8]{0:T(128)S(1)}, s32[8]{0:T(128)}, u32[]{:S(2)}) copy-start(s32[8]{0:T(128)} %counts_ref.1) | copy-start | bytes 100
  43.9 7.3 %collective-permute-start.17 = (bf16[24,1792]{1,0:T(8,128)(2,1)S(1)}, bf16[24,1792]{1,0:T(8,128)(2,1)S(1)}, u32[]{:S(2)}, u32[]{:S(2)}) collective-permute-start(bf16[24,1792]{1,0:T(8,128)(2,1)S(1)} %get-tuple-element.56.refs_0_), channel_id=1, source_target_pairs={{0,12},{1,15},{2,14},{3,13},{4,8},{5,11},{6,10},{7,9},{8,4},{9,7},... | collective-permute-start | bytes 258056 | tf_op jit(solution)/shard_map/ppermute | solution.py:420
  47.3 7.6 %collective-permute-start.16 = (bf16[24,1792]{1,0:T(8,128)(2,1)S(1)}, bf16[24,1792]{1,0:T(8,128)(2,1)S(1)}, u32[]{:S(2)}, u32[]{:S(2)}) collective-permute-start(bf16[24,1792]{1,0:T(8,128)(2,1)S(1)} %get-tuple-element.56.refs_0_), channel_id=1, source_target_pairs={{0,8},{1,11},{2,10},{3,9},{4,12},{5,15},{6,14},{7,13},{8,0},{9,3},... | collective-permute-start | bytes 258056 | tf_op jit(solution)/shard_map/ppermute | solution.py:420
  47.3 8.1 %collective-permute-start.15 = (bf16[24,1792]{1,0:T(8,128)(2,1)S(1)}, bf16[24,1792]{1,0:T(8,128)(2,1)S(1)}, u32[]{:S(2)}, u32[]{:S(2)}) collective-permute-start(bf16[24,1792]{1,0:T(8,128)(2,1)S(1)} %get-tuple-element.56.refs_0_), channel_id=1, source_target_pairs={{0,4},{1,7},{2,6},{3,5},{4,0},{5,3},{6,2},{7,1},{8,12},{9,15},{10,... | collective-permute-start | bytes 258056 | tf_op jit(solution)/shard_map/ppermute | solution.py:420
  48.4 7.1 %collective-permute-start.14 = (bf16[24,1792]{1,0:T(8,128)(2,1)S(1)}, bf16[24,1792]{1,0:T(8,128)(2,1)S(1)}, u32[]{:S(2)}, u32[]{:S(2)}) collective-permute-start(bf16[24,1792]{1,0:T(8,128)(2,1)S(1)} %get-tuple-element.56.refs_0_), channel_id=1, source_target_pairs={{1,3},{3,1},{5,7},{7,5},{9,11},{11,9},{13,15},{15,13},{17,19},{19,... | collective-permute-start | bytes 258056 | tf_op jit(solution)/shard_map/ppermute | solution.py:420
  51.3 4.7 %collective-permute-start.21 = (bf16[24,1792]{1,0:T(8,128)(2,1)S(1)}, bf16[24,1792]{1,0:T(8,128)(2,1)S(1)}, u32[]{:S(2)}, u32[]{:S(2)}) collective-permute-start(bf16[24,1792]{1,0:T(8,128)(2,1)S(1)} %collective-permute-done.17.refs_4_), channel_id=1, source_target_pairs={{0,1},{1,0},{2,3},{3,2},{4,5},{5,4},{6,7},{7,6},{8,9},{9,8},{10,11... | collective-permute-start | bytes 258056 | tf_op jit(solution)/shard_map/ppermute | solution.py:416
  54.9 1.5 %collective-permute-start.20 = (bf16[24,1792]{1,0:T(8,128)(2,1)S(1)}, bf16[24,1792]{1,0:T(8,128)(2,1)S(1)}, u32[]{:S(2)}, u32[]{:S(2)}) collective-permute-start(bf16[24,1792]{1,0:T(8,128)(2,1)S(1)} %collective-permute-done.16.refs_3_), channel_id=1, source_target_pairs={{0,1},{1,0},{2,3},{3,2},{4,5},{5,4},{6,7},{7,6},{8,9},{9,8},{10,11... | collective-permute-start | bytes 258056 | tf_op jit(solution)/shard_map/ppermute | solution.py:416
  55.5 1.3 %collective-permute-start.19 = (bf16[24,1792]{1,0:T(8,128)(2,1)S(1)}, bf16[24,1792]{1,0:T(8,128)(2,1)S(1)}, u32[]{:S(2)}, u32[]{:S(2)}) collective-permute-start(bf16[24,1792]{1,0:T(8,128)(2,1)S(1)} %collective-permute-done.15.refs_2_), channel_id=1, source_target_pairs={{0,1},{1,0},{2,3},{3,2},{4,5},{5,4},{6,7},{7,6},{8,9},{9,8},{10,11... | collective-permute-start | bytes 258056 | tf_op jit(solution)/shard_map/ppermute | solution.py:416
  55.5 1.4 %collective-permute-start.18 = (bf16[24,1792]{1,0:T(8,128)(2,1)S(1)}, bf16[24,1792]{1,0:T(8,128)(2,1)S(1)}, u32[]{:S(2)}, u32[]{:S(2)}) collective-permute-start(bf16[24,1792]{1,0:T(8,128)(2,1)S(1)} %collective-permute-done.14.refs_1_), channel_id=1, source_target_pairs={{0,1},{1,0},{2,3},{3,2},{4,5},{5,4},{6,7},{7,6},{8,9},{9,8},{10,11... | collective-permute-start | bytes 258056 | tf_op jit(solution)/shard_map/ppermute | solution.py:416
  64.9 1.7 %collective-permute-start.22 = (bf16[96,1792]{1,0:T(8,128)(2,1)S(1)}, bf16[96,1792]{1,0:T(8,128)(2,1)S(1)}, u32[]{:S(2)}, u32[]{:S(2)}) collective-permute-start(bf16[96,1792]{1,0:T(8,128)(2,1)S(1)} %get-tuple-element.58), channel_id=1, source_target_pairs={{0,1},{1,0},{2,3},{3,2},{4,5},{5,4},{6,7},{7,6},{8,9},{9,8},{10,11... | collective-permute-start | bytes 1032200 | tf_op jit(solution)/shard_map/ppermute | solution.py:416
  66.7 5.1 %collective-permute-start.23 = (bf16[24,1792]{1,0:T(8,128)(2,1)S(1)}, bf16[24,1792]{1,0:T(8,128)(2,1)S(1)}, u32[]{:S(2)}, u32[]{:S(2)}) collective-permute-start(bf16[24,1792]{1,0:T(8,128)(2,1)S(1)} %get-tuple-element.60), channel_id=1, source_target_pairs={{1,3},{3,1},{5,7},{7,5},{9,11},{11,9},{13,15},{15,13},{17,19},{19,... | collective-permute-start | bytes 258056 | tf_op jit(solution)/shard_map/ppermute | solution.py:420
  67.4 4.6 %collective-permute-start.24 = (bf16[24,1792]{1,0:T(8,128)(2,1)S(1)}, bf16[24,1792]{1,0:T(8,128)(2,1)S(1)}, u32[]{:S(2)}, u32[]{:S(2)}) collective-permute-start(bf16[24,1792]{1,0:T(8,128)(2,1)S(1)} %get-tuple-element.61), channel_id=1, source_target_pairs={{0,4},{1,7},{2,6},{3,5},{4,0},{5,3},{6,2},{7,1},{8,12},{9,15},{10,... | collective-permute-start | bytes 258056 | tf_op jit(solution)/shard_map/ppermute | solution.py:420
  68.1 5.5 %collective-permute-start.25 = (bf16[24,1792]{1,0:T(8,128)(2,1)S(1)}, bf16[24,1792]{1,0:T(8,128)(2,1)S(1)}, u32[]{:S(2)}, u32[]{:S(2)}) collective-permute-start(bf16[24,1792]{1,0:T(8,128)(2,1)S(1)} %get-tuple-element.62), channel_id=1, source_target_pairs={{0,8},{1,11},{2,10},{3,9},{4,12},{5,15},{6,14},{7,13},{8,0},{9,3},... | collective-permute-start | bytes 258056 | tf_op jit(solution)/shard_map/ppermute | solution.py:420
  70.8 6.3 %collective-permute-start.26 = (bf16[24,1792]{1,0:T(8,128)(2,1)S(1)}, bf16[24,1792]{1,0:T(8,128)(2,1)S(1)}, u32[]{:S(2)}, u32[]{:S(2)}) collective-permute-start(bf16[24,1792]{1,0:T(8,128)(2,1)S(1)} %get-tuple-element.63), channel_id=1, source_target_pairs={{0,12},{1,15},{2,14},{3,13},{4,8},{5,11},{6,10},{7,9},{8,4},{9,7},... | collective-permute-start | bytes 258056 | tf_op jit(solution)/shard_map/ppermute | solution.py:420
  77.1 3.6 %collective-permute-start.27 = (f32[24,1792]{1,0:T(8,128)S(1)}, f32[24,1792]{1,0:T(8,128)S(1)}, u32[]{:S(2)}, u32[]{:S(2)}) collective-permute-start(f32[24,1792]{1,0:T(8,128)S(1)} %sum_units.3.mine_ref), channel_id=1, source_target_pairs={{0,1},{1,0},{2,3},{3,2},{4,5},{5,4},{6,7},{7,6},{8,9},{9,8},{10,11... | collective-permute-start | bytes 516104 | tf_op jit(solution)/shard_map/ppermute | solution.py:416

commit v3 on v2

v3 whole, which is shorter than its diff:
```python
import functools

import jax
import jax.numpy as jnp
from jax import lax
from jax.experimental import pallas as pl
from jax.experimental.pallas import tpu as pltpu
from jax.sharding import PartitionSpec as P

LATENT_WIDTH = 512
PIECES = 8
PARTS = 4

score_scale = 0.07216878364870322
norm_epsilon = 1e-06
masked_score = -1e30
f32 = jnp.float32
bf16 = jnp.bfloat16
VMEM = pltpu.VMEM
MIB = 1 << 20


def in_hbm(arrays):
    return [pltpu.with_memory_space_constraint(x, pltpu.HBM) for x in arrays]


def vmem(n):
    return [pl.BlockSpec(memory_space=VMEM)] * n


def params(mib):
    return pltpu.CompilerParams(vmem_limit_bytes=mib * MIB)


def piece_count(rows, most):
    return next(p for p in range(most, 0, -1) if p == 1 or rows % (8 * p) == 0)


def piece_copies(source, target, sems):
    count = sems.shape[0]
    if len(source.shape) == 2:
        count = piece_count(source.shape[0], count)
    step = source.shape[0] // count
    copies = []
    for p in range(count):
        at = pl.ds(p * step, step)
        here = source.at[at]
        if target.shape != source.shape:
            here = source.at[at, pl.ds(0, target.shape[1])]
        copies.append(pltpu.make_async_copy(here, target.at[at], sems.at[p]))
    return copies


def load_kernel(_, source, target, sems):
    copies = piece_copies(source, target, sems)
    for copy in copies:
        copy.start()
    for copy in copies:
        copy.wait()


def load(after, weight):
    return pl.pallas_call(
        load_kernel,
        out_shape=jax.ShapeDtypeStruct(weight.shape, weight.dtype),
        in_specs=[pl.BlockSpec(memory_space=pl.ANY)] * 2,
        out_specs=vmem(1)[0],
        scratch_shapes=[pltpu.SemaphoreType.DMA((PIECES,))],
        compiler_params=params(2),
        cost_estimate=pl.CostEstimate(flops=0, bytes_accessed=4 * weight.size, transcendentals=0),
        name="load",
    )(after, *in_hbm([weight]))


def row_ids(rows, columns, slots):
    i = lax.broadcasted_iota(jnp.int32, (rows, columns), 0).astype(f32)
    unit = float(slots * PARTS)
    block = jnp.floor((i + 0.5) / unit)
    inner = i - block * unit
    part = jnp.floor((inner + 0.5) / slots)
    return part, block * slots + (inner - part * slots)


def attention_kernel(n_dp, counts_hbm, lengths_hbm, q_hbm, cache_hbm, residual_hbm, gain_hbm, *refs):
    n_weights = 2
    weights, outs = refs[:n_weights], refs[n_weights : n_weights + n_dp]
    residual_unit, gain_unit, to_heads, to_units, to_parts = refs[n_weights + n_dp : n_weights + n_dp + 5]
    loaded = refs[n_weights + n_dp + 5 : 2 * n_weights + n_dp + 5]
    counts_ref, lengths_ref, q_ref, cache_ref, residual_ref, gain_ref, held, sems, weight_sems = refs[
        2 * n_weights + n_dp + 5 :
    ]
    slots = q_ref.shape[0]
    pairs = [
        (counts_hbm, counts_ref),
        (lengths_hbm, lengths_ref),
        (q_hbm, q_ref),
        (cache_hbm, cache_ref),
        (residual_hbm, residual_ref),
        (gain_hbm, gain_ref),
    ]
    copies = [pltpu.make_async_copy(src, dst, sems.at[n]) for n, (src, dst) in enumerate(pairs)]
    fetches = []
    for n in range(n_weights):
        fetches += piece_copies(weights[n], loaded[n], weight_sems.at[n])
    for copy in copies + fetches:
        copy.start()
    me, me_head = lax.axis_index("dp"), lax.axis_index("head")
    for copy in copies:
        copy.wait()
    rows = range(slots)
    scores = []
    for row in rows:
        score = lax.dot_general(q_ref[row], cache_ref[row], (((1,), (1,)), ((), ())), preferred_element_type=f32)
        position = lax.broadcasted_iota(jnp.int32, score.shape, 1)
        scores.append(jnp.where(position < lengths_ref[row], score * score_scale, masked_score))
    probs = [jnp.exp(x - jnp.max(x, axis=-1, keepdims=True)) for x in scores]
    for row in rows:
        weighted = jnp.dot(probs[row].astype(bf16), cache_ref[row, :, :LATENT_WIDTH], preferred_element_type=f32)
        denominator = jnp.sum(probs[row], axis=-1, keepdims=True)
        latent = jnp.where(row < counts_ref[me], weighted / denominator, 0.0).astype(bf16)
        held[row] = latent.reshape(held.shape[1:])
    for k in range(n_dp):
        for row in rows:
            outs[k][row] = held[row, me ^ k]
    to_heads[...] = regroup(to_heads.shape[0], held.shape[2], n_dp * slots)
    to_units[...] = regroup(to_units.shape[0], n_dp // 2, PARTS)
    to_parts[...] = regroup(to_parts.shape[0], PARTS, n_dp)
    owner_rows = residual_ref.shape[0]
    part = residual_unit.shape[1]
    gain = gain_ref[...].reshape(1, PARTS * part)
    residual_unit[...] = jnp.zeros_like(residual_unit)
    for q in range(PARTS):
        at = pl.ds(q * part, part)
        mine = residual_ref[:, at].astype(f32)
        for r in range(owner_rows):
            residual_unit[pl.ds(q * slots + me_head * owner_rows + r, 1), :] = mine[r : r + 1]
        gain_unit[pl.ds(q * slots, slots), :] = jnp.broadcast_to(gain[:, q * part : (q + 1) * part], (slots, part))
    for copy in fetches:
        copy.wait()


def attend(n_dp, counts, lengths, queries, cache, residual, gain, value_up, proj):
    slots, heads, _ = queries.shape
    per_rank = heads // n_dp
    part = gain.shape[0] // PARTS
    block = jax.ShapeDtypeStruct((slots, per_rank, LATENT_WIDTH), bf16)
    unit = jax.ShapeDtypeStruct((slots * PARTS, part), f32)
    rows = n_dp * slots
    moves = [jax.ShapeDtypeStruct((n, n), bf16) for n in (rows * per_rank, rows * PARTS // 2, rows * PARTS)]
    loaded = [
        jax.ShapeDtypeStruct(value_up.shape, bf16),
        jax.ShapeDtypeStruct((proj.shape[0], part * (PARTS - 1)), bf16),
    ]
    return pl.pallas_call(
        functools.partial(attention_kernel, n_dp),
        out_shape=[block] * n_dp + [unit] * 2 + moves + loaded,
        in_specs=[pl.BlockSpec(memory_space=pl.ANY)] * 8,
        out_specs=vmem(n_dp + 7),
        scratch_shapes=[
            pltpu.SMEM(counts.shape, jnp.int32),
            pltpu.SMEM(lengths.shape, jnp.int32),
            VMEM(queries.shape, bf16),
            VMEM(cache.shape, bf16),
            VMEM(residual.shape, bf16),
            VMEM(gain.shape, f32),
            VMEM((slots, n_dp, per_rank, LATENT_WIDTH), bf16),
            pltpu.SemaphoreType.DMA((6,)),
            pltpu.SemaphoreType.DMA((2, 2)),
        ],
        compiler_params=params(10),
        name="attend",
    )(*in_hbm([counts, lengths, queries, cache, residual, gain, value_up, proj]))


def write_parts(x, weight_part, keep_ref, give_ref):
    half = x.shape[0] // 2
    for q in range(PARTS):
        product = jnp.dot(x, weight_part(q), preferred_element_type=f32)
        at = pl.ds(q * half, half)
        keep_ref[at, :] = product[:half]
        give_ref[at, :] = product[half:].astype(bf16)


def regroup(rows, inner, outer):
    slots = rows // (inner * outer)
    i = lax.broadcasted_iota(jnp.int32, (rows, rows), 0).astype(f32)
    j = lax.broadcasted_iota(jnp.int32, (rows, rows), 1).astype(f32)
    b = jnp.floor((i + 0.5) / (outer * slots))
    rest = i - b * (outer * slots)
    a = jnp.floor((rest + 0.5) / slots)
    return (a * (inner * slots) + b * slots + (rest - a * slots) == j).astype(bf16)


def move_rows(matrix, x):
    return jnp.dot(matrix, x, preferred_element_type=f32).astype(bf16)


def block_order(n_dp):
    far = list(range(n_dp // 2, n_dp))
    return [*far[::-1][1::2], *far[::-1][::2], *reversed(range(n_dp // 2))]


def set_order(half):
    return [*range(half // 2, half), *reversed(range(half // 2))]


def project_kernel(n_dp, slots, *refs):
    blocks = refs[:n_dp]
    up_ref, weight_ref, move_ref, weight_hbm, _, keep_ref, give_ref, last_ref, rows_ref, values_ref, sems = refs[n_dp:]
    per_rank = up_ref.shape[0]
    rows = n_dp * slots
    width = last_ref.shape[1]
    copies = piece_copies(weight_hbm.at[:, pl.ds((PARTS - 1) * width, width)], last_ref, sems)
    for copy in copies:
        copy.start()
    me_head = lax.axis_index("head")
    size = slots * per_rank
    for n, k in enumerate(block_order(n_dp)):
        place = ((k & 1) ^ me_head) * (n_dp // 2) + (k >> 1)
        x = blocks[n][...].reshape(size, -1)
        if size % 8 == 0:
            rows_ref[pl.ds(pl.multiple_of(place * size, 8), size), :] = x
        else:
            x = x.astype(f32)
            for c in range(rows_ref.shape[0]):
                rows_ref[c, pl.ds(pl.multiple_of(place * size, 4), size), :] = x[:, c * 128 : (c + 1) * 128]
    if size % 8 == 0:
        gathered = rows_ref[...]
    else:
        gathered = jnp.concatenate([rows_ref[c] for c in range(rows_ref.shape[0])], axis=1).astype(bf16)
    by_head = move_rows(move_ref[...], gathered)
    for j in range(per_rank):
        v = jnp.dot(by_head[j * rows : (j + 1) * rows], up_ref[j], preferred_element_type=f32).astype(bf16)
        values_ref[:, pl.ds(j * v.shape[1], v.shape[1])] = v

    def weight_part(q):
        if q < PARTS - 1:
            return weight_ref[:, pl.ds(q * width, width)]
        for copy in copies:
            copy.wait()
        return last_ref[...]

    write_parts(values_ref[...], weight_part, keep_ref, give_ref)


def unit_mib(rows, part):
    return -(-8 * rows * PARTS * part * 4 // MIB)


def project(n_dp, blocks, value_up, most, move, weight, after):
    slots, per_rank, _ = blocks[0].shape
    depth, width = weight.shape
    rows = n_dp * slots
    part = width // PARTS
    own = rows * PARTS // 2
    out = lambda dtype: jax.ShapeDtypeStruct((own, part), dtype)
    gathered = VMEM((rows * per_rank, LATENT_WIDTH), bf16)
    if slots * per_rank % 8:
        gathered = VMEM((LATENT_WIDTH // 128, rows * per_rank, 128), f32)
    return pl.pallas_call(
        functools.partial(project_kernel, n_dp, slots),
        out_shape=[out(f32), out(bf16)],
        in_specs=vmem(n_dp + 3) + [pl.BlockSpec(memory_space=pl.ANY)] * 2,
        out_specs=vmem(2),
        scratch_shapes=[
            VMEM((depth, part), bf16),
            gathered,
            VMEM((rows, depth), bf16),
            pltpu.SemaphoreType.DMA((PIECES,)),
        ],
        compiler_params=params(unit_mib(rows, part) + 4),
        name="project",
    )(*blocks, value_up, most, move, *in_hbm([weight]), after)


def add_kernel(n_units, keep_ref, got_ref, move_ref, *outs):
    total = (keep_ref[...] + got_ref[...].astype(f32)).astype(bf16)
    units = move_rows(move_ref[...], total)
    size = units.shape[0] // n_units
    for s in range(n_units):
        outs[s][...] = units[s * size : (s + 1) * size]


def add_halves(n_units, keep, got, move):
    unit = keep.shape[0] // n_units
    return pl.pallas_call(
        functools.partial(add_kernel, n_units),
        out_shape=[jax.ShapeDtypeStruct((unit, keep.shape[1]), bf16)] * n_units,
        in_specs=vmem(3),
        out_specs=vmem(n_units),
        compiler_params=params(unit_mib(keep.shape[0] // PARTS, keep.shape[1])),
        name="add_halves",
    )(keep, got, move)


def sum_kernel(n_units, own_ref, base_ref, *refs):
    got, out_ref = refs[:n_units], refs[-1]
    me_head = lax.axis_index("head")
    zeroth = set_order(n_units).index(0)
    total = base_ref[...] + jnp.where(me_head == 0, own_ref[...], got[zeroth][...]).astype(f32)
    for ref in got[:zeroth] + got[zeroth + 1 :]:
        total = total + ref[...].astype(f32)
    out_ref[...] = total


def sum_units(own, base, got, after):
    return pl.pallas_call(
        functools.partial(sum_kernel, len(got)),
        out_shape=jax.ShapeDtypeStruct(own.shape, f32),
        in_specs=vmem(2 + len(got)) + [pl.BlockSpec(memory_space=pl.ANY)] * len(after),
        out_specs=vmem(1)[0],
        compiler_params=params(4),
        name="sum_units",
    )(own, base, *got, *after)


def norm_kernel(slots, width, mine_ref, twin_ref, gain_ref, state_ref, normed_ref):
    state = mine_ref[...] + twin_ref[...]
    square = jnp.sum(state * state, axis=1, keepdims=True)
    rows = state.shape[0]
    _, slot = row_ids(rows, 1, slots)
    first = (lax.axis_index("head") * (slots // 2)).astype(f32)
    owned = (slot >= first) & (slot < first + slots // 2)
    state_ref[...] = jnp.where(owned, state, 0.0)
    mean = jnp.zeros_like(square)
    for r in range(slots):
        total = jnp.sum(jnp.where(slot == r, square, 0.0), axis=0, keepdims=True)
        mean = jnp.where(slot == r, total, mean)
    scaled = state * lax.rsqrt(mean * (1.0 / width) + norm_epsilon)
    normed_ref[...] = (scaled * gain_ref[...]).astype(bf16)


def norm_rows(slots, mine, twin, gain):
    shape = mine.shape
    return pl.pallas_call(
        functools.partial(norm_kernel, slots, shape[1] * PARTS),
        out_shape=[jax.ShapeDtypeStruct(shape, f32), jax.ShapeDtypeStruct(shape, bf16)],
        in_specs=vmem(3),
        out_specs=vmem(2),
        compiler_params=params(4),
        name="norm_rows",
    )(mine, twin, gain)


def ffn_kernel(n_dp, slots, *refs):
    half = n_dp // 2
    normed_ref = refs[0]
    own, other = refs[1 : 1 + half], refs[1 + half : 1 + n_dp]
    gate_ref, up_ref, down_ref, move_ref, keep_ref, give_ref, units_ref, rows_ref = refs[1 + n_dp :]
    rows = n_dp * slots
    unit, part = normed_ref.shape
    me_head = lax.axis_index("head")
    for s in range(half):
        mine, twins = own[s][...], other[s][...]
        if s == 0:
            mine = jnp.where(me_head == 0, normed_ref[...], mine)
            twins = jnp.where(me_head == 0, twins, normed_ref[...])
        units_ref[pl.ds(s * unit, unit), :] = mine
        units_ref[pl.ds((half + s) * unit, unit), :] = twins
    moved = move_rows(move_ref[...], units_ref[...])
    for q in range(PARTS):
        rows_ref[:, pl.ds(q * part, part)] = moved[q * rows : (q + 1) * rows]
    x = rows_ref[...]
    contract = (((1,), (1,)), ((), ()))
    gate = lax.dot_general(x, gate_ref[...], contract, preferred_element_type=f32)
    up = lax.dot_general(x, up_ref[...], contract, preferred_element_type=f32)
    hidden = (gate / (1.0 + jnp.exp(-gate)) * up).astype(bf16)
    write_parts(hidden, lambda q: down_ref[:, pl.ds(q * part, part)], keep_ref, give_ref)


def feed_forward(n_dp, slots, normed, own, other, gate_t, up_t, down, move):
    _, part = normed.shape
    rows = n_dp * slots
    out = lambda dtype: jax.ShapeDtypeStruct((rows * PARTS // 2, part), dtype)
    return pl.pallas_call(
        functools.partial(ffn_kernel, n_dp, slots),
        out_shape=[out(f32), out(bf16)],
        in_specs=vmem(1 + n_dp + 4),
        out_specs=vmem(2),
        scratch_shapes=[VMEM((rows * PARTS, part), bf16), VMEM((rows, PARTS * part), bf16)],
        compiler_params=params(unit_mib(rows, part)),
        name="feed_forward",
    )(normed, *own, *other, gate_t, up_t, down, move)


def final_kernel(slots, owner_rows, counts_ref, mine_ref, twin_ref, out_ref):
    me, me_head = lax.axis_index("dp"), lax.axis_index("head")
    total = mine_ref[...] + twin_ref[...]
    rows = total.shape[0]
    _, slot = row_ids(rows, 1, slots)
    total = jnp.where(slot < counts_ref[me].astype(f32), total, 0.0).astype(bf16)
    part = total.shape[1]
    padded = 8
    i = lax.broadcasted_iota(jnp.int32, (padded, rows), 0)
    j = lax.broadcasted_iota(jnp.int32, (padded, rows), 1)
    for q in range(PARTS):
        pick = (j == q * slots + me_head * owner_rows + i).astype(bf16)
        chosen = jnp.dot(pick, total, preferred_element_type=f32)
        out_ref[:, pl.ds(q * part, part)] = chosen[:owner_rows].astype(bf16)


def final_rows(slots, owner_rows, counts, mine, twin):
    return pl.pallas_call(
        functools.partial(final_kernel, slots, owner_rows),
        out_shape=jax.ShapeDtypeStruct((owner_rows, mine.shape[1] * PARTS), bf16),
        in_specs=[pl.BlockSpec(memory_space=pltpu.SMEM)] + vmem(2),
        out_specs=vmem(1)[0],
        compiler_params=params(4),
        name="final_rows",
    )(counts, mine, twin)


def on_device(n_dp, queries, latent_key_cache, lengths, counts, residual, value_up_weight,
              output_proj, norm_gain, gate_weight, up_weight, down_weight):
    slots = queries.shape[0]
    owner_rows = residual.shape[0]
    half = n_dp // 2

    def to_peer(x, k):
        return lax.ppermute(x, "dp", [(i, i ^ k) for i in range(n_dp)])

    def to_twin(x):
        return lax.ppermute(x, "head", [(0, 1), (1, 0)])

    def to_set(x, s):
        pairs = [(2 * i + h, 2 * (i ^ (2 * s + h)) + h) for i in range(n_dp) for h in range(2) if 2 * s + h]
        return lax.ppermute(x, ("dp", "head"), pairs)

    outs = attend(
        n_dp, counts, lengths, queries, latent_key_cache, residual, norm_gain, value_up_weight[0], output_proj[0]
    )
    blocks, (residual_unit, gain_unit, to_heads, to_units, to_parts, value_up, most) = outs[:n_dp], outs[n_dp:]
    def reduce_units(keep, give, base, weights):
        units = add_halves(half, keep, to_twin(give), to_units)
        weights = [load(units[0], w) for w in weights]
        got = [to_set(units[s], s) for s in set_order(half)]
        mine = sum_units(units[0], base, got, weights)
        return mine, to_twin(mine), weights

    gate = load(blocks[0], gate_weight.T)
    blocks = [to_peer(blocks[k], k) if k else blocks[0] for k in block_order(n_dp)]
    keep, give = project(n_dp, blocks, value_up, most, to_heads, output_proj[0], gate)
    mine, twin, (up,) = reduce_units(keep, give, residual_unit, [up_weight.T])
    state, normed = norm_rows(slots, mine, twin, gain_unit)
    down = load(normed, down_weight)
    own = {s: to_set(normed, s) for s in reversed(set_order(half))}
    tied = set_order(half)[1]
    own[tied], down = lax.optimization_barrier((own[tied], down))
    other = {s: to_twin(own[s]) for s in set_order(half)}
    own, other = [own[s] for s in range(half)], [other[s] for s in range(half)]
    keep, give = feed_forward(n_dp, slots, normed, own, other, gate, up, down, to_parts)
    mine, twin, _ = reduce_units(keep, give, state, [])
    return final_rows(slots, owner_rows, counts, mine, twin)


def solution(mesh):
    n_dp = mesh.shape["dp"]
    in_specs = (
        P(("groups", "dp"), "head", None),
        P(("groups", "dp"), None, None),
        P(("groups", "dp")),
        P("groups"),
        P(("groups", "dp", "head"), None),
        P("head", "dp", None, None),
        P("head", "dp", None),
        P(),
        P(None, ("dp", "head")),
        P(None, ("dp", "head")),
        P(("dp", "head"), None),
    )
    out_specs = P(("groups", "dp", "head"), None)

    def step(*args):
        return on_device(n_dp, *args)

    return jax.shard_map(step, mesh=mesh, in_specs=in_specs, out_specs=out_specs, check_vma=False)
```

time: 82.3 us -> 76.3 us (0.927)
  starting transfers between devices: 36.6 us -> 29.6 us
  waiting for transfers between devices: 16.2 us -> 18.7 us
  Pallas kernels: 29.1 us -> 27.6 us
    ppermute x9 -> x8, starting transfers between devices: 8.49 us -> 2.62 us  [to_twin(): return lax.ppermute(x, 'head', [(0, 1), (1, 0)])]
    ppermute x12, waiting for transfers between devices: 10.2 us -> 12.7 us  [to_set(): return lax.ppermute(x, ('dp', 'head'), pairs)]
    pallas_call x1, Pallas kernels: 7.97 us -> 6.52 us  [feed_forward(): pl.pallas_call(functools.partial(ffn_kernel, n_dp, slots), out_shape=[out...]
    ppermute x12, starting transfers between devices: 15.5 us -> 14.1 us  [to_set(): return lax.ppermute(x, ('dp', 'head'), pairs)]
    pallas_call x5, Pallas kernels: 9.52 us -> 10.8 us  [the longest x3 10.3 us: load(): pl.pallas_call(load_kernel, out_shape=jax.ShapeDtypeStruct(weight.shape,...]
    pallas_call x1, Pallas kernels: 6.38 us -> 5.18 us  [attend(): pl.pallas_call(functools.partial(attention_kernel, n_dp), out_shape=[bloc...]
    ppermute x9 -> x8, waiting for transfers between devices: 5.8 us -> 5.96 us  [to_twin(): return lax.ppermute(x, 'head', [(0, 1), (1, 0)])]
  transfers between devices with their start and end apart: 28 -> 27, of which waited for: 14 -> 13; matrix products, arithmetic and copies ran while one was open for 0% -> 0% of each run, Pallas kernels for 11% -> 14%
where the time goes in v3:
time: 76.3 us; the launch traced here: 76.1 us
  starting transfers between devices  29.6 us (39%)
  Pallas kernels  27.6 us (36%)
  waiting for transfers between devices  18.7 us (25%)
    ppermute x12, starting transfers between devices, to_set(): return lax.ppermute(x, ('dp', 'head'), pairs)  14.1 us
    ppermute x7, starting transfers between devices, to_peer(): return lax.ppermute(x, 'dp', [(i, i ^ k) for i in range(n_dp)])  12.9 us
    ppermute x12, waiting for transfers between devices, to_set(): return lax.ppermute(x, ('dp', 'head'), pairs)  12.7 us
    pallas_call x3, Pallas kernels, load(): pl.pallas_call(load_kernel, out_shape=jax.ShapeDtypeStruct(weight.shape,...  10.3 us
    pallas_call x1, Pallas kernels, feed_forward(): pl.pallas_call(functools.partial(ffn_kernel, n_dp, slots), out_shape=[out...  6.52 us
    ppermute x8, waiting for transfers between devices, to_twin(): return lax.ppermute(x, 'head', [(0, 1), (1, 0)])  5.96 us
    pallas_call x1, Pallas kernels, attend(): pl.pallas_call(functools.partial(attention_kernel, n_dp), out_shape=[bloc...  5.18 us
    pallas_call x1, Pallas kernels, project(): pl.pallas_call(functools.partial(project_kernel, n_dp, slots), out_shape=...  3.43 us
  transfers between devices with their start and end apart: 27, of which 13 were waited for; matrix products, arithmetic and copies ran while one was open for 0% of the time, Pallas kernels for 14%

profile of v3, /device:TPU:0, one launch (start us, length us, event | category | flops | bytes accessed | tf_op | source)
XLA Modules:
  0.0 76.1 jit_solution(15805526268091215710)
XLA Ops:
  0.0 5.2 %attend.1 = (bf16[6,8,512]{2,1,0:T(8,128)(2,1)S(1)}, bf16[6,8,512]{2,1,0:T(8,128)(2,1)S(1)}, bf16[6,8,512]{2,1,0:T(8,128)(2,1)S(1)}, bf16[6,8,512]{2,1,0:T(8,128...) custom-call(s32[8]{0:T(128)} %counts_ref.1, ...), custom_call_target="tpu_custom_call" | custom-call | tf_op jit(solution)/shard_map/attend/pallas_call | solution.py:154
  5.2 5.1 %collective-permute-start = (bf16[6,8,512]{2,1,0:T(8,128)(2,1)S(1)}, bf16[6,8,512]{2,1,0:T(8,128)(2,1)S(1)}, u32[]{:S(2)}, u32[]{:S(2)}) collective-permute-start(bf16[6,8,512]{2,1,0:T(8,128)(2,1)S(1)} %get-tuple-element.36), channel_id=1, source_target_pairs={{0,12},{2,14},{4,8},{6,10},{8,4},{10,6},{12,0},{14,2},{1,13},{3,15... | collective-permute-start | bytes 147464 | tf_op jit(solution)/shard_map/ppermute | solution.py:420
  10.3 2.9 %collective-permute-start.2 = (bf16[6,8,512]{2,1,0:T(8,128)(2,1)S(1)}, bf16[6,8,512]{2,1,0:T(8,128)(2,1)S(1)}, u32[]{:S(2)}, u32[]{:S(2)}) collective-permute-start(bf16[6,8,512]{2,1,0:T(8,128)(2,1)S(1)} %get-tuple-element.38), channel_id=1, source_target_pairs={{0,14},{2,12},{4,10},{6,8},{8,6},{10,4},{12,2},{14,0},{1,15},{3,13... | collective-permute-start | bytes 147464 | tf_op jit(solution)/shard_map/ppermute | solution.py:420
  13.2 1.0 %collective-permute-start.3 = (bf16[6,8,512]{2,1,0:T(8,128)(2,1)S(1)}, bf16[6,8,512]{2,1,0:T(8,128)(2,1)S(1)}, u32[]{:S(2)}, u32[]{:S(2)}) collective-permute-start(bf16[6,8,512]{2,1,0:T(8,128)(2,1)S(1)} %get-tuple-element.39), channel_id=1, source_target_pairs={{0,10},{2,8},{4,14},{6,12},{8,2},{10,0},{12,6},{14,4},{1,11},{3,9}... | collective-permute-start | bytes 147464 | tf_op jit(solution)/shard_map/ppermute | solution.py:420
  14.2 2.4 %collective-permute-start.4 = (bf16[6,8,512]{2,1,0:T(8,128)(2,1)S(1)}, bf16[6,8,512]{2,1,0:T(8,128)(2,1)S(1)}, u32[]{:S(2)}, u32[]{:S(2)}) collective-permute-start(bf16[6,8,512]{2,1,0:T(8,128)(2,1)S(1)} %get-tuple-element.40), channel_id=1, source_target_pairs={{0,6},{2,4},{4,2},{6,0},{8,14},{10,12},{12,10},{14,8},{1,7},{3,5},... | collective-permute-start | bytes 147464 | tf_op jit(solution)/shard_map/ppermute | solution.py:420
  16.6 1.5 %collective-permute-start.6 = (bf16[6,8,512]{2,1,0:T(8,128)(2,1)S(1)}, bf16[6,8,512]{2,1,0:T(8,128)(2,1)S(1)}, u32[]{:S(2)}, u32[]{:S(2)}) collective-permute-start(bf16[6,8,512]{2,1,0:T(8,128)(2,1)S(1)} %get-tuple-element.42), channel_id=1, source_target_pairs={{0,2},{2,0},{4,6},{6,4},{8,10},{10,8},{12,14},{14,12},{1,3},{3,1},... | collective-permute-start | bytes 147464 | tf_op jit(solution)/shard_map/ppermute | solution.py:420
  18.1 3.4 %load.3.refs_12_.refs_9_ = bf16[576,7168]{1,0:T(8,128)(2,1)S(1)} custom-call(bf16[6,8,512]{2,1,0:T(8,128)(2,1)S(1)} %get-tuple-element.43._.refs_7_, bf16[576,7168]{1,0:T(8,128)(2,1)} %bitcast.6), custom_call_target="tpu_custom_call" | custom-call | bytes 16515072 | tf_op jit(solution)/shard_map/load/pallas_call | solution.py:63
  21.6 3.4 %project.1 = (f32[96,1792]{1,0:T(8,128)S(1)}, bf16[96,1792]{1,0:T(8,128)(2,1)S(1)}) custom-call(bf16[6,8,512]{2,1,0:T(8,128)(2,1)S(1)} %collective-permute-done.refs_0_, bf16[6,8,512]{2,1,0:T(8,128)(2,1)S(1)} %collective-permute-done.1.refs_1_, bf16[6,8,512]{2,1,0:T(8,128)(2,1)S(1)} %collective-permute-done.2.refs_2_, ...), custom_call_target="tpu_custom_call" | custom-call | tf_op jit(solution)/shard_map/project/pallas_call | solution.py:260
  25.0 0.1 collective-permute-start.7
  25.1 1.6 %collective-permute-done.7.got_ref = bf16[96,1792]{1,0:T(8,128)(2,1)S(1)} collective-permute-done((bf16[96,1792]{1,0:T(8,128)(2,1)S(1)}, bf16[96,1792]{1,0:T(8,128)(2,1)S(1)}, u32[]{:S(2)}, u32[]{:S(2)}) %collective-permute-start.7) | collective-permute-done | bytes 344096 | tf_op jit(solution)/shard_map/ppermute | solution.py:423
  26.7 0.2 add_halves.2
  27.0 1.6 %collective-permute-start.8 = (bf16[24,1792]{1,0:T(8,128)(2,1)S(1)}, bf16[24,1792]{1,0:T(8,128)(2,1)S(1)}, u32[]{:S(2)}, u32[]{:S(2)}) collective-permute-start(bf16[24,1792]{1,0:T(8,128)(2,1)S(1)} %get-tuple-element.52), channel_id=1, source_target_pairs={{0,8},{1,11},{2,10},{3,9},{4,12},{5,15},{6,14},{7,13},{8,0},{9,3},... | collective-permute-start | bytes 258056 | tf_op jit(solution)/shard_map/ppermute | solution.py:427
  28.6 2.0 %collective-permute-start.9 = (bf16[24,1792]{1,0:T(8,128)(2,1)S(1)}, bf16[24,1792]{1,0:T(8,128)(2,1)S(1)}, u32[]{:S(2)}, u32[]{:S(2)}) collective-permute-start(bf16[24,1792]{1,0:T(8,128)(2,1)S(1)} %get-tuple-element.53), channel_id=1, source_target_pairs={{0,12},{1,15},{2,14},{3,13},{4,8},{5,11},{6,10},{7,9},{8,4},{9,7},... | collective-permute-start | bytes 258056 | tf_op jit(solution)/shard_map/ppermute | solution.py:427
  30.7 0.5 collective-permute-start.10
  31.1 0.7 collective-permute-start.11
  31.8 3.4 %load.4.refs_4_.refs_10_ = bf16[576,7168]{1,0:T(8,128)(2,1)S(1)} custom-call(bf16[24,1792]{1,0:T(8,128)(2,1)S(1)} %get-tuple-element.50._.own_ref, bf16[576,7168]{1,0:T(8,128)(2,1)} %bitcast.7), custom_call_target="tpu_custom_call" | custom-call | bytes 16515072 | tf_op jit(solution)/shard_map/load/pallas_call | solution.py:63
  35.2 1.3 %collective-permute-done.8.refs_0_ = bf16[24,1792]{1,0:T(8,128)(2,1)S(1)} collective-permute-done((bf16[24,1792]{1,0:T(8,128)(2,1)S(1)}, bf16[24,1792]{1,0:T(8,128)(2,1)S(1)}, u32[]{:S(2)}, u32[]{:S(2)}) %collective-permute-start.8) | collective-permute-done | bytes 86048 | tf_op jit(solution)/shard_map/ppermute | solution.py:427
  36.5 1.5 %collective-permute-done.10.refs_2_ = bf16[24,1792]{1,0:T(8,128)(2,1)S(1)} collective-permute-done((bf16[24,1792]{1,0:T(8,128)(2,1)S(1)}, bf16[24,1792]{1,0:T(8,128)(2,1)S(1)}, u32[]{:S(2)}, u32[]{:S(2)}) %collective-permute-start.10) | collective-permute-done | bytes 86048 | tf_op jit(solution)/shard_map/ppermute | solution.py:427
  38.1 0.7 collective-permute-start.12
  38.8 1.0 %collective-permute-done.12.twin_ref = f32[24,1792]{1,0:T(8,128)S(1)} collective-permute-done((f32[24,1792]{1,0:T(8,128)S(1)}, f32[24,1792]{1,0:T(8,128)S(1)}, u32[]{:S(2)}, u32[]{:S(2)}) %collective-permute-start.12) | collective-permute-done | bytes 172064 | tf_op jit(solution)/shard_map/ppermute | solution.py:423
  39.8 0.1 norm_rows.1
  40.0 3.1 %collective-permute-start.16 = (bf16[24,1792]{1,0:T(8,128)(2,1)S(1)}, bf16[24,1792]{1,0:T(8,128)(2,1)S(1)}, u32[]{:S(2)}, u32[]{:S(2)}) collective-permute-start(bf16[24,1792]{1,0:T(8,128)(2,1)S(1)} %get-tuple-element.56._.refs_0_), channel_id=1, source_target_pairs={{0,12},{1,15},{2,14},{3,13},{4,8},{5,11},{6,10},{7,9},{8,4},{9,7},... | collective-permute-start | bytes 258056 | tf_op jit(solution)/shard_map/ppermute | solution.py:427
  43.1 1.4 %collective-permute-start.14 = (bf16[24,1792]{1,0:T(8,128)(2,1)S(1)}, bf16[24,1792]{1,0:T(8,128)(2,1)S(1)}, u32[]{:S(2)}, u32[]{:S(2)}) collective-permute-start(bf16[24,1792]{1,0:T(8,128)(2,1)S(1)} %get-tuple-element.56._.refs_0_), channel_id=1, source_target_pairs={{0,4},{1,7},{2,6},{3,5},{4,0},{5,3},{6,2},{7,1},{8,12},{9,15},{10,... | collective-permute-start | bytes 258056 | tf_op jit(solution)/shard_map/ppermute | solution.py:427
  44.5 0.7 collective-permute-start.13
  45.1 3.4 %load.5.refs_11_ = bf16[576,7168]{1,0:T(8,128)(2,1)S(1)} custom-call(bf16[24,1792]{1,0:T(8,128)(2,1)S(1)} %get-tuple-element.56._.refs_0_, bf16[576,7168]{1,0:T(8,128)(2,1)} %source.1), custom_call_target="tpu_custom_call" | custom-call | bytes 16515072 | tf_op jit(solution)/shard_map/load/pallas_call | solution.py:63
  48.6 2.8 %collective-permute-done.15.refs_3_ = bf16[24,1792]{1,0:T(8,128)(2,1)S(1)} collective-permute-done((bf16[24,1792]{1,0:T(8,128)(2,1)S(1)}, bf16[24,1792]{1,0:T(8,128)(2,1)S(1)}, u32[]{:S(2)}, u32[]{:S(2)}) %collective-permute-start.15) | collective-permute-done | bytes 86048 | tf_op jit(solution)/shard_map/ppermute | solution.py:427
  51.3 0.2 collective-permute-start.19
  51.5 0.4 collective-permute-start.18
  51.9 0.2 collective-permute-start.17
  52.0 0.4 collective-permute-start.20
  52.4 0.3 collective-permute-done.19.refs_7_
  52.6 0.2 collective-permute-done.18.refs_6_
  52.8 0.4 collective-permute-done.17.refs_5_
  53.1 0.2 collective-permute-done.20.refs_8_
  53.3 6.5 %feed_forward.1 = (f32[96,1792]{1,0:T(8,128)S(1)}, bf16[96,1792]{1,0:T(8,128)(2,1)S(1)}) custom-call(bf16[24,1792]{1,0:T(8,128)(2,1)S(1)} %get-tuple-element.56._.refs_0_, bf16[24,1792]{1,0:T(8,128)(2,1)S(1)} %collective-permute-done.13.refs_1_, bf16[24,1792]{1,0:T(8,128)(2,1)S(1)} %collective-permute-done.14.refs_2_, ...), custom_call_target="tpu_custom_call" | custom-call | tf_op jit(solution)/shard_map/feed_forward/pallas_call | solution.py:375
  59.8 0.4 collective-permute-start.21
  60.2 1.3 %collective-permute-done.21.got_ref = bf16[96,1792]{1,0:T(8,128)(2,1)S(1)} collective-permute-done((bf16[96,1792]{1,0:T(8,128)(2,1)S(1)}, bf16[96,1792]{1,0:T(8,128)(2,1)S(1)}, u32[]{:S(2)}, u32[]{:S(2)}) %collective-permute-start.21) | collective-permute-done | bytes 344096 | tf_op jit(solution)/shard_map/ppermute | solution.py:423
  61.5 0.3 add_halves.3
  61.8 1.4 %collective-permute-start.22 = (bf16[24,1792]{1,0:T(8,128)(2,1)S(1)}, bf16[24,1792]{1,0:T(8,128)(2,1)S(1)}, u32[]{:S(2)}, u32[]{:S(2)}) collective-permute-start(bf16[24,1792]{1,0:T(8,128)(2,1)S(1)} %get-tuple-element.64), channel_id=1, source_target_pairs={{0,8},{1,11},{2,10},{3,9},{4,12},{5,15},{6,14},{7,13},{8,0},{9,3},... | collective-permute-start | bytes 258056 | tf_op jit(solution)/shard_map/ppermute | solution.py:427
  63.2 1.5 %collective-permute-start.23 = (bf16[24,1792]{1,0:T(8,128)(2,1)S(1)}, bf16[24,1792]{1,0:T(8,128)(2,1)S(1)}, u32[]{:S(2)}, u32[]{:S(2)}) collective-permute-start(bf16[24,1792]{1,0:T(8,128)(2,1)S(1)} %get-tuple-element.65), channel_id=1, source_target_pairs={{0,12},{1,15},{2,14},{3,13},{4,8},{5,11},{6,10},{7,9},{8,4},{9,7},... | collective-permute-start | bytes 258056 | tf_op jit(solution)/shard_map/ppermute | solution.py:427
  64.7 0.6 collective-permute-start.24
  65.4 0.7 collective-permute-start.25
  66.0 5.4 %collective-permute-done.22.refs_0_ = bf16[24,1792]{1,0:T(8,128)(2,1)S(1)} collective-permute-done((bf16[24,1792]{1,0:T(8,128)(2,1)S(1)}, bf16[24,1792]{1,0:T(8,128)(2,1)S(1)}, u32[]{:S(2)}, u32[]{:S(2)}) %collective-permute-start.22) | collective-permute-done | bytes 86048 | tf_op jit(solution)/shard_map/ppermute | solution.py:427
  71.4 1.7 %collective-permute-done.24.refs_2_ = bf16[24,1792]{1,0:T(8,128)(2,1)S(1)} collective-permute-done((bf16[24,1792]{1,0:T(8,128)(2,1)S(1)}, bf16[24,1792]{1,0:T(8,128)(2,1)S(1)}, u32[]{:S(2)}, u32[]{:S(2)}) %collective-permute-start.24) | collective-permute-done | bytes 86048 | tf_op jit(solution)/shard_map/ppermute | solution.py:427
  73.2 0.1 sum_units.3.mine_ref
  73.2 0.4 collective-permute-start.26
  73.7 1.1 %collective-permute-done.26.twin_ref = f32[24,1792]{1,0:T(8,128)S(1)} collective-permute-done((f32[24,1792]{1,0:T(8,128)S(1)}, f32[24,1792]{1,0:T(8,128)S(1)}, u32[]{:S(2)}, u32[]{:S(2)}) %collective-permute-start.26) | collective-permute-done | bytes 172064 | tf_op jit(solution)/shard_map/ppermute | solution.py:423
  74.7 1.4 %final_rows.1 = bf16[3,7168]{1,0:T(4,128)(2,1)} custom-call(s32[8]{0:T(128)S(1)} %copy-done, f32[24,1792]{1,0:T(8,128)S(1)} %sum_units.3.mine_ref, f32[24,1792]{1,0:T(8,128)S(1)} %collective-permute-done.26.twin_ref), custom_call_target="tpu_custom_call" | custom-call | tf_op jit(solution)/shard_map/final_rows/pallas_call | solution.py:403
  (20 shorter events, 0.1 us)
Async XLA Ops:
  5.2 11.4 %collective-permute-start = (bf16[6,8,512]{2,1,0:T(8,128)(2,1)S(1)}, bf16[6,8,512]{2,1,0:T(8,128)(2,1)S(1)}, u32[]{:S(2)}, u32[]{:S(2)}) collective-permute-start(bf16[6,8,512]{2,1,0:T(8,128)(2,1)S(1)} %get-tuple-element.36), channel_id=1, source_target_pairs={{0,12},{2,14},{4,8},{6,10},{8,4},{10,6},{12,0},{14,2},{1,13},{3,15... | collective-permute-start | bytes 147464 | tf_op jit(solution)/shard_map/ppermute | solution.py:420
  10.3 6.3 %collective-permute-start.1 = (bf16[6,8,512]{2,1,0:T(8,128)(2,1)S(1)}, bf16[6,8,512]{2,1,0:T(8,128)(2,1)S(1)}, u32[]{:S(2)}, u32[]{:S(2)}) collective-permute-start(bf16[6,8,512]{2,1,0:T(8,128)(2,1)S(1)} %get-tuple-element.37), channel_id=1, source_target_pairs={{0,8},{2,10},{4,12},{6,14},{8,0},{10,2},{12,4},{14,6},{1,9},{3,11}... | collective-permute-start | bytes 147464 | tf_op jit(solution)/shard_map/ppermute | solution.py:420
  10.3 11.2 %collective-permute-start.2 = (bf16[6,8,512]{2,1,0:T(8,128)(2,1)S(1)}, bf16[6,8,512]{2,1,0:T(8,128)(2,1)S(1)}, u32[]{:S(2)}, u32[]{:S(2)}) collective-permute-start(bf16[6,8,512]{2,1,0:T(8,128)(2,1)S(1)} %get-tuple-element.38), channel_id=1, source_target_pairs={{0,14},{2,12},{4,10},{6,8},{8,6},{10,4},{12,2},{14,0},{1,15},{3,13... | collective-permute-start | bytes 147464 | tf_op jit(solution)/shard_map/ppermute | solution.py:420
  13.2 8.3 %collective-permute-start.3 = (bf16[6,8,512]{2,1,0:T(8,128)(2,1)S(1)}, bf16[6,8,512]{2,1,0:T(8,128)(2,1)S(1)}, u32[]{:S(2)}, u32[]{:S(2)}) collective-permute-start(bf16[6,8,512]{2,1,0:T(8,128)(2,1)S(1)} %get-tuple-element.39), channel_id=1, source_target_pairs={{0,10},{2,8},{4,14},{6,12},{8,2},{10,0},{12,6},{14,4},{1,11},{3,9}... | collective-permute-start | bytes 147464 | tf_op jit(solution)/shard_map/ppermute | solution.py:420
  14.2 7.3 %collective-permute-start.4 = (bf16[6,8,512]{2,1,0:T(8,128)(2,1)S(1)}, bf16[6,8,512]{2,1,0:T(8,128)(2,1)S(1)}, u32[]{:S(2)}, u32[]{:S(2)}) collective-permute-start(bf16[6,8,512]{2,1,0:T(8,128)(2,1)S(1)} %get-tuple-element.40), channel_id=1, source_target_pairs={{0,6},{2,4},{4,2},{6,0},{8,14},{10,12},{12,10},{14,8},{1,7},{3,5},... | collective-permute-start | bytes 147464 | tf_op jit(solution)/shard_map/ppermute | solution.py:420
  16.6 5.0 %collective-permute-start.5 = (bf16[6,8,512]{2,1,0:T(8,128)(2,1)S(1)}, bf16[6,8,512]{2,1,0:T(8,128)(2,1)S(1)}, u32[]{:S(2)}, u32[]{:S(2)}) collective-permute-start(bf16[6,8,512]{2,1,0:T(8,128)(2,1)S(1)} %get-tuple-element.41), channel_id=1, source_target_pairs={{0,4},{2,6},{4,0},{6,2},{8,12},{10,14},{12,8},{14,10},{1,5},{3,7},... | collective-permute-start | bytes 147464 | tf_op jit(solution)/shard_map/ppermute | solution.py:420
  16.6 5.0 %collective-permute-start.6 = (bf16[6,8,512]{2,1,0:T(8,128)(2,1)S(1)}, bf16[6,8,512]{2,1,0:T(8,128)(2,1)S(1)}, u32[]{:S(2)}, u32[]{:S(2)}) collective-permute-start(bf16[6,8,512]{2,1,0:T(8,128)(2,1)S(1)} %get-tuple-element.42), channel_id=1, source_target_pairs={{0,2},{2,0},{4,6},{6,4},{8,10},{10,8},{12,14},{14,12},{1,3},{3,1},... | collective-permute-start | bytes 147464 | tf_op jit(solution)/shard_map/ppermute | solution.py:420
  25.0 1.7 %collective-permute-start.7 = (bf16[96,1792]{1,0:T(8,128)(2,1)S(1)}, bf16[96,1792]{1,0:T(8,128)(2,1)S(1)}, u32[]{:S(2)}, u32[]{:S(2)}) collective-permute-start(bf16[96,1792]{1,0:T(8,128)(2,1)S(1)} %get-tuple-element.48), channel_id=1, source_target_pairs={{0,1},{1,0},{2,3},{3,2},{4,5},{5,4},{6,7},{7,6},{8,9},{9,8},{10,11... | collective-permute-start | bytes 1032200 | tf_op jit(solution)/shard_map/ppermute | solution.py:423
  27.0 9.6 %collective-permute-start.8 = (bf16[24,1792]{1,0:T(8,128)(2,1)S(1)}, bf16[24,1792]{1,0:T(8,128)(2,1)S(1)}, u32[]{:S(2)}, u32[]{:S(2)}) collective-permute-start(bf16[24,1792]{1,0:T(8,128)(2,1)S(1)} %get-tuple-element.52), channel_id=1, source_target_pairs={{0,8},{1,11},{2,10},{3,9},{4,12},{5,15},{6,14},{7,13},{8,0},{9,3},... | collective-permute-start | bytes 258056 | tf_op jit(solution)/shard_map/ppermute | solution.py:427
  28.6 7.9 %collective-permute-start.9 = (bf16[24,1792]{1,0:T(8,128)(2,1)S(1)}, bf16[24,1792]{1,0:T(8,128)(2,1)S(1)}, u32[]{:S(2)}, u32[]{:S(2)}) collective-permute-start(bf16[24,1792]{1,0:T(8,128)(2,1)S(1)} %get-tuple-element.53), channel_id=1, source_target_pairs={{0,12},{1,15},{2,14},{3,13},{4,8},{5,11},{6,10},{7,9},{8,4},{9,7},... | collective-permute-start | bytes 258056 | tf_op jit(solution)/shard_map/ppermute | solution.py:427
  30.7 7.4 %collective-permute-start.10 = (bf16[24,1792]{1,0:T(8,128)(2,1)S(1)}, bf16[24,1792]{1,0:T(8,128)(2,1)S(1)}, u32[]{:S(2)}, u32[]{:S(2)}) collective-permute-start(bf16[24,1792]{1,0:T(8,128)(2,1)S(1)} %get-tuple-element.54), channel_id=1, source_target_pairs={{0,4},{1,7},{2,6},{3,5},{4,0},{5,3},{6,2},{7,1},{8,12},{9,15},{10,... | collective-permute-start | bytes 258056 | tf_op jit(solution)/shard_map/ppermute | solution.py:427
  31.1 6.9 %collective-permute-start.11 = (bf16[24,1792]{1,0:T(8,128)(2,1)S(1)}, bf16[24,1792]{1,0:T(8,128)(2,1)S(1)}, u32[]{:S(2)}, u32[]{:S(2)}) collective-permute-start(bf16[24,1792]{1,0:T(8,128)(2,1)S(1)} %get-tuple-element.50._.own_ref), channel_id=1, source_target_pairs={{1,3},{3,1},{5,7},{7,5},{9,11},{11,9},{13,15},{15,13},{17,19},{19,... | collective-permute-start | bytes 258056 | tf_op jit(solution)/shard_map/ppermute | solution.py:427
  38.1 1.7 %collective-permute-start.12 = (f32[24,1792]{1,0:T(8,128)S(1)}, f32[24,1792]{1,0:T(8,128)S(1)}, u32[]{:S(2)}, u32[]{:S(2)}) collective-permute-start(f32[24,1792]{1,0:T(8,128)S(1)} %sum_units.2.mine_ref), channel_id=1, source_target_pairs={{0,1},{1,0},{2,3},{3,2},{4,5},{5,4},{6,7},{7,6},{8,9},{9,8},{10,11... | collective-permute-start | bytes 516104 | tf_op jit(solution)/shard_map/ppermute | solution.py:423
  40.0 8.6 %collective-permute-start.16 = (bf16[24,1792]{1,0:T(8,128)(2,1)S(1)}, bf16[24,1792]{1,0:T(8,128)(2,1)S(1)}, u32[]{:S(2)}, u32[]{:S(2)}) collective-permute-start(bf16[24,1792]{1,0:T(8,128)(2,1)S(1)} %get-tuple-element.56._.refs_0_), channel_id=1, source_target_pairs={{0,12},{1,15},{2,14},{3,13},{4,8},{5,11},{6,10},{7,9},{8,4},{9,7},... | collective-permute-start | bytes 258056 | tf_op jit(solution)/shard_map/ppermute | solution.py:427
  43.1 8.3 %collective-permute-start.15 = (bf16[24,1792]{1,0:T(8,128)(2,1)S(1)}, bf16[24,1792]{1,0:T(8,128)(2,1)S(1)}, u32[]{:S(2)}, u32[]{:S(2)}) collective-permute-start(bf16[24,1792]{1,0:T(8,128)(2,1)S(1)} %get-tuple-element.56._.refs_0_), channel_id=1, source_target_pairs={{0,8},{1,11},{2,10},{3,9},{4,12},{5,15},{6,14},{7,13},{8,0},{9,3},... | collective-permute-start | bytes 258056 | tf_op jit(solution)/shard_map/ppermute | solution.py:427
  43.1 8.4 %collective-permute-start.14 = (bf16[24,1792]{1,0:T(8,128)(2,1)S(1)}, bf16[24,1792]{1,0:T(8,128)(2,1)S(1)}, u32[]{:S(2)}, u32[]{:S(2)}) collective-permute-start(bf16[24,1792]{1,0:T(8,128)(2,1)S(1)} %get-tuple-element.56._.refs_0_), channel_id=1, source_target_pairs={{0,4},{1,7},{2,6},{3,5},{4,0},{5,3},{6,2},{7,1},{8,12},{9,15},{10,... | collective-permute-start | bytes 258056 | tf_op jit(solution)/shard_map/ppermute | solution.py:427
  44.5 7.4 %collective-permute-start.13 = (bf16[24,1792]{1,0:T(8,128)(2,1)S(1)}, bf16[24,1792]{1,0:T(8,128)(2,1)S(1)}, u32[]{:S(2)}, u32[]{:S(2)}) collective-permute-start(bf16[24,1792]{1,0:T(8,128)(2,1)S(1)} %get-tuple-element.56._.refs_0_), channel_id=1, source_target_pairs={{1,3},{3,1},{5,7},{7,5},{9,11},{11,9},{13,15},{15,13},{17,19},{19,... | collective-permute-start | bytes 258056 | tf_op jit(solution)/shard_map/ppermute | solution.py:427
  51.3 1.3 %collective-permute-start.19 = (bf16[24,1792]{1,0:T(8,128)(2,1)S(1)}, bf16[24,1792]{1,0:T(8,128)(2,1)S(1)}, u32[]{:S(2)}, u32[]{:S(2)}) collective-permute-start(bf16[24,1792]{1,0:T(8,128)(2,1)S(1)} %collective-permute-done.15.refs_3_), channel_id=1, source_target_pairs={{0,1},{1,0},{2,3},{3,2},{4,5},{5,4},{6,7},{7,6},{8,9},{9,8},{10,11... | collective-permute-start | bytes 258056 | tf_op jit(solution)/shard_map/ppermute | solution.py:423
  51.5 1.3 %collective-permute-start.18 = (bf16[24,1792]{1,0:T(8,128)(2,1)S(1)}, bf16[24,1792]{1,0:T(8,128)(2,1)S(1)}, u32[]{:S(2)}, u32[]{:S(2)}) collective-permute-start(bf16[24,1792]{1,0:T(8,128)(2,1)S(1)} %collective-permute-done.14.refs_2_), channel_id=1, source_target_pairs={{0,1},{1,0},{2,3},{3,2},{4,5},{5,4},{6,7},{7,6},{8,9},{9,8},{10,11... | collective-permute-start | bytes 258056 | tf_op jit(solution)/shard_map/ppermute | solution.py:423
  51.9 1.3 %collective-permute-start.17 = (bf16[24,1792]{1,0:T(8,128)(2,1)S(1)}, bf16[24,1792]{1,0:T(8,128)(2,1)S(1)}, u32[]{:S(2)}, u32[]{:S(2)}) collective-permute-start(bf16[24,1792]{1,0:T(8,128)(2,1)S(1)} %collective-permute-done.13.refs_1_), channel_id=1, source_target_pairs={{0,1},{1,0},{2,3},{3,2},{4,5},{5,4},{6,7},{7,6},{8,9},{9,8},{10,11... | collective-permute-start | bytes 258056 | tf_op jit(solution)/shard_map/ppermute | solution.py:423
  52.0 1.3 %collective-permute-start.20 = (bf16[24,1792]{1,0:T(8,128)(2,1)S(1)}, bf16[24,1792]{1,0:T(8,128)(2,1)S(1)}, u32[]{:S(2)}, u32[]{:S(2)}) collective-permute-start(bf16[24,1792]{1,0:T(8,128)(2,1)S(1)} %collective-permute-done.16.refs_4_), channel_id=1, source_target_pairs={{0,1},{1,0},{2,3},{3,2},{4,5},{5,4},{6,7},{7,6},{8,9},{9,8},{10,11... | collective-permute-start | bytes 258056 | tf_op jit(solution)/shard_map/ppermute | solution.py:423
  53.3 21.4 %copy-start = (s32[8]{0:T(128)S(1)}, s32[8]{0:T(128)}, u32[]{:S(2)}) copy-start(s32[8]{0:T(128)} %counts_ref.1) | copy-start | bytes 100
  59.8 1.7 %collective-permute-start.21 = (bf16[96,1792]{1,0:T(8,128)(2,1)S(1)}, bf16[96,1792]{1,0:T(8,128)(2,1)S(1)}, u32[]{:S(2)}, u32[]{:S(2)}) collective-permute-start(bf16[96,1792]{1,0:T(8,128)(2,1)S(1)} %get-tuple-element.61), channel_id=1, source_target_pairs={{0,1},{1,0},{2,3},{3,2},{4,5},{5,4},{6,7},{7,6},{8,9},{9,8},{10,11... | collective-permute-start | bytes 1032200 | tf_op jit(solution)/shard_map/ppermute | solution.py:423
  61.8 9.6 %collective-permute-start.22 = (bf16[24,1792]{1,0:T(8,128)(2,1)S(1)}, bf16[24,1792]{1,0:T(8,128)(2,1)S(1)}, u32[]{:S(2)}, u32[]{:S(2)}) collective-permute-start(bf16[24,1792]{1,0:T(8,128)(2,1)S(1)} %get-tuple-element.64), channel_id=1, source_target_pairs={{0,8},{1,11},{2,10},{3,9},{4,12},{5,15},{6,14},{7,13},{8,0},{9,3},... | collective-permute-start | bytes 258056 | tf_op jit(solution)/shard_map/ppermute | solution.py:427
  63.2 8.2 %collective-permute-start.23 = (bf16[24,1792]{1,0:T(8,128)(2,1)S(1)}, bf16[24,1792]{1,0:T(8,128)(2,1)S(1)}, u32[]{:S(2)}, u32[]{:S(2)}) collective-permute-start(bf16[24,1792]{1,0:T(8,128)(2,1)S(1)} %get-tuple-element.65), channel_id=1, source_target_pairs={{0,12},{1,15},{2,14},{3,13},{4,8},{5,11},{6,10},{7,9},{8,4},{9,7},... | collective-permute-start | bytes 258056 | tf_op jit(solution)/shard_map/ppermute | solution.py:427
  64.7 8.4 %collective-permute-start.24 = (bf16[24,1792]{1,0:T(8,128)(2,1)S(1)}, bf16[24,1792]{1,0:T(8,128)(2,1)S(1)}, u32[]{:S(2)}, u32[]{:S(2)}) collective-permute-start(bf16[24,1792]{1,0:T(8,128)(2,1)S(1)} %get-tuple-element.66), channel_id=1, source_target_pairs={{0,4},{1,7},{2,6},{3,5},{4,0},{5,3},{6,2},{7,1},{8,12},{9,15},{10,... | collective-permute-start | bytes 258056 | tf_op jit(solution)/shard_map/ppermute | solution.py:427
  65.4 7.8 %collective-permute-start.25 = (bf16[24,1792]{1,0:T(8,128)(2,1)S(1)}, bf16[24,1792]{1,0:T(8,128)(2,1)S(1)}, u32[]{:S(2)}, u32[]{:S(2)}) collective-permute-start(bf16[24,1792]{1,0:T(8,128)(2,1)S(1)} %get-tuple-element.62.own_ref), channel_id=1, source_target_pairs={{1,3},{3,1},{5,7},{7,5},{9,11},{11,9},{13,15},{15,13},{17,19},{19,... | collective-permute-start | bytes 258056 | tf_op jit(solution)/shard_map/ppermute | solution.py:427
  73.2 1.5 %collective-permute-start.26 = (f32[24,1792]{1,0:T(8,128)S(1)}, f32[24,1792]{1,0:T(8,128)S(1)}, u32[]{:S(2)}, u32[]{:S(2)}) collective-permute-start(f32[24,1792]{1,0:T(8,128)S(1)} %sum_units.3.mine_ref), channel_id=1, source_target_pairs={{0,1},{1,0},{2,3},{3,2},{4,5},{5,4},{6,7},{7,6},{8,9},{9,8},{10,11... | collective-permute-start | bytes 516104 | tf_op jit(solution)/shard_map/ppermute | solution.py:423

commit v4 on v3

--- a/solution.py
+++ b/solution.py
@@ -84,10 +84,10 @@
 def attention_kernel(n_dp, counts_hbm, lengths_hbm, q_hbm, cache_hbm, residual_hbm, gain_hbm, *refs):
     n_weights = 2
     weights, outs = refs[:n_weights], refs[n_weights : n_weights + n_dp]
-    residual_unit, gain_unit, to_heads, to_units, to_parts = refs[n_weights + n_dp : n_weights + n_dp + 5]
-    loaded = refs[n_weights + n_dp + 5 : 2 * n_weights + n_dp + 5]
+    residual_unit, gain_unit, live_ref, to_heads, to_units, to_parts = refs[n_weights + n_dp : n_weights + n_dp + 6]
+    loaded = refs[n_weights + n_dp + 6 : 2 * n_weights + n_dp + 6]
     counts_ref, lengths_ref, q_ref, cache_ref, residual_ref, gain_ref, held, sems, weight_sems = refs[
-        2 * n_weights + n_dp + 5 :
+        2 * n_weights + n_dp + 6 :
     ]
     slots = q_ref.shape[0]
     pairs = [
@@ -122,6 +122,8 @@
     for k in range(n_dp):
         for row in rows:
             outs[k][row] = held[row, me ^ k]
+    _, slot = row_ids(*live_ref.shape, slots)
+    live_ref[...] = (slot < counts_ref[me].astype(f32)).astype(f32)
     to_heads[...] = regroup(to_heads.shape[0], held.shape[2], n_dp * slots)
     to_units[...] = regroup(to_units.shape[0], n_dp // 2, PARTS)
     to_parts[...] = regroup(to_parts.shape[0], PARTS, n_dp)
@@ -146,6 +148,7 @@
     block = jax.ShapeDtypeStruct((slots, per_rank, LATENT_WIDTH), bf16)
     unit = jax.ShapeDtypeStruct((slots * PARTS, part), f32)
     rows = n_dp * slots
+    live = jax.ShapeDtypeStruct((slots * PARTS, 128), f32)
     moves = [jax.ShapeDtypeStruct((n, n), bf16) for n in (rows * per_rank, rows * PARTS // 2, rows * PARTS)]
     loaded = [
         jax.ShapeDtypeStruct(value_up.shape, bf16),
@@ -153,9 +156,9 @@
     ]
     return pl.pallas_call(
         functools.partial(attention_kernel, n_dp),
-        out_shape=[block] * n_dp + [unit] * 2 + moves + loaded,
+        out_shape=[block] * n_dp + [unit] * 2 + [live] + moves + loaded,
         in_specs=[pl.BlockSpec(memory_space=pl.ANY)] * 8,
-        out_specs=vmem(n_dp + 7),
+        out_specs=vmem(n_dp + 8),
         scratch_shapes=[
             pltpu.SMEM(counts.shape, jnp.int32),
             pltpu.SMEM(lengths.shape, jnp.int32),
@@ -362,8 +365,13 @@
         rows_ref[:, pl.ds(q * part, part)] = moved[q * rows : (q + 1) * rows]
     x = rows_ref[...]
     contract = (((1,), (1,)), ((), ()))
-    gate = lax.dot_general(x, gate_ref[...], contract, preferred_element_type=f32)
-    up = lax.dot_general(x, up_ref[...], contract, preferred_element_type=f32)
+    gate = up = None
+    for q in range(PARTS):
+        at = pl.ds(q * part, part)
+        gate_q = lax.dot_general(x[:, q * part : (q + 1) * part], gate_ref[:, at], contract, preferred_element_type=f32)
+        up_q = lax.dot_general(x[:, q * part : (q + 1) * part], up_ref[:, at], contract, preferred_element_type=f32)
+        gate = gate_q if q == 0 else gate + gate_q
+        up = up_q if q == 0 else up + up_q
     hidden = (gate / (1.0 + jnp.exp(-gate)) * up).astype(bf16)
     write_parts(hidden, lambda q: down_ref[:, pl.ds(q * part, part)], keep_ref, give_ref)
 
@@ -383,12 +391,11 @@
     )(normed, *own, *other, gate_t, up_t, down, move)
 
 
-def final_kernel(slots, owner_rows, counts_ref, mine_ref, twin_ref, out_ref):
-    me, me_head = lax.axis_index("dp"), lax.axis_index("head")
+def final_kernel(slots, owner_rows, live_ref, mine_ref, twin_ref, out_ref):
+    me_head = lax.axis_index("head")
     total = mine_ref[...] + twin_ref[...]
     rows = total.shape[0]
-    _, slot = row_ids(rows, 1, slots)
-    total = jnp.where(slot < counts_ref[me].astype(f32), total, 0.0).astype(bf16)
+    total = jnp.where(live_ref[:, :1] > 0.5, total, 0.0).astype(bf16)
     part = total.shape[1]
     padded = 8
     i = lax.broadcasted_iota(jnp.int32, (padded, rows), 0)
@@ -399,15 +406,15 @@
         out_ref[:, pl.ds(q * part, part)] = chosen[:owner_rows].astype(bf16)
 
 
-def final_rows(slots, owner_rows, counts, mine, twin):
+def final_rows(slots, owner_rows, live, mine, twin):
     return pl.pallas_call(
         functools.partial(final_kernel, slots, owner_rows),
         out_shape=jax.ShapeDtypeStruct((owner_rows, mine.shape[1] * PARTS), bf16),
-        in_specs=[pl.BlockSpec(memory_space=pltpu.SMEM)] + vmem(2),
+        in_specs=vmem(3),
         out_specs=vmem(1)[0],
         compiler_params=params(4),
         name="final_rows",
-    )(counts, mine, twin)
+    )(live, mine, twin)
 
 
 def on_device(n_dp, queries, latent_key_cache, lengths, counts, residual, value_up_weight,
@@ -429,7 +436,7 @@
     outs = attend(
         n_dp, counts, lengths, queries, latent_key_cache, residual, norm_gain, value_up_weight[0], output_proj[0]
     )
-    blocks, (residual_unit, gain_unit, to_heads, to_units, to_parts, value_up, most) = outs[:n_dp], outs[n_dp:]
+    blocks, (residual_unit, gain_unit, live, to_heads, to_units, to_parts, value_up, most) = outs[:n_dp], outs[n_dp:]
     def reduce_units(keep, give, base, weights):
         units = add_halves(half, keep, to_twin(give), to_units)
         weights = [load(units[0], w) for w in weights]
@@ -450,7 +457,7 @@
     own, other = [own[s] for s in range(half)], [other[s] for s in range(half)]
     keep, give = feed_forward(n_dp, slots, normed, own, other, gate, up, down, to_parts)
     mine, twin, _ = reduce_units(keep, give, state, [])
-    return final_rows(slots, owner_rows, counts, mine, twin)
+    return final_rows(slots, owner_rows, live, mine, twin)
 
 
 def solution(mesh):

time: 76.3 us -> 75.5 us (0.990)
  no operation moved by 1% of the time
where the time goes in v4:
time: 75.5 us; the launch traced here: 75.4 us
  starting transfers between devices  29.6 us (39%)
  Pallas kernels  26.9 us (36%)
  waiting for transfers between devices  18.7 us (25%)
    ppermute x12, starting transfers between devices, to_set(): return lax.ppermute(x, ('dp', 'head'), pairs)  14.1 us
    ppermute x7, starting transfers between devices, to_peer(): return lax.ppermute(x, 'dp', [(i, i ^ k) for i in range(n_dp)])  12.9 us
    ppermute x12, waiting for transfers between devices, to_set(): return lax.ppermute(x, ('dp', 'head'), pairs)  12.7 us
    pallas_call x3, Pallas kernels, load(): pl.pallas_call(load_kernel, out_shape=jax.ShapeDtypeStruct(weight.shape,...  10.3 us
    pallas_call x1, Pallas kernels, feed_forward(): pl.pallas_call(functools.partial(ffn_kernel, n_dp, slots), out_shape=[out...  6.3 us
    ppermute x8, waiting for transfers between devices, to_twin(): return lax.ppermute(x, 'head', [(0, 1), (1, 0)])  5.96 us
    pallas_call x1, Pallas kernels, attend(): pl.pallas_call(functools.partial(attention_kernel, n_dp), out_shape=[bloc...  5.18 us
    pallas_call x1, Pallas kernels, project(): pl.pallas_call(functools.partial(project_kernel, n_dp, slots), out_shape=...  3.43 us
  transfers between devices with their start and end apart: 27, of which 13 were waited for; matrix products, arithmetic and copies ran while one was open for 0% of the time, Pallas kernels for 14%

profile of v4, /device:TPU:0, one launch (start us, length us, event | category | flops | bytes accessed | tf_op | source)
XLA Modules:
  0.0 75.4 jit_solution(15726373309472047234)
XLA Ops:
  0.0 5.2 %attend.1 = (bf16[6,8,512]{2,1,0:T(8,128)(2,1)S(1)}, bf16[6,8,512]{2,1,0:T(8,128)(2,1)S(1)}, bf16[6,8,512]{2,1,0:T(8,128)(2,1)S(1)}, bf16[6,8,512]{2,1,0:T(8,128...) custom-call(s32[8]{0:T(128)} %counts_hbm.1, ...), custom_call_target="tpu_custom_call" | custom-call | tf_op jit(solution)/shard_map/attend/pallas_call | solution.py:157
  5.2 5.1 %collective-permute-start = (bf16[6,8,512]{2,1,0:T(8,128)(2,1)S(1)}, bf16[6,8,512]{2,1,0:T(8,128)(2,1)S(1)}, u32[]{:S(2)}, u32[]{:S(2)}) collective-permute-start(bf16[6,8,512]{2,1,0:T(8,128)(2,1)S(1)} %get-tuple-element.38), channel_id=1, source_target_pairs={{0,12},{2,14},{4,8},{6,10},{8,4},{10,6},{12,0},{14,2},{1,13},{3,15... | collective-permute-start | bytes 147464 | tf_op jit(solution)/shard_map/ppermute | solution.py:427
  10.3 2.9 %collective-permute-start.2 = (bf16[6,8,512]{2,1,0:T(8,128)(2,1)S(1)}, bf16[6,8,512]{2,1,0:T(8,128)(2,1)S(1)}, u32[]{:S(2)}, u32[]{:S(2)}) collective-permute-start(bf16[6,8,512]{2,1,0:T(8,128)(2,1)S(1)} %get-tuple-element.40), channel_id=1, source_target_pairs={{0,14},{2,12},{4,10},{6,8},{8,6},{10,4},{12,2},{14,0},{1,15},{3,13... | collective-permute-start | bytes 147464 | tf_op jit(solution)/shard_map/ppermute | solution.py:427
  13.2 1.0 %collective-permute-start.3 = (bf16[6,8,512]{2,1,0:T(8,128)(2,1)S(1)}, bf16[6,8,512]{2,1,0:T(8,128)(2,1)S(1)}, u32[]{:S(2)}, u32[]{:S(2)}) collective-permute-start(bf16[6,8,512]{2,1,0:T(8,128)(2,1)S(1)} %get-tuple-element.41), channel_id=1, source_target_pairs={{0,10},{2,8},{4,14},{6,12},{8,2},{10,0},{12,6},{14,4},{1,11},{3,9}... | collective-permute-start | bytes 147464 | tf_op jit(solution)/shard_map/ppermute | solution.py:427
  14.2 2.4 %collective-permute-start.4 = (bf16[6,8,512]{2,1,0:T(8,128)(2,1)S(1)}, bf16[6,8,512]{2,1,0:T(8,128)(2,1)S(1)}, u32[]{:S(2)}, u32[]{:S(2)}) collective-permute-start(bf16[6,8,512]{2,1,0:T(8,128)(2,1)S(1)} %get-tuple-element.42), channel_id=1, source_target_pairs={{0,6},{2,4},{4,2},{6,0},{8,14},{10,12},{12,10},{14,8},{1,7},{3,5},... | collective-permute-start | bytes 147464 | tf_op jit(solution)/shard_map/ppermute | solution.py:427
  16.6 1.5 %collective-permute-start.6 = (bf16[6,8,512]{2,1,0:T(8,128)(2,1)S(1)}, bf16[6,8,512]{2,1,0:T(8,128)(2,1)S(1)}, u32[]{:S(2)}, u32[]{:S(2)}) collective-permute-start(bf16[6,8,512]{2,1,0:T(8,128)(2,1)S(1)} %get-tuple-element.44), channel_id=1, source_target_pairs={{0,2},{2,0},{4,6},{6,4},{8,10},{10,8},{12,14},{14,12},{1,3},{3,1},... | collective-permute-start | bytes 147464 | tf_op jit(solution)/shard_map/ppermute | solution.py:427
  18.1 3.4 %load.3.refs_12_.refs_9_ = bf16[576,7168]{1,0:T(8,128)(2,1)S(1)} custom-call(bf16[6,8,512]{2,1,0:T(8,128)(2,1)S(1)} %get-tuple-element.45._.refs_7_, bf16[576,7168]{1,0:T(8,128)(2,1)} %bitcast.6), custom_call_target="tpu_custom_call" | custom-call | bytes 16515072 | tf_op jit(solution)/shard_map/load/pallas_call | solution.py:63
  21.6 3.4 %project.1 = (f32[96,1792]{1,0:T(8,128)S(1)}, bf16[96,1792]{1,0:T(8,128)(2,1)S(1)}) custom-call(bf16[6,8,512]{2,1,0:T(8,128)(2,1)S(1)} %collective-permute-done.refs_0_, bf16[6,8,512]{2,1,0:T(8,128)(2,1)S(1)} %collective-permute-done.1.refs_1_, bf16[6,8,512]{2,1,0:T(8,128)(2,1)S(1)} %collective-permute-done.2.refs_2_, ...), custom_call_target="tpu_custom_call" | custom-call | tf_op jit(solution)/shard_map/project/pallas_call | solution.py:263
  25.0 0.1 collective-permute-start.7
  25.1 1.6 %collective-permute-done.7.got_ref = bf16[96,1792]{1,0:T(8,128)(2,1)S(1)} collective-permute-done((bf16[96,1792]{1,0:T(8,128)(2,1)S(1)}, bf16[96,1792]{1,0:T(8,128)(2,1)S(1)}, u32[]{:S(2)}, u32[]{:S(2)}) %collective-permute-start.7) | collective-permute-done | bytes 344096 | tf_op jit(solution)/shard_map/ppermute | solution.py:430
  26.7 0.2 add_halves.2
  27.0 1.6 %collective-permute-start.8 = (bf16[24,1792]{1,0:T(8,128)(2,1)S(1)}, bf16[24,1792]{1,0:T(8,128)(2,1)S(1)}, u32[]{:S(2)}, u32[]{:S(2)}) collective-permute-start(bf16[24,1792]{1,0:T(8,128)(2,1)S(1)} %get-tuple-element.54), channel_id=1, source_target_pairs={{0,8},{1,11},{2,10},{3,9},{4,12},{5,15},{6,14},{7,13},{8,0},{9,3},... | collective-permute-start | bytes 258056 | tf_op jit(solution)/shard_map/ppermute | solution.py:434
  28.6 2.0 %collective-permute-start.9 = (bf16[24,1792]{1,0:T(8,128)(2,1)S(1)}, bf16[24,1792]{1,0:T(8,128)(2,1)S(1)}, u32[]{:S(2)}, u32[]{:S(2)}) collective-permute-start(bf16[24,1792]{1,0:T(8,128)(2,1)S(1)} %get-tuple-element.55), channel_id=1, source_target_pairs={{0,12},{1,15},{2,14},{3,13},{4,8},{5,11},{6,10},{7,9},{8,4},{9,7},... | collective-permute-start | bytes 258056 | tf_op jit(solution)/shard_map/ppermute | solution.py:434
  30.7 0.5 collective-permute-start.10
  31.1 0.7 collective-permute-start.11
  31.8 3.4 %load.4.refs_4_.refs_10_ = bf16[576,7168]{1,0:T(8,128)(2,1)S(1)} custom-call(bf16[24,1792]{1,0:T(8,128)(2,1)S(1)} %get-tuple-element.52._.own_ref, bf16[576,7168]{1,0:T(8,128)(2,1)} %bitcast.7), custom_call_target="tpu_custom_call" | custom-call | bytes 16515072 | tf_op jit(solution)/shard_map/load/pallas_call | solution.py:63
  35.2 1.3 %collective-permute-done.8.refs_0_ = bf16[24,1792]{1,0:T(8,128)(2,1)S(1)} collective-permute-done((bf16[24,1792]{1,0:T(8,128)(2,1)S(1)}, bf16[24,1792]{1,0:T(8,128)(2,1)S(1)}, u32[]{:S(2)}, u32[]{:S(2)}) %collective-permute-start.8) | collective-permute-done | bytes 86048 | tf_op jit(solution)/shard_map/ppermute | solution.py:434
  36.5 1.5 %collective-permute-done.10.refs_2_ = bf16[24,1792]{1,0:T(8,128)(2,1)S(1)} collective-permute-done((bf16[24,1792]{1,0:T(8,128)(2,1)S(1)}, bf16[24,1792]{1,0:T(8,128)(2,1)S(1)}, u32[]{:S(2)}, u32[]{:S(2)}) %collective-permute-start.10) | collective-permute-done | bytes 86048 | tf_op jit(solution)/shard_map/ppermute | solution.py:434
  38.1 0.7 collective-permute-start.12
  38.8 1.0 %collective-permute-done.12.twin_ref = f32[24,1792]{1,0:T(8,128)S(1)} collective-permute-done((f32[24,1792]{1,0:T(8,128)S(1)}, f32[24,1792]{1,0:T(8,128)S(1)}, u32[]{:S(2)}, u32[]{:S(2)}) %collective-permute-start.12) | collective-permute-done | bytes 172064 | tf_op jit(solution)/shard_map/ppermute | solution.py:430
  39.8 0.1 norm_rows.1
  40.0 3.1 %collective-permute-start.16 = (bf16[24,1792]{1,0:T(8,128)(2,1)S(1)}, bf16[24,1792]{1,0:T(8,128)(2,1)S(1)}, u32[]{:S(2)}, u32[]{:S(2)}) collective-permute-start(bf16[24,1792]{1,0:T(8,128)(2,1)S(1)} %get-tuple-element.58._.refs_0_), channel_id=1, source_target_pairs={{0,12},{1,15},{2,14},{3,13},{4,8},{5,11},{6,10},{7,9},{8,4},{9,7},... | collective-permute-start | bytes 258056 | tf_op jit(solution)/shard_map/ppermute | solution.py:434
  43.1 1.4 %collective-permute-start.14 = (bf16[24,1792]{1,0:T(8,128)(2,1)S(1)}, bf16[24,1792]{1,0:T(8,128)(2,1)S(1)}, u32[]{:S(2)}, u32[]{:S(2)}) collective-permute-start(bf16[24,1792]{1,0:T(8,128)(2,1)S(1)} %get-tuple-element.58._.refs_0_), channel_id=1, source_target_pairs={{0,4},{1,7},{2,6},{3,5},{4,0},{5,3},{6,2},{7,1},{8,12},{9,15},{10,... | collective-permute-start | bytes 258056 | tf_op jit(solution)/shard_map/ppermute | solution.py:434
  44.5 0.7 collective-permute-start.13
  45.1 3.4 %load.5.refs_11_ = bf16[576,7168]{1,0:T(8,128)(2,1)S(1)} custom-call(bf16[24,1792]{1,0:T(8,128)(2,1)S(1)} %get-tuple-element.58._.refs_0_, bf16[576,7168]{1,0:T(8,128)(2,1)} %source.1), custom_call_target="tpu_custom_call" | custom-call | bytes 16515072 | tf_op jit(solution)/shard_map/load/pallas_call | solution.py:63
  48.6 2.8 %collective-permute-done.15.refs_3_ = bf16[24,1792]{1,0:T(8,128)(2,1)S(1)} collective-permute-done((bf16[24,1792]{1,0:T(8,128)(2,1)S(1)}, bf16[24,1792]{1,0:T(8,128)(2,1)S(1)}, u32[]{:S(2)}, u32[]{:S(2)}) %collective-permute-start.15) | collective-permute-done | bytes 86048 | tf_op jit(solution)/shard_map/ppermute | solution.py:434
  51.3 0.2 collective-permute-start.19
  51.5 0.4 collective-permute-start.18
  51.9 0.2 collective-permute-start.17
  52.0 0.4 collective-permute-start.20
  52.4 0.3 collective-permute-done.19.refs_7_
  52.6 0.2 collective-permute-done.18.refs_6_
  52.8 0.4 collective-permute-done.17.refs_5_
  53.1 0.2 collective-permute-done.20.refs_8_
  53.3 6.3 %feed_forward.1 = (f32[96,1792]{1,0:T(8,128)S(1)}, bf16[96,1792]{1,0:T(8,128)(2,1)S(1)}) custom-call(bf16[24,1792]{1,0:T(8,128)(2,1)S(1)} %get-tuple-element.58._.refs_0_, bf16[24,1792]{1,0:T(8,128)(2,1)S(1)} %collective-permute-done.13.refs_1_, bf16[24,1792]{1,0:T(8,128)(2,1)S(1)} %collective-permute-done.14.refs_2_, ...), custom_call_target="tpu_custom_call" | custom-call | tf_op jit(solution)/shard_map/feed_forward/pallas_call | solution.py:383
  59.6 0.4 collective-permute-start.21
  60.0 1.3 %collective-permute-done.21.got_ref = bf16[96,1792]{1,0:T(8,128)(2,1)S(1)} collective-permute-done((bf16[96,1792]{1,0:T(8,128)(2,1)S(1)}, bf16[96,1792]{1,0:T(8,128)(2,1)S(1)}, u32[]{:S(2)}, u32[]{:S(2)}) %collective-permute-start.21) | collective-permute-done | bytes 344096 | tf_op jit(solution)/shard_map/ppermute | solution.py:430
  61.3 0.3 add_halves.3
  61.6 1.4 %collective-permute-start.22 = (bf16[24,1792]{1,0:T(8,128)(2,1)S(1)}, bf16[24,1792]{1,0:T(8,128)(2,1)S(1)}, u32[]{:S(2)}, u32[]{:S(2)}) collective-permute-start(bf16[24,1792]{1,0:T(8,128)(2,1)S(1)} %get-tuple-element.66), channel_id=1, source_target_pairs={{0,8},{1,11},{2,10},{3,9},{4,12},{5,15},{6,14},{7,13},{8,0},{9,3},... | collective-permute-start | bytes 258056 | tf_op jit(solution)/shard_map/ppermute | solution.py:434
  63.0 1.5 %collective-permute-start.23 = (bf16[24,1792]{1,0:T(8,128)(2,1)S(1)}, bf16[24,1792]{1,0:T(8,128)(2,1)S(1)}, u32[]{:S(2)}, u32[]{:S(2)}) collective-permute-start(bf16[24,1792]{1,0:T(8,128)(2,1)S(1)} %get-tuple-element.67), channel_id=1, source_target_pairs={{0,12},{1,15},{2,14},{3,13},{4,8},{5,11},{6,10},{7,9},{8,4},{9,7},... | collective-permute-start | bytes 258056 | tf_op jit(solution)/shard_map/ppermute | solution.py:434
  64.5 0.6 collective-permute-start.24
  65.1 0.7 collective-permute-start.25
  65.8 5.4 %collective-permute-done.22.refs_0_ = bf16[24,1792]{1,0:T(8,128)(2,1)S(1)} collective-permute-done((bf16[24,1792]{1,0:T(8,128)(2,1)S(1)}, bf16[24,1792]{1,0:T(8,128)(2,1)S(1)}, u32[]{:S(2)}, u32[]{:S(2)}) %collective-permute-start.22) | collective-permute-done | bytes 86048 | tf_op jit(solution)/shard_map/ppermute | solution.py:434
  71.2 1.7 %collective-permute-done.24.refs_2_ = bf16[24,1792]{1,0:T(8,128)(2,1)S(1)} collective-permute-done((bf16[24,1792]{1,0:T(8,128)(2,1)S(1)}, bf16[24,1792]{1,0:T(8,128)(2,1)S(1)}, u32[]{:S(2)}, u32[]{:S(2)}) %collective-permute-start.24) | collective-permute-done | bytes 86048 | tf_op jit(solution)/shard_map/ppermute | solution.py:434
  72.9 0.1 sum_units.3.mine_ref
  73.0 0.4 collective-permute-start.26
  73.4 1.1 %collective-permute-done.26.twin_ref = f32[24,1792]{1,0:T(8,128)S(1)} collective-permute-done((f32[24,1792]{1,0:T(8,128)S(1)}, f32[24,1792]{1,0:T(8,128)S(1)}, u32[]{:S(2)}, u32[]{:S(2)}) %collective-permute-start.26) | collective-permute-done | bytes 172064 | tf_op jit(solution)/shard_map/ppermute | solution.py:430
  74.5 0.9 %final_rows.1 = bf16[3,7168]{1,0:T(4,128)(2,1)} custom-call(f32[24,128]{1,0:T(8,128)S(1)} %get-tuple-element.37.live_ref, f32[24,1792]{1,0:T(8,128)S(1)} %sum_units.3.mine_ref, f32[24,1792]{1,0:T(8,128)S(1)} %collective-permute-done.26.twin_ref), custom_call_target="tpu_custom_call" | custom-call | tf_op jit(solution)/shard_map/final_rows/pallas_call | solution.py:410
  (18 shorter events, 0.1 us)
Async XLA Ops:
  5.2 11.4 %collective-permute-start = (bf16[6,8,512]{2,1,0:T(8,128)(2,1)S(1)}, bf16[6,8,512]{2,1,0:T(8,128)(2,1)S(1)}, u32[]{:S(2)}, u32[]{:S(2)}) collective-permute-start(bf16[6,8,512]{2,1,0:T(8,128)(2,1)S(1)} %get-tuple-element.38), channel_id=1, source_target_pairs={{0,12},{2,14},{4,8},{6,10},{8,4},{10,6},{12,0},{14,2},{1,13},{3,15... | collective-permute-start | bytes 147464 | tf_op jit(solution)/shard_map/ppermute | solution.py:427
  10.3 6.3 %collective-permute-start.1 = (bf16[6,8,512]{2,1,0:T(8,128)(2,1)S(1)}, bf16[6,8,512]{2,1,0:T(8,128)(2,1)S(1)}, u32[]{:S(2)}, u32[]{:S(2)}) collective-permute-start(bf16[6,8,512]{2,1,0:T(8,128)(2,1)S(1)} %get-tuple-element.39), channel_id=1, source_target_pairs={{0,8},{2,10},{4,12},{6,14},{8,0},{10,2},{12,4},{14,6},{1,9},{3,11}... | collective-permute-start | bytes 147464 | tf_op jit(solution)/shard_map/ppermute | solution.py:427
  10.3 11.2 %collective-permute-start.2 = (bf16[6,8,512]{2,1,0:T(8,128)(2,1)S(1)}, bf16[6,8,512]{2,1,0:T(8,128)(2,1)S(1)}, u32[]{:S(2)}, u32[]{:S(2)}) collective-permute-start(bf16[6,8,512]{2,1,0:T(8,128)(2,1)S(1)} %get-tuple-element.40), channel_id=1, source_target_pairs={{0,14},{2,12},{4,10},{6,8},{8,6},{10,4},{12,2},{14,0},{1,15},{3,13... | collective-permute-start | bytes 147464 | tf_op jit(solution)/shard_map/ppermute | solution.py:427
  13.2 8.3 %collective-permute-start.3 = (bf16[6,8,512]{2,1,0:T(8,128)(2,1)S(1)}, bf16[6,8,512]{2,1,0:T(8,128)(2,1)S(1)}, u32[]{:S(2)}, u32[]{:S(2)}) collective-permute-start(bf16[6,8,512]{2,1,0:T(8,128)(2,1)S(1)} %get-tuple-element.41), channel_id=1, source_target_pairs={{0,10},{2,8},{4,14},{6,12},{8,2},{10,0},{12,6},{14,4},{1,11},{3,9}... | collective-permute-start | bytes 147464 | tf_op jit(solution)/shard_map/ppermute | solution.py:427
  14.2 7.3 %collective-permute-start.4 = (bf16[6,8,512]{2,1,0:T(8,128)(2,1)S(1)}, bf16[6,8,512]{2,1,0:T(8,128)(2,1)S(1)}, u32[]{:S(2)}, u32[]{:S(2)}) collective-permute-start(bf16[6,8,512]{2,1,0:T(8,128)(2,1)S(1)} %get-tuple-element.42), channel_id=1, source_target_pairs={{0,6},{2,4},{4,2},{6,0},{8,14},{10,12},{12,10},{14,8},{1,7},{3,5},... | collective-permute-start | bytes 147464 | tf_op jit(solution)/shard_map/ppermute | solution.py:427
  16.6 5.0 %collective-permute-start.5 = (bf16[6,8,512]{2,1,0:T(8,128)(2,1)S(1)}, bf16[6,8,512]{2,1,0:T(8,128)(2,1)S(1)}, u32[]{:S(2)}, u32[]{:S(2)}) collective-permute-start(bf16[6,8,512]{2,1,0:T(8,128)(2,1)S(1)} %get-tuple-element.43), channel_id=1, source_target_pairs={{0,4},{2,6},{4,0},{6,2},{8,12},{10,14},{12,8},{14,10},{1,5},{3,7},... | collective-permute-start | bytes 147464 | tf_op jit(solution)/shard_map/ppermute | solution.py:427
  16.6 5.0 %collective-permute-start.6 = (bf16[6,8,512]{2,1,0:T(8,128)(2,1)S(1)}, bf16[6,8,512]{2,1,0:T(8,128)(2,1)S(1)}, u32[]{:S(2)}, u32[]{:S(2)}) collective-permute-start(bf16[6,8,512]{2,1,0:T(8,128)(2,1)S(1)} %get-tuple-element.44), channel_id=1, source_target_pairs={{0,2},{2,0},{4,6},{6,4},{8,10},{10,8},{12,14},{14,12},{1,3},{3,1},... | collective-permute-start | bytes 147464 | tf_op jit(solution)/shard_map/ppermute | solution.py:427
  25.0 1.7 %collective-permute-start.7 = (bf16[96,1792]{1,0:T(8,128)(2,1)S(1)}, bf16[96,1792]{1,0:T(8,128)(2,1)S(1)}, u32[]{:S(2)}, u32[]{:S(2)}) collective-permute-start(bf16[96,1792]{1,0:T(8,128)(2,1)S(1)} %get-tuple-element.50), channel_id=1, source_target_pairs={{0,1},{1,0},{2,3},{3,2},{4,5},{5,4},{6,7},{7,6},{8,9},{9,8},{10,11... | collective-permute-start | bytes 1032200 | tf_op jit(solution)/shard_map/ppermute | solution.py:430
  27.0 9.6 %collective-permute-start.8 = (bf16[24,1792]{1,0:T(8,128)(2,1)S(1)}, bf16[24,1792]{1,0:T(8,128)(2,1)S(1)}, u32[]{:S(2)}, u32[]{:S(2)}) collective-permute-start(bf16[24,1792]{1,0:T(8,128)(2,1)S(1)} %get-tuple-element.54), channel_id=1, source_target_pairs={{0,8},{1,11},{2,10},{3,9},{4,12},{5,15},{6,14},{7,13},{8,0},{9,3},... | collective-permute-start | bytes 258056 | tf_op jit(solution)/shard_map/ppermute | solution.py:434
  28.6 7.9 %collective-permute-start.9 = (bf16[24,1792]{1,0:T(8,128)(2,1)S(1)}, bf16[24,1792]{1,0:T(8,128)(2,1)S(1)}, u32[]{:S(2)}, u32[]{:S(2)}) collective-permute-start(bf16[24,1792]{1,0:T(8,128)(2,1)S(1)} %get-tuple-element.55), channel_id=1, source_target_pairs={{0,12},{1,15},{2,14},{3,13},{4,8},{5,11},{6,10},{7,9},{8,4},{9,7},... | collective-permute-start | bytes 258056 | tf_op jit(solution)/shard_map/ppermute | solution.py:434
  30.7 7.4 %collective-permute-start.10 = (bf16[24,1792]{1,0:T(8,128)(2,1)S(1)}, bf16[24,1792]{1,0:T(8,128)(2,1)S(1)}, u32[]{:S(2)}, u32[]{:S(2)}) collective-permute-start(bf16[24,1792]{1,0:T(8,128)(2,1)S(1)} %get-tuple-element.56), channel_id=1, source_target_pairs={{0,4},{1,7},{2,6},{3,5},{4,0},{5,3},{6,2},{7,1},{8,12},{9,15},{10,... | collective-permute-start | bytes 258056 | tf_op jit(solution)/shard_map/ppermute | solution.py:434
  31.1 6.9 %collective-permute-start.11 = (bf16[24,1792]{1,0:T(8,128)(2,1)S(1)}, bf16[24,1792]{1,0:T(8,128)(2,1)S(1)}, u32[]{:S(2)}, u32[]{:S(2)}) collective-permute-start(bf16[24,1792]{1,0:T(8,128)(2,1)S(1)} %get-tuple-element.52._.own_ref), channel_id=1, source_target_pairs={{1,3},{3,1},{5,7},{7,5},{9,11},{11,9},{13,15},{15,13},{17,19},{19,... | collective-permute-start | bytes 258056 | tf_op jit(solution)/shard_map/ppermute | solution.py:434
  38.1 1.7 %collective-permute-start.12 = (f32[24,1792]{1,0:T(8,128)S(1)}, f32[24,1792]{1,0:T(8,128)S(1)}, u32[]{:S(2)}, u32[]{:S(2)}) collective-permute-start(f32[24,1792]{1,0:T(8,128)S(1)} %sum_units.2.mine_ref), channel_id=1, source_target_pairs={{0,1},{1,0},{2,3},{3,2},{4,5},{5,4},{6,7},{7,6},{8,9},{9,8},{10,11... | collective-permute-start | bytes 516104 | tf_op jit(solution)/shard_map/ppermute | solution.py:430
  40.0 8.6 %collective-permute-start.16 = (bf16[24,1792]{1,0:T(8,128)(2,1)S(1)}, bf16[24,1792]{1,0:T(8,128)(2,1)S(1)}, u32[]{:S(2)}, u32[]{:S(2)}) collective-permute-start(bf16[24,1792]{1,0:T(8,128)(2,1)S(1)} %get-tuple-element.58._.refs_0_), channel_id=1, source_target_pairs={{0,12},{1,15},{2,14},{3,13},{4,8},{5,11},{6,10},{7,9},{8,4},{9,7},... | collective-permute-start | bytes 258056 | tf_op jit(solution)/shard_map/ppermute | solution.py:434
  43.1 8.3 %collective-permute-start.15 = (bf16[24,1792]{1,0:T(8,128)(2,1)S(1)}, bf16[24,1792]{1,0:T(8,128)(2,1)S(1)}, u32[]{:S(2)}, u32[]{:S(2)}) collective-permute-start(bf16[24,1792]{1,0:T(8,128)(2,1)S(1)} %get-tuple-element.58._.refs_0_), channel_id=1, source_target_pairs={{0,8},{1,11},{2,10},{3,9},{4,12},{5,15},{6,14},{7,13},{8,0},{9,3},... | collective-permute-start | bytes 258056 | tf_op jit(solution)/shard_map/ppermute | solution.py:434
  43.1 8.4 %collective-permute-start.14 = (bf16[24,1792]{1,0:T(8,128)(2,1)S(1)}, bf16[24,1792]{1,0:T(8,128)(2,1)S(1)}, u32[]{:S(2)}, u32[]{:S(2)}) collective-permute-start(bf16[24,1792]{1,0:T(8,128)(2,1)S(1)} %get-tuple-element.58._.refs_0_), channel_id=1, source_target_pairs={{0,4},{1,7},{2,6},{3,5},{4,0},{5,3},{6,2},{7,1},{8,12},{9,15},{10,... | collective-permute-start | bytes 258056 | tf_op jit(solution)/shard_map/ppermute | solution.py:434
  44.5 7.4 %collective-permute-start.13 = (bf16[24,1792]{1,0:T(8,128)(2,1)S(1)}, bf16[24,1792]{1,0:T(8,128)(2,1)S(1)}, u32[]{:S(2)}, u32[]{:S(2)}) collective-permute-start(bf16[24,1792]{1,0:T(8,128)(2,1)S(1)} %get-tuple-element.58._.refs_0_), channel_id=1, source_target_pairs={{1,3},{3,1},{5,7},{7,5},{9,11},{11,9},{13,15},{15,13},{17,19},{19,... | collective-permute-start | bytes 258056 | tf_op jit(solution)/shard_map/ppermute | solution.py:434
  51.3 1.3 %collective-permute-start.19 = (bf16[24,1792]{1,0:T(8,128)(2,1)S(1)}, bf16[24,1792]{1,0:T(8,128)(2,1)S(1)}, u32[]{:S(2)}, u32[]{:S(2)}) collective-permute-start(bf16[24,1792]{1,0:T(8,128)(2,1)S(1)} %collective-permute-done.15.refs_3_), channel_id=1, source_target_pairs={{0,1},{1,0},{2,3},{3,2},{4,5},{5,4},{6,7},{7,6},{8,9},{9,8},{10,11... | collective-permute-start | bytes 258056 | tf_op jit(solution)/shard_map/ppermute | solution.py:430
  51.5 1.3 %collective-permute-start.18 = (bf16[24,1792]{1,0:T(8,128)(2,1)S(1)}, bf16[24,1792]{1,0:T(8,128)(2,1)S(1)}, u32[]{:S(2)}, u32[]{:S(2)}) collective-permute-start(bf16[24,1792]{1,0:T(8,128)(2,1)S(1)} %collective-permute-done.14.refs_2_), channel_id=1, source_target_pairs={{0,1},{1,0},{2,3},{3,2},{4,5},{5,4},{6,7},{7,6},{8,9},{9,8},{10,11... | collective-permute-start | bytes 258056 | tf_op jit(solution)/shard_map/ppermute | solution.py:430
  51.9 1.3 %collective-permute-start.17 = (bf16[24,1792]{1,0:T(8,128)(2,1)S(1)}, bf16[24,1792]{1,0:T(8,128)(2,1)S(1)}, u32[]{:S(2)}, u32[]{:S(2)}) collective-permute-start(bf16[24,1792]{1,0:T(8,128)(2,1)S(1)} %collective-permute-done.13.refs_1_), channel_id=1, source_target_pairs={{0,1},{1,0},{2,3},{3,2},{4,5},{5,4},{6,7},{7,6},{8,9},{9,8},{10,11... | collective-permute-start | bytes 258056 | tf_op jit(solution)/shard_map/ppermute | solution.py:430
  52.0 1.3 %collective-permute-start.20 = (bf16[24,1792]{1,0:T(8,128)(2,1)S(1)}, bf16[24,1792]{1,0:T(8,128)(2,1)S(1)}, u32[]{:S(2)}, u32[]{:S(2)}) collective-permute-start(bf16[24,1792]{1,0:T(8,128)(2,1)S(1)} %collective-permute-done.16.refs_4_), channel_id=1, source_target_pairs={{0,1},{1,0},{2,3},{3,2},{4,5},{5,4},{6,7},{7,6},{8,9},{9,8},{10,11... | collective-permute-start | bytes 258056 | tf_op jit(solution)/shard_map/ppermute | solution.py:430
  59.6 1.7 %collective-permute-start.21 = (bf16[96,1792]{1,0:T(8,128)(2,1)S(1)}, bf16[96,1792]{1,0:T(8,128)(2,1)S(1)}, u32[]{:S(2)}, u32[]{:S(2)}) collective-permute-start(bf16[96,1792]{1,0:T(8,128)(2,1)S(1)} %get-tuple-element.63), channel_id=1, source_target_pairs={{0,1},{1,0},{2,3},{3,2},{4,5},{5,4},{6,7},{7,6},{8,9},{9,8},{10,11... | collective-permute-start | bytes 1032200 | tf_op jit(solution)/shard_map/ppermute | solution.py:430
  61.6 9.6 %collective-permute-start.22 = (bf16[24,1792]{1,0:T(8,128)(2,1)S(1)}, bf16[24,1792]{1,0:T(8,128)(2,1)S(1)}, u32[]{:S(2)}, u32[]{:S(2)}) collective-permute-start(bf16[24,1792]{1,0:T(8,128)(2,1)S(1)} %get-tuple-element.66), channel_id=1, source_target_pairs={{0,8},{1,11},{2,10},{3,9},{4,12},{5,15},{6,14},{7,13},{8,0},{9,3},... | collective-permute-start | bytes 258056 | tf_op jit(solution)/shard_map/ppermute | solution.py:434
  63.0 8.2 %collective-permute-start.23 = (bf16[24,1792]{1,0:T(8,128)(2,1)S(1)}, bf16[24,1792]{1,0:T(8,128)(2,1)S(1)}, u32[]{:S(2)}, u32[]{:S(2)}) collective-permute-start(bf16[24,1792]{1,0:T(8,128)(2,1)S(1)} %get-tuple-element.67), channel_id=1, source_target_pairs={{0,12},{1,15},{2,14},{3,13},{4,8},{5,11},{6,10},{7,9},{8,4},{9,7},... | collective-permute-start | bytes 258056 | tf_op jit(solution)/shard_map/ppermute | solution.py:434
  64.5 8.4 %collective-permute-start.24 = (bf16[24,1792]{1,0:T(8,128)(2,1)S(1)}, bf16[24,1792]{1,0:T(8,128)(2,1)S(1)}, u32[]{:S(2)}, u32[]{:S(2)}) collective-permute-start(bf16[24,1792]{1,0:T(8,128)(2,1)S(1)} %get-tuple-element.68), channel_id=1, source_target_pairs={{0,4},{1,7},{2,6},{3,5},{4,0},{5,3},{6,2},{7,1},{8,12},{9,15},{10,... | collective-permute-start | bytes 258056 | tf_op jit(solution)/shard_map/ppermute | solution.py:434
  65.1 7.8 %collective-permute-start.25 = (bf16[24,1792]{1,0:T(8,128)(2,1)S(1)}, bf16[24,1792]{1,0:T(8,128)(2,1)S(1)}, u32[]{:S(2)}, u32[]{:S(2)}) collective-permute-start(bf16[24,1792]{1,0:T(8,128)(2,1)S(1)} %get-tuple-element.64.own_ref), channel_id=1, source_target_pairs={{1,3},{3,1},{5,7},{7,5},{9,11},{11,9},{13,15},{15,13},{17,19},{19,... | collective-permute-start | bytes 258056 | tf_op jit(solution)/shard_map/ppermute | solution.py:434
  73.0 1.5 %collective-permute-start.26 = (f32[24,1792]{1,0:T(8,128)S(1)}, f32[24,1792]{1,0:T(8,128)S(1)}, u32[]{:S(2)}, u32[]{:S(2)}) collective-permute-start(f32[24,1792]{1,0:T(8,128)S(1)} %sum_units.3.mine_ref), channel_id=1, source_target_pairs={{0,1},{1,0},{2,3},{3,2},{4,5},{5,4},{6,7},{7,6},{8,9},{9,8},{10,11... | collective-permute-start | bytes 516104 | tf_op jit(solution)/shard_map/ppermute | solution.py:430

commit v5 on v4

--- a/solution.py
+++ b/solution.py
@@ -204,7 +204,7 @@
 
 
 def set_order(half):
-    return [*range(half // 2, half), *reversed(range(half // 2))]
+    return [*reversed(range(half))]
 
 
 def project_kernel(n_dp, slots, *refs):
@@ -297,21 +297,22 @@
 
 
 def sum_kernel(n_units, own_ref, base_ref, *refs):
-    got, out_ref = refs[:n_units], refs[-1]
+    got, (out_ref, give_ref) = refs[:n_units], refs[-2:]
     me_head = lax.axis_index("head")
     zeroth = set_order(n_units).index(0)
     total = base_ref[...] + jnp.where(me_head == 0, own_ref[...], got[zeroth][...]).astype(f32)
     for ref in got[:zeroth] + got[zeroth + 1 :]:
         total = total + ref[...].astype(f32)
     out_ref[...] = total
-
-
-def sum_units(own, base, got, after):
+    give_ref[...] = total.astype(give_ref.dtype)
+
+
+def sum_units(own, base, got, after, sent):
     return pl.pallas_call(
         functools.partial(sum_kernel, len(got)),
-        out_shape=jax.ShapeDtypeStruct(own.shape, f32),
+        out_shape=[jax.ShapeDtypeStruct(own.shape, f32), jax.ShapeDtypeStruct(own.shape, sent)],
         in_specs=vmem(2 + len(got)) + [pl.BlockSpec(memory_space=pl.ANY)] * len(after),
-        out_specs=vmem(1)[0],
+        out_specs=vmem(2),
         compiler_params=params(4),
         name="sum_units",
     )(own, base, *got, *after)
@@ -393,7 +394,7 @@
 
 def final_kernel(slots, owner_rows, live_ref, mine_ref, twin_ref, out_ref):
     me_head = lax.axis_index("head")
-    total = mine_ref[...] + twin_ref[...]
+    total = mine_ref[...] + twin_ref[...].astype(f32)
     rows = total.shape[0]
     total = jnp.where(live_ref[:, :1] > 0.5, total, 0.0).astype(bf16)
     part = total.shape[1]
@@ -441,8 +442,8 @@
         units = add_halves(half, keep, to_twin(give), to_units)
         weights = [load(units[0], w) for w in weights]
         got = [to_set(units[s], s) for s in set_order(half)]
-        mine = sum_units(units[0], base, got, weights)
-        return mine, to_twin(mine), weights
+        mine, give = sum_units(units[0], base, got, weights, f32 if weights else bf16)
+        return mine, to_twin(give), weights
 
     gate = load(blocks[0], gate_weight.T)
     blocks = [to_peer(blocks[k], k) if k else blocks[0] for k in block_order(n_dp)]

time: 75.5 us -> 75.3 us (level)
    ppermute x8, starting transfers between devices: 2.62 us -> 1.79 us  [to_twin(): return lax.ppermute(x, 'head', [(0, 1), (1, 0)])]
  transfers between devices with their start and end apart: 27 -> 27, of which waited for: 13 -> 12; matrix products, arithmetic and copies ran while one was open for 0% -> 0% of each run, Pallas kernels for 14% -> 14%
where the time goes in v5:
time: 75.3 us; the launch traced here: 75.2 us
  starting transfers between devices  29.1 us (39%)
  Pallas kernels  26.9 us (36%)
  waiting for transfers between devices  19 us (25%)
    ppermute x12, starting transfers between devices, to_set(): return lax.ppermute(x, ('dp', 'head'), pairs)  14.4 us
    ppermute x7, starting transfers between devices, to_peer(): return lax.ppermute(x, 'dp', [(i, i ^ k) for i in range(n_dp)])  12.9 us
    ppermute x12, waiting for transfers between devices, to_set(): return lax.ppermute(x, ('dp', 'head'), pairs)  12.4 us
    pallas_call x3, Pallas kernels, load(): pl.pallas_call(load_kernel, out_shape=jax.ShapeDtypeStruct(weight.shape,...  10.3 us
    ppermute x8, waiting for transfers between devices, to_twin(): return lax.ppermute(x, 'head', [(0, 1), (1, 0)])  6.63 us
    pallas_call x1, Pallas kernels, feed_forward(): pl.pallas_call(functools.partial(ffn_kernel, n_dp, slots), out_shape=[out...  6.3 us
    pallas_call x1, Pallas kernels, attend(): pl.pallas_call(functools.partial(attention_kernel, n_dp), out_shape=[bloc...  5.18 us
    pallas_call x1, Pallas kernels, project(): pl.pallas_call(functools.partial(project_kernel, n_dp, slots), out_shape=...  3.43 us
  transfers between devices with their start and end apart: 27, of which 12 were waited for; matrix products, arithmetic and copies ran while one was open for 0% of the time, Pallas kernels for 14%

profile of v5, /device:TPU:0, one launch (start us, length us, event | category | flops | bytes accessed | tf_op | source)
XLA Modules:
  0.0 75.2 jit_solution(6034975663279002406)
XLA Ops:
  0.0 5.2 %attend.1 = (bf16[6,8,512]{2,1,0:T(8,128)(2,1)S(1)}, bf16[6,8,512]{2,1,0:T(8,128)(2,1)S(1)}, bf16[6,8,512]{2,1,0:T(8,128)(2,1)S(1)}, bf16[6,8,512]{2,1,0:T(8,128...) custom-call(s32[8]{0:T(128)} %counts_hbm.1, ...), custom_call_target="tpu_custom_call" | custom-call | tf_op jit(solution)/shard_map/attend/pallas_call | solution.py:157
  5.2 5.1 %collective-permute-start = (bf16[6,8,512]{2,1,0:T(8,128)(2,1)S(1)}, bf16[6,8,512]{2,1,0:T(8,128)(2,1)S(1)}, u32[]{:S(2)}, u32[]{:S(2)}) collective-permute-start(bf16[6,8,512]{2,1,0:T(8,128)(2,1)S(1)} %get-tuple-element.42), channel_id=1, source_target_pairs={{0,12},{2,14},{4,8},{6,10},{8,4},{10,6},{12,0},{14,2},{1,13},{3,15... | collective-permute-start | bytes 147464 | tf_op jit(solution)/shard_map/ppermute | solution.py:428
  10.3 2.9 %collective-permute-start.2 = (bf16[6,8,512]{2,1,0:T(8,128)(2,1)S(1)}, bf16[6,8,512]{2,1,0:T(8,128)(2,1)S(1)}, u32[]{:S(2)}, u32[]{:S(2)}) collective-permute-start(bf16[6,8,512]{2,1,0:T(8,128)(2,1)S(1)} %get-tuple-element.44), channel_id=1, source_target_pairs={{0,14},{2,12},{4,10},{6,8},{8,6},{10,4},{12,2},{14,0},{1,15},{3,13... | collective-permute-start | bytes 147464 | tf_op jit(solution)/shard_map/ppermute | solution.py:428
  13.2 1.0 %collective-permute-start.3 = (bf16[6,8,512]{2,1,0:T(8,128)(2,1)S(1)}, bf16[6,8,512]{2,1,0:T(8,128)(2,1)S(1)}, u32[]{:S(2)}, u32[]{:S(2)}) collective-permute-start(bf16[6,8,512]{2,1,0:T(8,128)(2,1)S(1)} %get-tuple-element.45), channel_id=1, source_target_pairs={{0,10},{2,8},{4,14},{6,12},{8,2},{10,0},{12,6},{14,4},{1,11},{3,9}... | collective-permute-start | bytes 147464 | tf_op jit(solution)/shard_map/ppermute | solution.py:428
  14.2 2.4 %collective-permute-start.4 = (bf16[6,8,512]{2,1,0:T(8,128)(2,1)S(1)}, bf16[6,8,512]{2,1,0:T(8,128)(2,1)S(1)}, u32[]{:S(2)}, u32[]{:S(2)}) collective-permute-start(bf16[6,8,512]{2,1,0:T(8,128)(2,1)S(1)} %get-tuple-element.46), channel_id=1, source_target_pairs={{0,6},{2,4},{4,2},{6,0},{8,14},{10,12},{12,10},{14,8},{1,7},{3,5},... | collective-permute-start | bytes 147464 | tf_op jit(solution)/shard_map/ppermute | solution.py:428
  16.6 1.5 %collective-permute-start.6 = (bf16[6,8,512]{2,1,0:T(8,128)(2,1)S(1)}, bf16[6,8,512]{2,1,0:T(8,128)(2,1)S(1)}, u32[]{:S(2)}, u32[]{:S(2)}) collective-permute-start(bf16[6,8,512]{2,1,0:T(8,128)(2,1)S(1)} %get-tuple-element.48), channel_id=1, source_target_pairs={{0,2},{2,0},{4,6},{6,4},{8,10},{10,8},{12,14},{14,12},{1,3},{3,1},... | collective-permute-start | bytes 147464 | tf_op jit(solution)/shard_map/ppermute | solution.py:428
  18.1 3.4 %load.3.refs_12_.refs_9_ = bf16[576,7168]{1,0:T(8,128)(2,1)S(1)} custom-call(bf16[6,8,512]{2,1,0:T(8,128)(2,1)S(1)} %get-tuple-element.49._.refs_7_, bf16[576,7168]{1,0:T(8,128)(2,1)} %bitcast.6), custom_call_target="tpu_custom_call" | custom-call | bytes 16515072 | tf_op jit(solution)/shard_map/load/pallas_call | solution.py:63
  21.6 3.4 %project.1 = (f32[96,1792]{1,0:T(8,128)S(1)}, bf16[96,1792]{1,0:T(8,128)(2,1)S(1)}) custom-call(bf16[6,8,512]{2,1,0:T(8,128)(2,1)S(1)} %collective-permute-done.refs_0_, bf16[6,8,512]{2,1,0:T(8,128)(2,1)S(1)} %collective-permute-done.1.refs_1_, bf16[6,8,512]{2,1,0:T(8,128)(2,1)S(1)} %collective-permute-done.2.refs_2_, ...), custom_call_target="tpu_custom_call" | custom-call | tf_op jit(solution)/shard_map/project/pallas_call | solution.py:263
  25.0 0.1 collective-permute-start.7
  25.1 1.6 %collective-permute-done.7.got_ref = bf16[96,1792]{1,0:T(8,128)(2,1)S(1)} collective-permute-done((bf16[96,1792]{1,0:T(8,128)(2,1)S(1)}, bf16[96,1792]{1,0:T(8,128)(2,1)S(1)}, u32[]{:S(2)}, u32[]{:S(2)}) %collective-permute-start.7) | collective-permute-done | bytes 344096 | tf_op jit(solution)/shard_map/ppermute | solution.py:431
  26.7 0.2 add_halves.2
  27.0 3.6 %collective-permute-start.8 = (bf16[24,1792]{1,0:T(8,128)(2,1)S(1)}, bf16[24,1792]{1,0:T(8,128)(2,1)S(1)}, u32[]{:S(2)}, u32[]{:S(2)}) collective-permute-start(bf16[24,1792]{1,0:T(8,128)(2,1)S(1)} %get-tuple-element.58), channel_id=1, source_target_pairs={{0,12},{1,15},{2,14},{3,13},{4,8},{5,11},{6,10},{7,9},{8,4},{9,7},... | collective-permute-start | bytes 258056 | tf_op jit(solution)/shard_map/ppermute | solution.py:435
  30.6 0.8 %collective-permute-start.10 = (bf16[24,1792]{1,0:T(8,128)(2,1)S(1)}, bf16[24,1792]{1,0:T(8,128)(2,1)S(1)}, u32[]{:S(2)}, u32[]{:S(2)}) collective-permute-start(bf16[24,1792]{1,0:T(8,128)(2,1)S(1)} %get-tuple-element.60), channel_id=1, source_target_pairs={{0,4},{1,7},{2,6},{3,5},{4,0},{5,3},{6,2},{7,1},{8,12},{9,15},{10,... | collective-permute-start | bytes 258056 | tf_op jit(solution)/shard_map/ppermute | solution.py:435
  31.4 0.7 collective-permute-start.11
  32.1 3.4 %load.4.refs_4_.refs_10_ = bf16[576,7168]{1,0:T(8,128)(2,1)S(1)} custom-call(bf16[24,1792]{1,0:T(8,128)(2,1)S(1)} %get-tuple-element.56._.own_ref, bf16[576,7168]{1,0:T(8,128)(2,1)} %bitcast.7), custom_call_target="tpu_custom_call" | custom-call | bytes 16515072 | tf_op jit(solution)/shard_map/load/pallas_call | solution.py:63
  35.5 2.9 %collective-permute-done.9.refs_1_ = bf16[24,1792]{1,0:T(8,128)(2,1)S(1)} collective-permute-done((bf16[24,1792]{1,0:T(8,128)(2,1)S(1)}, bf16[24,1792]{1,0:T(8,128)(2,1)S(1)}, u32[]{:S(2)}, u32[]{:S(2)}) %collective-permute-start.9) | collective-permute-done | bytes 86048 | tf_op jit(solution)/shard_map/ppermute | solution.py:435
  38.5 0.1 sum_units.2
  38.6 0.1 collective-permute-start.12
  38.6 1.4 %collective-permute-done.12.twin_ref = f32[24,1792]{1,0:T(8,128)S(1)} collective-permute-done((f32[24,1792]{1,0:T(8,128)S(1)}, f32[24,1792]{1,0:T(8,128)S(1)}, u32[]{:S(2)}, u32[]{:S(2)}) %collective-permute-start.12) | collective-permute-done | bytes 172064 | tf_op jit(solution)/shard_map/ppermute | solution.py:431
  40.0 0.1 norm_rows.1
  40.2 1.0 %collective-permute-start.15 = (bf16[24,1792]{1,0:T(8,128)(2,1)S(1)}, bf16[24,1792]{1,0:T(8,128)(2,1)S(1)}, u32[]{:S(2)}, u32[]{:S(2)}) collective-permute-start(bf16[24,1792]{1,0:T(8,128)(2,1)S(1)} %get-tuple-element.64._.refs_0_), channel_id=1, source_target_pairs={{0,8},{1,11},{2,10},{3,9},{4,12},{5,15},{6,14},{7,13},{8,0},{9,3},... | collective-permute-start | bytes 258056 | tf_op jit(solution)/shard_map/ppermute | solution.py:435
  41.2 2.1 %collective-permute-start.16 = (bf16[24,1792]{1,0:T(8,128)(2,1)S(1)}, bf16[24,1792]{1,0:T(8,128)(2,1)S(1)}, u32[]{:S(2)}, u32[]{:S(2)}) collective-permute-start(bf16[24,1792]{1,0:T(8,128)(2,1)S(1)} %get-tuple-element.64._.refs_0_), channel_id=1, source_target_pairs={{0,12},{1,15},{2,14},{3,13},{4,8},{5,11},{6,10},{7,9},{8,4},{9,7},... | collective-permute-start | bytes 258056 | tf_op jit(solution)/shard_map/ppermute | solution.py:435
  43.3 0.4 collective-permute-start.14
  43.7 0.7 collective-permute-start.13
  44.4 3.4 %load.5.refs_11_ = bf16[576,7168]{1,0:T(8,128)(2,1)S(1)} custom-call(bf16[24,1792]{1,0:T(8,128)(2,1)S(1)} %get-tuple-element.64._.refs_0_, bf16[576,7168]{1,0:T(8,128)(2,1)} %source.1), custom_call_target="tpu_custom_call" | custom-call | bytes 16515072 | tf_op jit(solution)/shard_map/load/pallas_call | solution.py:63
  47.8 2.3 %collective-permute-done.15.refs_3_ = bf16[24,1792]{1,0:T(8,128)(2,1)S(1)} collective-permute-done((bf16[24,1792]{1,0:T(8,128)(2,1)S(1)}, bf16[24,1792]{1,0:T(8,128)(2,1)S(1)}, u32[]{:S(2)}, u32[]{:S(2)}) %collective-permute-start.15) | collective-permute-done | bytes 86048 | tf_op jit(solution)/shard_map/ppermute | solution.py:435
  50.2 0.4 collective-permute-start.20
  50.6 1.3 %collective-permute-done.14.refs_2_ = bf16[24,1792]{1,0:T(8,128)(2,1)S(1)} collective-permute-done((bf16[24,1792]{1,0:T(8,128)(2,1)S(1)}, bf16[24,1792]{1,0:T(8,128)(2,1)S(1)}, u32[]{:S(2)}, u32[]{:S(2)}) %collective-permute-start.14) | collective-permute-done | bytes 86048 | tf_op jit(solution)/shard_map/ppermute | solution.py:435
  51.9 0.1 collective-permute-start.18
  52.0 0.4 collective-permute-start.17
  52.4 0.1 collective-permute-start.19
  52.5 0.7 collective-permute-done.18.refs_6_
  53.2 0.2 collective-permute-done.17.refs_5_
  53.3 0.4 collective-permute-done.19.refs_7_
  53.7 6.3 %feed_forward.1 = (f32[96,1792]{1,0:T(8,128)S(1)}, bf16[96,1792]{1,0:T(8,128)(2,1)S(1)}) custom-call(bf16[24,1792]{1,0:T(8,128)(2,1)S(1)} %get-tuple-element.64._.refs_0_, bf16[24,1792]{1,0:T(8,128)(2,1)S(1)} %collective-permute-done.13.refs_1_, bf16[24,1792]{1,0:T(8,128)(2,1)S(1)} %collective-permute-done.14.refs_2_, ...), custom_call_target="tpu_custom_call" | custom-call | tf_op jit(solution)/shard_map/feed_forward/pallas_call | solution.py:384
  60.0 0.2 collective-permute-start.21
  60.2 1.5 %collective-permute-done.21.got_ref = bf16[96,1792]{1,0:T(8,128)(2,1)S(1)} collective-permute-done((bf16[96,1792]{1,0:T(8,128)(2,1)S(1)}, bf16[96,1792]{1,0:T(8,128)(2,1)S(1)}, u32[]{:S(2)}, u32[]{:S(2)}) %collective-permute-start.21) | collective-permute-done | bytes 344096 | tf_op jit(solution)/shard_map/ppermute | solution.py:431
  61.7 0.3 add_halves.3
  62.0 2.1 %collective-permute-start.22 = (bf16[24,1792]{1,0:T(8,128)(2,1)S(1)}, bf16[24,1792]{1,0:T(8,128)(2,1)S(1)}, u32[]{:S(2)}, u32[]{:S(2)}) collective-permute-start(bf16[24,1792]{1,0:T(8,128)(2,1)S(1)} %get-tuple-element.72), channel_id=1, source_target_pairs={{0,12},{1,15},{2,14},{3,13},{4,8},{5,11},{6,10},{7,9},{8,4},{9,7},... | collective-permute-start | bytes 258056 | tf_op jit(solution)/shard_map/ppermute | solution.py:435
  64.1 0.2 collective-permute-start.23
  64.2 2.2 %collective-permute-start.24 = (bf16[24,1792]{1,0:T(8,128)(2,1)S(1)}, bf16[24,1792]{1,0:T(8,128)(2,1)S(1)}, u32[]{:S(2)}, u32[]{:S(2)}) collective-permute-start(bf16[24,1792]{1,0:T(8,128)(2,1)S(1)} %get-tuple-element.74), channel_id=1, source_target_pairs={{0,4},{1,7},{2,6},{3,5},{4,0},{5,3},{6,2},{7,1},{8,12},{9,15},{10,... | collective-permute-start | bytes 258056 | tf_op jit(solution)/shard_map/ppermute | solution.py:435
  66.4 0.7 collective-permute-start.25
  67.1 2.2 %collective-permute-done.22.refs_0_ = bf16[24,1792]{1,0:T(8,128)(2,1)S(1)} collective-permute-done((bf16[24,1792]{1,0:T(8,128)(2,1)S(1)}, bf16[24,1792]{1,0:T(8,128)(2,1)S(1)}, u32[]{:S(2)}, u32[]{:S(2)}) %collective-permute-start.22) | collective-permute-done | bytes 86048 | tf_op jit(solution)/shard_map/ppermute | solution.py:435
  69.3 3.5 %collective-permute-done.23.refs_1_ = bf16[24,1792]{1,0:T(8,128)(2,1)S(1)} collective-permute-done((bf16[24,1792]{1,0:T(8,128)(2,1)S(1)}, bf16[24,1792]{1,0:T(8,128)(2,1)S(1)}, u32[]{:S(2)}, u32[]{:S(2)}) %collective-permute-start.23) | collective-permute-done | bytes 86048 | tf_op jit(solution)/shard_map/ppermute | solution.py:435
  72.8 0.1 sum_units.3
  72.9 0.4 collective-permute-start.26
  73.3 0.9 %collective-permute-done.26.twin_ref = bf16[24,1792]{1,0:T(8,128)(2,1)S(1)} collective-permute-done((bf16[24,1792]{1,0:T(8,128)(2,1)S(1)}, bf16[24,1792]{1,0:T(8,128)(2,1)S(1)}, u32[]{:S(2)}, u32[]{:S(2)}) %collective-permute-start.26) | collective-permute-done | bytes 86048 | tf_op jit(solution)/shard_map/ppermute | solution.py:431
  74.3 0.9 %final_rows.1 = bf16[3,7168]{1,0:T(4,128)(2,1)} custom-call(f32[24,128]{1,0:T(8,128)S(1)} %get-tuple-element.41.live_ref, f32[24,1792]{1,0:T(8,128)S(1)} %get-tuple-element.75.mine_ref, bf16[24,1792]{1,0:T(8,128)(2,1)S(1)} %collective-permute-done.26.twin_ref), custom_call_target="tpu_custom_call" | custom-call | tf_op jit(solution)/shard_map/final_rows/pallas_call | solution.py:411
  (18 shorter events, 0.0 us)
Async XLA Ops:
  5.2 11.4 %collective-permute-start = (bf16[6,8,512]{2,1,0:T(8,128)(2,1)S(1)}, bf16[6,8,512]{2,1,0:T(8,128)(2,1)S(1)}, u32[]{:S(2)}, u32[]{:S(2)}) collective-permute-start(bf16[6,8,512]{2,1,0:T(8,128)(2,1)S(1)} %get-tuple-element.42), channel_id=1, source_target_pairs={{0,12},{2,14},{4,8},{6,10},{8,4},{10,6},{12,0},{14,2},{1,13},{3,15... | collective-permute-start | bytes 147464 | tf_op jit(solution)/shard_map/ppermute | solution.py:428
  10.3 6.3 %collective-permute-start.1 = (bf16[6,8,512]{2,1,0:T(8,128)(2,1)S(1)}, bf16[6,8,512]{2,1,0:T(8,128)(2,1)S(1)}, u32[]{:S(2)}, u32[]{:S(2)}) collective-permute-start(bf16[6,8,512]{2,1,0:T(8,128)(2,1)S(1)} %get-tuple-element.43), channel_id=1, source_target_pairs={{0,8},{2,10},{4,12},{6,14},{8,0},{10,2},{12,4},{14,6},{1,9},{3,11}... | collective-permute-start | bytes 147464 | tf_op jit(solution)/shard_map/ppermute | solution.py:428
  10.3 11.2 %collective-permute-start.2 = (bf16[6,8,512]{2,1,0:T(8,128)(2,1)S(1)}, bf16[6,8,512]{2,1,0:T(8,128)(2,1)S(1)}, u32[]{:S(2)}, u32[]{:S(2)}) collective-permute-start(bf16[6,8,512]{2,1,0:T(8,128)(2,1)S(1)} %get-tuple-element.44), channel_id=1, source_target_pairs={{0,14},{2,12},{4,10},{6,8},{8,6},{10,4},{12,2},{14,0},{1,15},{3,13... | collective-permute-start | bytes 147464 | tf_op jit(solution)/shard_map/ppermute | solution.py:428
  13.2 8.3 %collective-permute-start.3 = (bf16[6,8,512]{2,1,0:T(8,128)(2,1)S(1)}, bf16[6,8,512]{2,1,0:T(8,128)(2,1)S(1)}, u32[]{:S(2)}, u32[]{:S(2)}) collective-permute-start(bf16[6,8,512]{2,1,0:T(8,128)(2,1)S(1)} %get-tuple-element.45), channel_id=1, source_target_pairs={{0,10},{2,8},{4,14},{6,12},{8,2},{10,0},{12,6},{14,4},{1,11},{3,9}... | collective-permute-start | bytes 147464 | tf_op jit(solution)/shard_map/ppermute | solution.py:428
  14.2 7.3 %collective-permute-start.4 = (bf16[6,8,512]{2,1,0:T(8,128)(2,1)S(1)}, bf16[6,8,512]{2,1,0:T(8,128)(2,1)S(1)}, u32[]{:S(2)}, u32[]{:S(2)}) collective-permute-start(bf16[6,8,512]{2,1,0:T(8,128)(2,1)S(1)} %get-tuple-element.46), channel_id=1, source_target_pairs={{0,6},{2,4},{4,2},{6,0},{8,14},{10,12},{12,10},{14,8},{1,7},{3,5},... | collective-permute-start | bytes 147464 | tf_op jit(solution)/shard_map/ppermute | solution.py:428
  16.6 5.0 %collective-permute-start.5 = (bf16[6,8,512]{2,1,0:T(8,128)(2,1)S(1)}, bf16[6,8,512]{2,1,0:T(8,128)(2,1)S(1)}, u32[]{:S(2)}, u32[]{:S(2)}) collective-permute-start(bf16[6,8,512]{2,1,0:T(8,128)(2,1)S(1)} %get-tuple-element.47), channel_id=1, source_target_pairs={{0,4},{2,6},{4,0},{6,2},{8,12},{10,14},{12,8},{14,10},{1,5},{3,7},... | collective-permute-start | bytes 147464 | tf_op jit(solution)/shard_map/ppermute | solution.py:428
  16.6 5.0 %collective-permute-start.6 = (bf16[6,8,512]{2,1,0:T(8,128)(2,1)S(1)}, bf16[6,8,512]{2,1,0:T(8,128)(2,1)S(1)}, u32[]{:S(2)}, u32[]{:S(2)}) collective-permute-start(bf16[6,8,512]{2,1,0:T(8,128)(2,1)S(1)} %get-tuple-element.48), channel_id=1, source_target_pairs={{0,2},{2,0},{4,6},{6,4},{8,10},{10,8},{12,14},{14,12},{1,3},{3,1},... | collective-permute-start | bytes 147464 | tf_op jit(solution)/shard_map/ppermute | solution.py:428
  25.0 1.7 %collective-permute-start.7 = (bf16[96,1792]{1,0:T(8,128)(2,1)S(1)}, bf16[96,1792]{1,0:T(8,128)(2,1)S(1)}, u32[]{:S(2)}, u32[]{:S(2)}) collective-permute-start(bf16[96,1792]{1,0:T(8,128)(2,1)S(1)} %get-tuple-element.54), channel_id=1, source_target_pairs={{0,1},{1,0},{2,3},{3,2},{4,5},{5,4},{6,7},{7,6},{8,9},{9,8},{10,11... | collective-permute-start | bytes 1032200 | tf_op jit(solution)/shard_map/ppermute | solution.py:431
  27.0 8.6 %collective-permute-start.8 = (bf16[24,1792]{1,0:T(8,128)(2,1)S(1)}, bf16[24,1792]{1,0:T(8,128)(2,1)S(1)}, u32[]{:S(2)}, u32[]{:S(2)}) collective-permute-start(bf16[24,1792]{1,0:T(8,128)(2,1)S(1)} %get-tuple-element.58), channel_id=1, source_target_pairs={{0,12},{1,15},{2,14},{3,13},{4,8},{5,11},{6,10},{7,9},{8,4},{9,7},... | collective-permute-start | bytes 258056 | tf_op jit(solution)/shard_map/ppermute | solution.py:435
  30.6 7.9 %collective-permute-start.9 = (bf16[24,1792]{1,0:T(8,128)(2,1)S(1)}, bf16[24,1792]{1,0:T(8,128)(2,1)S(1)}, u32[]{:S(2)}, u32[]{:S(2)}) collective-permute-start(bf16[24,1792]{1,0:T(8,128)(2,1)S(1)} %get-tuple-element.59), channel_id=1, source_target_pairs={{0,8},{1,11},{2,10},{3,9},{4,12},{5,15},{6,14},{7,13},{8,0},{9,3},... | collective-permute-start | bytes 258056 | tf_op jit(solution)/shard_map/ppermute | solution.py:435
  30.6 7.9 %collective-permute-start.10 = (bf16[24,1792]{1,0:T(8,128)(2,1)S(1)}, bf16[24,1792]{1,0:T(8,128)(2,1)S(1)}, u32[]{:S(2)}, u32[]{:S(2)}) collective-permute-start(bf16[24,1792]{1,0:T(8,128)(2,1)S(1)} %get-tuple-element.60), channel_id=1, source_target_pairs={{0,4},{1,7},{2,6},{3,5},{4,0},{5,3},{6,2},{7,1},{8,12},{9,15},{10,... | collective-permute-start | bytes 258056 | tf_op jit(solution)/shard_map/ppermute | solution.py:435
  31.4 7.1 %collective-permute-start.11 = (bf16[24,1792]{1,0:T(8,128)(2,1)S(1)}, bf16[24,1792]{1,0:T(8,128)(2,1)S(1)}, u32[]{:S(2)}, u32[]{:S(2)}) collective-permute-start(bf16[24,1792]{1,0:T(8,128)(2,1)S(1)} %get-tuple-element.56._.own_ref), channel_id=1, source_target_pairs={{1,3},{3,1},{5,7},{7,5},{9,11},{11,9},{13,15},{15,13},{17,19},{19,... | collective-permute-start | bytes 258056 | tf_op jit(solution)/shard_map/ppermute | solution.py:435
  38.6 1.5 %collective-permute-start.12 = (f32[24,1792]{1,0:T(8,128)S(1)}, f32[24,1792]{1,0:T(8,128)S(1)}, u32[]{:S(2)}, u32[]{:S(2)}) collective-permute-start(f32[24,1792]{1,0:T(8,128)S(1)} %get-tuple-element.62), channel_id=1, source_target_pairs={{0,1},{1,0},{2,3},{3,2},{4,5},{5,4},{6,7},{7,6},{8,9},{9,8},{10,11... | collective-permute-start | bytes 516104 | tf_op jit(solution)/shard_map/ppermute | solution.py:431
  40.2 10.0 %collective-permute-start.15 = (bf16[24,1792]{1,0:T(8,128)(2,1)S(1)}, bf16[24,1792]{1,0:T(8,128)(2,1)S(1)}, u32[]{:S(2)}, u32[]{:S(2)}) collective-permute-start(bf16[24,1792]{1,0:T(8,128)(2,1)S(1)} %get-tuple-element.64._.refs_0_), channel_id=1, source_target_pairs={{0,8},{1,11},{2,10},{3,9},{4,12},{5,15},{6,14},{7,13},{8,0},{9,3},... | collective-permute-start | bytes 258056 | tf_op jit(solution)/shard_map/ppermute | solution.py:435
  41.2 9.0 %collective-permute-start.16 = (bf16[24,1792]{1,0:T(8,128)(2,1)S(1)}, bf16[24,1792]{1,0:T(8,128)(2,1)S(1)}, u32[]{:S(2)}, u32[]{:S(2)}) collective-permute-start(bf16[24,1792]{1,0:T(8,128)(2,1)S(1)} %get-tuple-element.64._.refs_0_), channel_id=1, source_target_pairs={{0,12},{1,15},{2,14},{3,13},{4,8},{5,11},{6,10},{7,9},{8,4},{9,7},... | collective-permute-start | bytes 258056 | tf_op jit(solution)/shard_map/ppermute | solution.py:435
  43.3 8.6 %collective-permute-start.14 = (bf16[24,1792]{1,0:T(8,128)(2,1)S(1)}, bf16[24,1792]{1,0:T(8,128)(2,1)S(1)}, u32[]{:S(2)}, u32[]{:S(2)}) collective-permute-start(bf16[24,1792]{1,0:T(8,128)(2,1)S(1)} %get-tuple-element.64._.refs_0_), channel_id=1, source_target_pairs={{0,4},{1,7},{2,6},{3,5},{4,0},{5,3},{6,2},{7,1},{8,12},{9,15},{10,... | collective-permute-start | bytes 258056 | tf_op jit(solution)/shard_map/ppermute | solution.py:435
  43.7 8.2 %collective-permute-start.13 = (bf16[24,1792]{1,0:T(8,128)(2,1)S(1)}, bf16[24,1792]{1,0:T(8,128)(2,1)S(1)}, u32[]{:S(2)}, u32[]{:S(2)}) collective-permute-start(bf16[24,1792]{1,0:T(8,128)(2,1)S(1)} %get-tuple-element.64._.refs_0_), channel_id=1, source_target_pairs={{1,3},{3,1},{5,7},{7,5},{9,11},{11,9},{13,15},{15,13},{17,19},{19,... | collective-permute-start | bytes 258056 | tf_op jit(solution)/shard_map/ppermute | solution.py:435
  50.2 2.3 %collective-permute-start.20 = (bf16[24,1792]{1,0:T(8,128)(2,1)S(1)}, bf16[24,1792]{1,0:T(8,128)(2,1)S(1)}, u32[]{:S(2)}, u32[]{:S(2)}) collective-permute-start(bf16[24,1792]{1,0:T(8,128)(2,1)S(1)} %collective-permute-done.16.refs_4_), channel_id=1, source_target_pairs={{0,1},{1,0},{2,3},{3,2},{4,5},{5,4},{6,7},{7,6},{8,9},{9,8},{10,11... | collective-permute-start | bytes 258056 | tf_op jit(solution)/shard_map/ppermute | solution.py:431
  51.9 1.3 %collective-permute-start.18 = (bf16[24,1792]{1,0:T(8,128)(2,1)S(1)}, bf16[24,1792]{1,0:T(8,128)(2,1)S(1)}, u32[]{:S(2)}, u32[]{:S(2)}) collective-permute-start(bf16[24,1792]{1,0:T(8,128)(2,1)S(1)} %collective-permute-done.14.refs_2_), channel_id=1, source_target_pairs={{0,1},{1,0},{2,3},{3,2},{4,5},{5,4},{6,7},{7,6},{8,9},{9,8},{10,11... | collective-permute-start | bytes 258056 | tf_op jit(solution)/shard_map/ppermute | solution.py:431
  52.0 1.3 %collective-permute-start.17 = (bf16[24,1792]{1,0:T(8,128)(2,1)S(1)}, bf16[24,1792]{1,0:T(8,128)(2,1)S(1)}, u32[]{:S(2)}, u32[]{:S(2)}) collective-permute-start(bf16[24,1792]{1,0:T(8,128)(2,1)S(1)} %collective-permute-done.13.refs_1_), channel_id=1, source_target_pairs={{0,1},{1,0},{2,3},{3,2},{4,5},{5,4},{6,7},{7,6},{8,9},{9,8},{10,11... | collective-permute-start | bytes 258056 | tf_op jit(solution)/shard_map/ppermute | solution.py:431
  52.4 1.3 %collective-permute-start.19 = (bf16[24,1792]{1,0:T(8,128)(2,1)S(1)}, bf16[24,1792]{1,0:T(8,128)(2,1)S(1)}, u32[]{:S(2)}, u32[]{:S(2)}) collective-permute-start(bf16[24,1792]{1,0:T(8,128)(2,1)S(1)} %collective-permute-done.15.refs_3_), channel_id=1, source_target_pairs={{0,1},{1,0},{2,3},{3,2},{4,5},{5,4},{6,7},{7,6},{8,9},{9,8},{10,11... | collective-permute-start | bytes 258056 | tf_op jit(solution)/shard_map/ppermute | solution.py:431
  60.0 1.7 %collective-permute-start.21 = (bf16[96,1792]{1,0:T(8,128)(2,1)S(1)}, bf16[96,1792]{1,0:T(8,128)(2,1)S(1)}, u32[]{:S(2)}, u32[]{:S(2)}) collective-permute-start(bf16[96,1792]{1,0:T(8,128)(2,1)S(1)} %get-tuple-element.69), channel_id=1, source_target_pairs={{0,1},{1,0},{2,3},{3,2},{4,5},{5,4},{6,7},{7,6},{8,9},{9,8},{10,11... | collective-permute-start | bytes 1032200 | tf_op jit(solution)/shard_map/ppermute | solution.py:431
  62.0 7.4 %collective-permute-start.22 = (bf16[24,1792]{1,0:T(8,128)(2,1)S(1)}, bf16[24,1792]{1,0:T(8,128)(2,1)S(1)}, u32[]{:S(2)}, u32[]{:S(2)}) collective-permute-start(bf16[24,1792]{1,0:T(8,128)(2,1)S(1)} %get-tuple-element.72), channel_id=1, source_target_pairs={{0,12},{1,15},{2,14},{3,13},{4,8},{5,11},{6,10},{7,9},{8,4},{9,7},... | collective-permute-start | bytes 258056 | tf_op jit(solution)/shard_map/ppermute | solution.py:435
  64.1 8.8 %collective-permute-start.23 = (bf16[24,1792]{1,0:T(8,128)(2,1)S(1)}, bf16[24,1792]{1,0:T(8,128)(2,1)S(1)}, u32[]{:S(2)}, u32[]{:S(2)}) collective-permute-start(bf16[24,1792]{1,0:T(8,128)(2,1)S(1)} %get-tuple-element.73), channel_id=1, source_target_pairs={{0,8},{1,11},{2,10},{3,9},{4,12},{5,15},{6,14},{7,13},{8,0},{9,3},... | collective-permute-start | bytes 258056 | tf_op jit(solution)/shard_map/ppermute | solution.py:435
  64.2 8.6 %collective-permute-start.24 = (bf16[24,1792]{1,0:T(8,128)(2,1)S(1)}, bf16[24,1792]{1,0:T(8,128)(2,1)S(1)}, u32[]{:S(2)}, u32[]{:S(2)}) collective-permute-start(bf16[24,1792]{1,0:T(8,128)(2,1)S(1)} %get-tuple-element.74), channel_id=1, source_target_pairs={{0,4},{1,7},{2,6},{3,5},{4,0},{5,3},{6,2},{7,1},{8,12},{9,15},{10,... | collective-permute-start | bytes 258056 | tf_op jit(solution)/shard_map/ppermute | solution.py:435
  66.4 6.4 %collective-permute-start.25 = (bf16[24,1792]{1,0:T(8,128)(2,1)S(1)}, bf16[24,1792]{1,0:T(8,128)(2,1)S(1)}, u32[]{:S(2)}, u32[]{:S(2)}) collective-permute-start(bf16[24,1792]{1,0:T(8,128)(2,1)S(1)} %get-tuple-element.70.own_ref), channel_id=1, source_target_pairs={{1,3},{3,1},{5,7},{7,5},{9,11},{11,9},{13,15},{15,13},{17,19},{19,... | collective-permute-start | bytes 258056 | tf_op jit(solution)/shard_map/ppermute | solution.py:435
  72.9 1.4 %collective-permute-start.26 = (bf16[24,1792]{1,0:T(8,128)(2,1)S(1)}, bf16[24,1792]{1,0:T(8,128)(2,1)S(1)}, u32[]{:S(2)}, u32[]{:S(2)}) collective-permute-start(bf16[24,1792]{1,0:T(8,128)(2,1)S(1)} %get-tuple-element.76), channel_id=1, source_target_pairs={{0,1},{1,0},{2,3},{3,2},{4,5},{5,4},{6,7},{7,6},{8,9},{9,8},{10,11... | collective-permute-start | bytes 258056 | tf_op jit(solution)/shard_map/ppermute | solution.py:431
